TPU v7x, 32 devices: a whole 2x2x4 slice. The times are simulated.
32 devices in a mesh: dp: 4 (over z), seq: 4 (over y, x), tensor: 2 (over core).
Axes of the slice: x: 2, y: 2, z: 4, core: 2. Of those that a mesh axis runs over, the one named last changes fastest.
Arguments:
- tokens: bfloat16 [8, 4, 256, 1152], P('dp', 'seq'), may hold values from -6 to 6
- conditioning: float32 [8, 1152], P(None, ('dp', 'seq', 'tensor')), may hold values from -5 to 5
- cotangent: bfloat16 [8, 4, 256, 1152], P('dp', 'seq'), may hold values from -6 to 6
- modulation_weight: bfloat16 [2, 1152, 6912], P(None, ('dp', 'seq', 'tensor')), may hold values from -0.25 to 0.25
- modulation_bias: bfloat16 [2, 6912], P(None, ('dp', 'seq', 'tensor')), may hold values from -2 to 2
- triple_weight: bfloat16 [2, 1152, 3, 1152], P(None, ('dp', 'seq'), None, 'tensor'), may hold values from -0.1875 to 0.1875
- pair_bias: bfloat16 [2, 2, 2, 576], P(None, None, 'tensor', ('dp', 'seq')), may hold values from -3 to 3
- out_weight: bfloat16 [2, 1152, 1152], P(None, 'tensor', ('dp', 'seq')), may hold values from -1 to 1
- out_bias: bfloat16 [2, 1152], P(None, ('dp', 'seq')), may hold values from -2 to 2
- hidden_weight: bfloat16 [2, 1152, 4608], P(None, ('dp', 'seq'), 'tensor'), may hold values from -0.1875 to 0.1875
- hidden_bias: bfloat16 [2, 2, 2304], P(None, 'tensor', ('dp', 'seq')), may hold values from -3 to 3
- output_weight: bfloat16 [2, 4608, 1152], P(None, 'tensor', ('dp', 'seq')), may hold values from -0.09375 to 0.09375
- output_bias: bfloat16 [2, 1152], P(None, ('dp', 'seq')), may hold values from -2 to 2
Outputs:
- activations: bfloat16 [8, 4, 256, 1152], P('dp', 'seq')
- input_grad: float32 [8, 4, 256, 1152], P('dp', 'seq')
- cond_grad: float32 [8, 1152], P(None, ('dp', 'seq', 'tensor'))
- modulation_weight_grad: float32 [2, 1152, 6912], P(None, ('dp', 'seq', 'tensor'))
- modulation_bias_grad: float32 [2, 6912], P(None, ('dp', 'seq', 'tensor'))
- triple_weight_grad: float32 [2, 1152, 3, 1152], P(None, ('dp', 'seq'), None, 'tensor')
- pair_bias_grad: float32 [2, 2, 2, 576], P(None, None, 'tensor', ('dp', 'seq'))
- out_weight_grad: float32 [2, 1152, 1152], P(None, 'tensor', ('dp', 'seq'))
- out_bias_grad: float32 [2, 1152], P(None, ('dp', 'seq'))
- hidden_weight_grad: float32 [2, 1152, 4608], P(None, ('dp', 'seq'), 'tensor')
- hidden_bias_grad: float32 [2, 2, 2304], P(None, 'tensor', ('dp', 'seq'))
- output_weight_grad: float32 [2, 4608, 1152], P(None, 'tensor', ('dp', 'seq'))
- output_bias_grad: float32 [2, 1152], P(None, ('dp', 'seq'))
All inputs are finite; a program needn't handle non-finite values.
Results may differ from a plain program's by a relative error of at most 0.028.
Values may be sent and summed in bfloat16 or wider, within the bound.
No kernel may reach another device: no remote copies, remote signals or barrier semaphores. Data moves between devices by JAX's collectives and lax.ppermute only.
A program may use at most 320 MiB of HBM per device.

v0:
```python
from functools import partial

import jax
import jax.numpy as jnp
from jax import lax
from jax.sharding import PartitionSpec as P

HEAD_DIM = 72
CL_MB = 1


epsilon = 1e-06


def as_sent(array):
    return jax.tree.map(lambda a: a.astype(jnp.bfloat16) if a.dtype == jnp.float32 else a, array)


def normalize(values):
    average = jnp.mean(values, axis=-1, keepdims=True)
    centered = values - average
    variance = jnp.mean(centered * centered, axis=-1, keepdims=True)
    return centered * lax.rsqrt(variance + epsilon)


def modulate(values, shift_row, scale_row):
    return normalize(values) * (1.0 + scale_row) + shift_row


def row_of(mod_rows, position):
    return mod_rows[:, position][:, None, None, :]


def split_heads(merged):
    return merged.reshape(merged.shape[:-1] + (merged.shape[-1] // HEAD_DIM, HEAD_DIM))


def join_heads(per_head):
    return per_head.reshape(per_head.shape[:-2] + (-1,))


def heads_total(partial_sum):
    return lax.psum(partial_sum, "tensor")


def inputs_total(partial_sum):
    return lax.psum(partial_sum.astype(jnp.bfloat16), "tensor").astype(jnp.float32)


def spatial_forward(queries, key_rows, value_rows):
    factor = HEAD_DIM ** (-0.5)
    scores = (
        jnp.einsum("cfphe,cfqhe->cfhpq", queries, key_rows, preferred_element_type=jnp.float32)
        * factor
    )
    highest_score = jnp.max(scores, axis=-1, keepdims=True)
    log_total = highest_score + jnp.log(
        jnp.sum(jnp.exp(scores - highest_score), axis=-1, keepdims=True)
    )
    probability = jnp.exp(scores - log_total).astype(jnp.bfloat16)
    attended = jnp.einsum(
        "cfhpq,cfqhe->cfphe", probability, value_rows, preferred_element_type=jnp.float32
    )
    return (join_heads(attended).astype(jnp.bfloat16), log_total)


def spatial_backward(queries, key_rows, value_rows, grad_att, log_total):
    factor = HEAD_DIM ** (-0.5)
    scores = (
        jnp.einsum("cfphe,cfqhe->cfhpq", queries, key_rows, preferred_element_type=jnp.float32)
        * factor
    )
    probability = jnp.exp(scores - log_total)
    grad_probs = jnp.einsum(
        "cfphe,cfqhe->cfhpq", grad_att, value_rows, preferred_element_type=jnp.float32
    )
    inner_sum = jnp.sum(grad_probs * probability, axis=-1, keepdims=True)
    grad_scores = (probability * (grad_probs - inner_sum)).astype(jnp.bfloat16)
    grad_query = (
        jnp.einsum("cfhpq,cfqhe->cfphe", grad_scores, key_rows, preferred_element_type=jnp.float32)
        * factor
    )
    grad_key = (
        jnp.einsum("cfhpq,cfphe->cfqhe", grad_scores, queries, preferred_element_type=jnp.float32)
        * factor
    )
    grad_value = jnp.einsum(
        "cfhpq,cfphe->cfqhe",
        probability.astype(jnp.bfloat16),
        grad_att,
        preferred_element_type=jnp.float32,
    )
    return (
        join_heads(grad_query).astype(jnp.bfloat16),
        join_heads(grad_key).astype(jnp.bfloat16),
        join_heads(grad_value).astype(jnp.bfloat16),
    )


def temporal_attend(pieces):
    factor = HEAD_DIM ** (-0.5)
    queries = split_heads(pieces[0])
    key_rows = split_heads(pieces[1])
    value_rows = split_heads(pieces[2])
    scores = (
        jnp.einsum("cfphe,cgphe->cphfg", queries, key_rows, preferred_element_type=jnp.float32)
        * factor
    )
    highest_score = jnp.max(scores, axis=-1, keepdims=True)
    log_total = highest_score + jnp.log(
        jnp.sum(jnp.exp(scores - highest_score), axis=-1, keepdims=True)
    )
    probability = jnp.exp(scores - log_total).astype(jnp.bfloat16)
    attended = jnp.einsum(
        "cphfg,cgphe->cfphe", probability, value_rows, preferred_element_type=jnp.float32
    )
    return lax.all_to_all(
        join_heads(attended).astype(jnp.bfloat16), "seq", split_axis=1, concat_axis=2, tiled=True
    )


def temporal_grads(pieces):
    factor = HEAD_DIM ** (-0.5)
    queries = split_heads(pieces[0])
    key_rows = split_heads(pieces[1])
    value_rows = split_heads(pieces[2])
    grad_att = split_heads(pieces[3])
    scores = (
        jnp.einsum("cfphe,cgphe->cphfg", queries, key_rows, preferred_element_type=jnp.float32)
        * factor
    )
    highest_score = jnp.max(scores, axis=-1, keepdims=True)
    log_total = highest_score + jnp.log(
        jnp.sum(jnp.exp(scores - highest_score), axis=-1, keepdims=True)
    )
    probability = jnp.exp(scores - log_total)
    grad_probs = jnp.einsum(
        "cfphe,cgphe->cphfg", grad_att, value_rows, preferred_element_type=jnp.float32
    )
    inner_sum = jnp.sum(grad_probs * probability, axis=-1, keepdims=True)
    grad_scores = (probability * (grad_probs - inner_sum)).astype(jnp.bfloat16)
    grad_query = (
        jnp.einsum("cphfg,cgphe->cfphe", grad_scores, key_rows, preferred_element_type=jnp.float32)
        * factor
    )
    grad_key = (
        jnp.einsum("cphfg,cfphe->cgphe", grad_scores, queries, preferred_element_type=jnp.float32)
        * factor
    )
    grad_value = jnp.einsum(
        "cphfg,cfphe->cgphe",
        probability.astype(jnp.bfloat16),
        grad_att,
        preferred_element_type=jnp.float32,
    )
    return (
        lax.all_to_all(
            join_heads(grad_query).astype(jnp.bfloat16),
            "seq",
            split_axis=1,
            concat_axis=2,
            tiled=True,
        ),
        lax.all_to_all(
            join_heads(grad_key).astype(jnp.bfloat16),
            "seq",
            split_axis=1,
            concat_axis=2,
            tiled=True,
        ),
        lax.all_to_all(
            join_heads(grad_value).astype(jnp.bfloat16),
            "seq",
            split_axis=1,
            concat_axis=2,
            tiled=True,
        ),
    )


def layer_forward(residual, mod_rows, weights, temporal):
    triple_mat, pair_vec, out_mat, out_vec, hidden_mat, hidden_vec, output_mat, output_vec = weights
    normed_one = modulate(residual, row_of(mod_rows, 0), row_of(mod_rows, 1)).astype(jnp.bfloat16)
    triple = jnp.einsum(
        "cfpd,dte->cfpte", normed_one, triple_mat, preferred_element_type=jnp.float32
    )
    bias_rows = jnp.stack([pair_vec[0, 0], jnp.zeros_like(pair_vec[0, 0]), pair_vec[1, 0]]).astype(
        jnp.float32
    )
    triple = (triple + bias_rows).astype(jnp.bfloat16)
    queries, key_rows, value_rows = (triple[:, :, :, 0], triple[:, :, :, 1], triple[:, :, :, 2])
    if temporal:
        attended = temporal_attend(
            (
                lax.all_to_all(queries, "seq", split_axis=2, concat_axis=1, tiled=True),
                lax.all_to_all(key_rows, "seq", split_axis=2, concat_axis=1, tiled=True),
                lax.all_to_all(value_rows, "seq", split_axis=2, concat_axis=1, tiled=True),
            )
        )
        log_total = None
    else:
        attended, log_total = spatial_forward(
            split_heads(queries), split_heads(key_rows), split_heads(value_rows)
        )
    branch = heads_total(
        jnp.einsum("cfpe,ed->cfpd", attended, out_mat, preferred_element_type=jnp.float32)
    ) + out_vec.astype(jnp.float32)
    resid_mid = residual + row_of(mod_rows, 2) * branch
    normed_two = modulate(resid_mid, row_of(mod_rows, 3), row_of(mod_rows, 4)).astype(jnp.bfloat16)
    pre_act = jnp.einsum(
        "cfpd,de->cfpe", normed_two, hidden_mat, preferred_element_type=jnp.float32
    ) + hidden_vec[0].astype(jnp.float32)
    hidden = jax.nn.gelu(pre_act, approximate=True).astype(jnp.bfloat16)
    mlp_out = heads_total(
        jnp.einsum("cfpe,ed->cfpd", hidden, output_mat, preferred_element_type=jnp.float32)
    ) + output_vec.astype(jnp.float32)
    resid_out = resid_mid + row_of(mod_rows, 5) * mlp_out
    saved_state = (
        residual,
        normed_one,
        queries,
        key_rows,
        value_rows,
        log_total,
        attended,
        branch,
        resid_mid,
        normed_two,
        pre_act,
        hidden,
        mlp_out,
    )
    return (resid_out, saved_state)


def layer_backward(grad_res, mod_rows, weights, saved_state, temporal):
    triple_mat, pair_vec, out_mat, out_vec, hidden_mat, hidden_vec, output_mat, output_vec = weights
    (
        residual,
        normed_one,
        queries,
        key_rows,
        value_rows,
        log_total,
        attended,
        branch,
        resid_mid,
        normed_two,
        pre_act,
        hidden,
        mlp_out,
    ) = saved_state
    grad_gate_two = jnp.sum(grad_res * mlp_out, axis=(1, 2))
    grad_mlp = (grad_res * row_of(mod_rows, 5)).astype(jnp.bfloat16)
    grad_output_bias = jnp.sum(grad_mlp, axis=(0, 1, 2), dtype=jnp.float32)
    grad_output = jnp.einsum("cfpe,cfpd->ed", hidden, grad_mlp, preferred_element_type=jnp.float32)
    grad_hidden = jnp.einsum(
        "cfpd,ed->cfpe", grad_mlp, output_mat, preferred_element_type=jnp.float32
    )
    gelu_back = jax.vjp(partial(jax.nn.gelu, approximate=True), pre_act)[1]
    grad_pre = gelu_back(grad_hidden)[0].astype(jnp.bfloat16)
    grad_hidden_bias = jnp.sum(grad_pre, axis=(0, 1, 2), dtype=jnp.float32)[None]
    grad_hidden_mat = jnp.einsum(
        "cfpd,cfpe->de", normed_two, grad_pre, preferred_element_type=jnp.float32
    )
    grad_normed_two = inputs_total(
        jnp.einsum("cfpe,de->cfpd", grad_pre, hidden_mat, preferred_element_type=jnp.float32)
    )
    back_two = jax.vjp(modulate, resid_mid, row_of(mod_rows, 3), row_of(mod_rows, 4))[1]
    grad_mid_norm, grad_shift_two, grad_scale_two = back_two(grad_normed_two)
    grad_mid = grad_res + grad_mid_norm
    grad_gate_one = jnp.sum(grad_mid * branch, axis=(1, 2))
    grad_branch = (grad_mid * row_of(mod_rows, 2)).astype(jnp.bfloat16)
    grad_out_bias = jnp.sum(grad_branch, axis=(0, 1, 2), dtype=jnp.float32)
    grad_out = jnp.einsum(
        "cfpe,cfpd->ed", attended, grad_branch, preferred_element_type=jnp.float32
    )
    grad_att = jnp.einsum(
        "cfpd,ed->cfpe", grad_branch, out_mat, preferred_element_type=jnp.float32
    ).astype(jnp.bfloat16)
    if temporal:
        grad_query, grad_key, grad_value = temporal_grads(
            (
                lax.all_to_all(
                    as_sent(queries), "seq", split_axis=2, concat_axis=1, tiled=True
                ).astype(queries.dtype),
                lax.all_to_all(
                    as_sent(key_rows), "seq", split_axis=2, concat_axis=1, tiled=True
                ).astype(key_rows.dtype),
                lax.all_to_all(
                    as_sent(value_rows), "seq", split_axis=2, concat_axis=1, tiled=True
                ).astype(value_rows.dtype),
                lax.all_to_all(grad_att, "seq", split_axis=2, concat_axis=1, tiled=True),
            )
        )
    else:
        grad_query, grad_key, grad_value = spatial_backward(
            split_heads(queries),
            split_heads(key_rows),
            split_heads(value_rows),
            split_heads(grad_att),
            log_total,
        )
    grad_triple = jnp.stack([grad_query, grad_key, grad_value], axis=3)
    grad_pair = jnp.stack(
        [
            jnp.sum(grad_query, axis=(0, 1, 2), dtype=jnp.float32),
            jnp.sum(grad_value, axis=(0, 1, 2), dtype=jnp.float32),
        ]
    )[:, None, :]
    grad_triple_mat = jnp.einsum(
        "cfpd,cfpte->dte", normed_one, grad_triple, preferred_element_type=jnp.float32
    )
    grad_normed_one = inputs_total(
        jnp.einsum("cfpte,dte->cfpd", grad_triple, triple_mat, preferred_element_type=jnp.float32)
    )
    back_one = jax.vjp(modulate, residual, row_of(mod_rows, 0), row_of(mod_rows, 1))[1]
    grad_in_norm, grad_shift_one, grad_scale_one = back_one(grad_normed_one)
    grad_in = grad_mid + grad_in_norm
    clip_count = grad_gate_one.shape[0]
    layer_mods = jnp.stack(
        [
            grad_shift_one.reshape(clip_count, -1),
            grad_scale_one.reshape(clip_count, -1),
            grad_gate_one,
            grad_shift_two.reshape(clip_count, -1),
            grad_scale_two.reshape(clip_count, -1),
            grad_gate_two,
        ],
        axis=1,
    )
    layer_grads = (
        grad_triple_mat,
        grad_pair,
        grad_out,
        grad_out_bias,
        grad_hidden_mat,
        grad_hidden_bias,
        grad_output,
        grad_output_bias,
    )
    return (grad_in, layer_mods, layer_grads)


def shards(
    tokens,
    conditioning,
    cotangent,
    modulation_weight,
    modulation_bias,
    triple_weight,
    pair_bias,
    out_weight,
    out_bias,
    hidden_weight,
    hidden_bias,
    output_weight,
    output_bias,
):
    layer_count = triple_weight.shape[0]
    model_width = tokens.shape[3]
    local_clips = tokens.shape[0]
    all_clips = conditioning.shape[0]
    act_cond, silu_back = jax.vjp(jax.nn.silu, conditioning)
    act_low = act_cond.astype(jnp.bfloat16)
    local_term = jnp.einsum(
        "cd,lde->cle", act_low, modulation_weight, preferred_element_type=jnp.float32
    )
    bias_cols = modulation_bias.shape[1]
    offset_cols = lax.axis_index(("dp", "seq", "tensor")) * bias_cols
    bias_full = lax.dynamic_update_slice(
        jnp.zeros((layer_count, local_term.shape[2]), jnp.float32),
        modulation_bias.astype(jnp.float32),
        (jnp.int32(0), offset_cols),
    )
    modulations = lax.psum(local_term + bias_full[None], ("dp", "seq", "tensor"))
    clip_start = lax.axis_index("dp") * local_clips
    own_mods = lax.dynamic_slice_in_dim(modulations, clip_start, local_clips, 0)
    batches = local_clips // CL_MB
    tok_batches = tokens.reshape((batches, CL_MB) + tokens.shape[1:])
    cot_batches = cotangent.reshape((batches, CL_MB) + cotangent.shape[1:])
    mod_batches = own_mods.reshape((batches, CL_MB) + own_mods.shape[1:])
    tensor_width = model_width // lax.axis_size("tensor")
    owned_cols = (jnp.arange(model_width) // tensor_width == lax.axis_index("tensor")).astype(
        jnp.float32
    )

    def gather_layer(layer_idx):
        return (
            lax.all_gather(triple_weight[layer_idx], ("dp", "seq"), axis=0, tiled=True),
            lax.all_gather(pair_bias[layer_idx], ("dp", "seq"), axis=2, tiled=True),
            lax.all_gather(out_weight[layer_idx], ("dp", "seq"), axis=1, tiled=True),
            lax.all_gather(out_bias[layer_idx], ("dp", "seq"), axis=0, tiled=True),
            lax.all_gather(hidden_weight[layer_idx], ("dp", "seq"), axis=0, tiled=True),
            lax.all_gather(hidden_bias[layer_idx], ("dp", "seq"), axis=1, tiled=True),
            lax.all_gather(output_weight[layer_idx], ("dp", "seq"), axis=1, tiled=True),
            lax.all_gather(output_bias[layer_idx], ("dp", "seq"), axis=0, tiled=True),
        )

    def micro_step(running, inputs):
        tok_rows, cot_rows, mod_batch = inputs
        residual = tok_rows.astype(jnp.float32)
        kept_rows = []
        for layer_idx in range(layer_count):
            weights = gather_layer(layer_idx)
            mod_rows = mod_batch[:, layer_idx].reshape(mod_batch.shape[0], 6, model_width)
            residual, saved_state = layer_forward(residual, mod_rows, weights, layer_idx == 1)
            kept_rows.append((mod_rows, saved_state))
        grad_res = cot_rows.astype(jnp.float32)
        grad_mods = [None] * layer_count
        updated = list(running)
        for layer_idx in reversed(range(layer_count)):
            weights = gather_layer(layer_idx)
            mod_rows, saved_state = kept_rows[layer_idx]
            grad_res, layer_mods, layer_grads = layer_backward(
                grad_res, mod_rows, weights, saved_state, layer_idx == 1
            )
            grad_mods[layer_idx] = (layer_mods * owned_cols).reshape(layer_mods.shape[0], -1)
            updated = [
                acc_sum.at[layer_idx].add(new_grad)
                for acc_sum, new_grad in zip(updated, layer_grads)
            ]
        return (
            tuple(updated),
            (residual.astype(jnp.bfloat16), grad_res, jnp.stack(grad_mods, axis=1)),
        )

    triple_cols = triple_weight.shape[3]
    hidden_cols = hidden_weight.shape[2]
    zero_grads = (
        jnp.zeros((layer_count, model_width, 3, triple_cols), jnp.float32),
        jnp.zeros((layer_count, 2, 1, triple_cols), jnp.float32),
        jnp.zeros((layer_count, triple_cols, model_width), jnp.float32),
        jnp.zeros((layer_count, model_width), jnp.float32),
        jnp.zeros((layer_count, model_width, hidden_cols), jnp.float32),
        jnp.zeros((layer_count, 1, hidden_cols), jnp.float32),
        jnp.zeros((layer_count, hidden_cols, model_width), jnp.float32),
        jnp.zeros((layer_count, model_width), jnp.float32),
    )
    summed, outputs = lax.scan(micro_step, zero_grads, (tok_batches, cot_batches, mod_batches))
    reduced = (
        lax.psum_scatter(summed[0], ("dp", "seq"), scatter_dimension=1, tiled=True),
        lax.psum_scatter(summed[1], ("dp", "seq"), scatter_dimension=3, tiled=True),
        lax.psum_scatter(summed[2], ("dp", "seq"), scatter_dimension=2, tiled=True),
        lax.psum_scatter(summed[3], ("dp", "seq"), scatter_dimension=1, tiled=True),
        lax.psum_scatter(summed[4], ("dp", "seq"), scatter_dimension=1, tiled=True),
        lax.psum_scatter(summed[5], ("dp", "seq"), scatter_dimension=2, tiled=True),
        lax.psum_scatter(summed[6], ("dp", "seq"), scatter_dimension=2, tiled=True),
        lax.psum_scatter(summed[7], ("dp", "seq"), scatter_dimension=1, tiled=True),
    )
    outs_act, outs_grad, outs_mods = outputs
    activations = outs_act.reshape(tokens.shape)
    input_grad = outs_grad.reshape(tokens.shape)
    mod_local = outs_mods.reshape((local_clips,) + outs_mods.shape[2:])
    mod_full = lax.dynamic_update_slice(
        jnp.zeros((all_clips,) + mod_local.shape[1:], jnp.float32),
        mod_local,
        (clip_start, jnp.int32(0), jnp.int32(0)),
    )
    grad_modulation = lax.psum(mod_full, ("dp", "seq", "tensor")).astype(jnp.bfloat16)
    modulation_weight_grad = jnp.einsum(
        "cd,cle->lde", act_low, grad_modulation, preferred_element_type=jnp.float32
    )
    modulation_bias_grad = lax.dynamic_slice_in_dim(
        jnp.sum(grad_modulation, axis=0, dtype=jnp.float32), offset_cols, bias_cols, 1
    )
    grad_act = jnp.einsum(
        "cle,lde->cd", grad_modulation, modulation_weight, preferred_element_type=jnp.float32
    )
    cond_grad = silu_back(grad_act)[0]
    return (
        activations,
        input_grad,
        cond_grad,
        modulation_weight_grad,
        modulation_bias_grad,
        reduced[0],
        reduced[1],
        reduced[2],
        reduced[3],
        reduced[4],
        reduced[5],
        reduced[6],
        reduced[7],
    )


def solution(mesh):
    placed = (
        P("dp", "seq", None, None),
        P(None, ("dp", "seq", "tensor")),
        P("dp", "seq", None, None),
        P(None, ("dp", "seq", "tensor"), None),
        P(None, ("dp", "seq", "tensor")),
        P(None, ("dp", "seq"), None, "tensor"),
        P(None, None, "tensor", ("dp", "seq")),
        P(None, "tensor", ("dp", "seq")),
        P(None, ("dp", "seq")),
        P(None, ("dp", "seq"), "tensor"),
        P(None, "tensor", ("dp", "seq")),
        P(None, "tensor", ("dp", "seq")),
        P(None, ("dp", "seq")),
    )
    return jax.shard_map(
        shards,
        mesh=mesh,
        in_specs=placed,
        out_specs=(
            P("dp", "seq", None, None),
            P("dp", "seq", None, None),
            P(None, ("dp", "seq", "tensor")),
            P(None, ("dp", "seq", "tensor"), None),
            P(None, ("dp", "seq", "tensor")),
            P(None, ("dp", "seq"), None, "tensor"),
            P(None, None, "tensor", ("dp", "seq")),
            P(None, "tensor", ("dp", "seq")),
            P(None, ("dp", "seq")),
            P(None, ("dp", "seq"), "tensor"),
            P(None, "tensor", ("dp", "seq")),
            P(None, "tensor", ("dp", "seq")),
            P(None, ("dp", "seq")),
        ),
        check_vma=False,
    )
```

profile of v0, /device:TPU:0, one launch (start us, length us, event | category | flops | bytes accessed | tf_op | source)
XLA Modules:
  0.0 3336.2 jit_solution(570472229517351606)
XLA Ops:
  10.4 132.1 %all-reduce.30.cloned.1.call-done = f32[8,2,6912]{2,0,1:T(8,128)} async-done(((f32[8,2,6912]{2,0,1:T(8,128)}), f32[8,2,6912]{2,0,1:T(8,128)}) %all-reduce.30.cloned.1.call-update) | async-done | bytes 442384 | tf_op jit(solution)/shard_map/psum | solution.py:376
  172.6 1954.9 %while.50 = (s32[]{:T(128)}, f32[2,1152,3,576]{1,3,2,0:T(8,128)}, f32[2,2,1,576]{3,2,1,0:T(1,128)}, f32[2,576,1152]{2,1,0:T(8,128)}, f32[2,1152]{1,0:T(2,128)}, ...) while((s32[]{:T(128)}, f32[2,1152,3,576]{1,3,2,0:T(8,128)}, ...), condition=%wide.region_54.55_spmd.clone, body=%wide.region_1.54_spmd.clone.sunk | while | flops 25075552256 | bytes 693705472 | solution.py:440
  177.8 43.0 %all-gather.40 = bf16[1,2,1,576]{2,1,0,3:T(2,128)(2,1)S(1)} all-gather(bf16[1,2,1,36]{2,1,0,3:T(2,128)(2,1)S(1)} %get-tuple-element.1213), channel_id=3, replica_groups=mesh['dp'=4,'seq'=4,'tensor'=2] {'dp','seq'}, dimensions={3}, use_global_device_ids=true | all-gather | bytes 2448 | tf_op jit(solution)/shard_map/while/body/eval_jaxpr/all_gather | solution.py:391
  223.4 39.0 %all-gather.41 = bf16[1,2,1,576]{2,1,0,3:T(2,128)(2,1)S(1)} all-gather(bf16[1,2,1,36]{2,1,0,3:T(2,128)(2,1)S(1)} %get-tuple-element.1216), channel_id=11, replica_groups=mesh['dp'=4,'seq'=4,'tensor'=2] {'dp','seq'}, dimensions={3}, use_global_device_ids=true | all-gather | bytes 2448 | tf_op jit(solution)/shard_map/while/body/eval_jaxpr/all_gather | solution.py:391
  272.4 48.6 %all-gather.63.cloned.1.call-done = bf16[1,576,1152]{1,2,0:T(8,128)(2,1)} async-done(((bf16[1,576,72]{1,2,0:T(8,128)(2,1)}), bf16[1,576,1152]{1,2,0:T(8,128)(2,1)}) %all-gather.63.cloned.1.call-update) | async-done | bytes 1327120 | tf_op jit(solution)/shard_map/while/body/eval_jaxpr/all_gather | solution.py:392
  331.6 75.8 %all-reduce.18 = (bf16[2304]{0:T(1024)(128)(2,1)}, bf16[1152]{0:T(1024)(128)(2,1)S(1)}, bf16[2304]{0:T(1024)(128)(2,1)S(1)}, bf16[1152]{0:T(1024)(128)(2,1)S(1)}...) all-reduce(bf16[2304]{0:T(1024)(128)(2,1)S(1)} %dynamic-update-slic, ...), channel_id=16, replica_groups=mesh['dp'=4,'seq'=4,'tensor'=2] {'dp','seq'}, use_global_device_ids=true, to_apply=%add.4 | all-reduce | flops 9216 | bytes 36864 | tf_op jit(solution)/shard_map/while
  410.5 23.0 all-gather.67.cloned.1.call-done
  439.5 81.4 %all-gather.65.cloned.1.call-done = bf16[1,2304,1152]{1,2,0:T(8,128)(2,1)} async-done(((bf16[1,2304,72]{1,2,0:T(8,128)(2,1)}), bf16[1,2304,1152]{1,2,0:T(8,128)(2,1)}) %all-gather.65.cloned.1.call-update) | async-done | bytes 5308432 | tf_op jit(solution)/shard_map/while/body/eval_jaxpr/all_gather | solution.py:396
  529.4 16.3 all-reduce.34.cloned.1.call-done
  548.9 79.5 %all-gather.69.cloned.1.call-done = bf16[1,1152,3,576]{3,1,2,0:T(8,128)(2,1)} async-done(((bf16[1,72,3,576]{3,1,2,0:T(8,128)(2,1)}), bf16[1,1152,3,576]{3,1,2,0:T(8,128)(2,1)}) %all-gather.69.cloned.1.call-update) | async-done | bytes 3981328 | tf_op jit(solution)/shard_map/while/body/eval_jaxpr/all_gather | solution.py:390
  711.1 15.3 all-reduce.36.cloned.1.call-done
  729.5 86.5 %all-gather.59.cloned.1.call-done = bf16[1,1152,2304]{2,1,0:T(8,128)(2,1)} async-done(((bf16[1,72,2304]{2,1,0:T(8,128)(2,1)}), bf16[1,1152,2304]{2,1,0:T(8,128)(2,1)}) %all-gather.59.cloned.1.call-update) | async-done | bytes 5308432 | tf_op jit(solution)/shard_map/while/body/eval_jaxpr/all_gather | solution.py:394
  822.2 81.2 %all-gather.57.cloned.1.call-done = bf16[1,2304,1152]{1,2,0:T(8,128)(2,1)} async-done(((bf16[1,2304,72]{1,2,0:T(8,128)(2,1)}), bf16[1,2304,1152]{1,2,0:T(8,128)(2,1)}) %all-gather.57.cloned.1.call-update) | async-done | bytes 5308432 | tf_op jit(solution)/shard_map/while/body/eval_jaxpr/all_gather | solution.py:396
  1152.5 43.3 %all-gather.40 = bf16[1,2,1,576]{2,1,0,3:T(2,128)(2,1)S(1)} all-gather(bf16[1,2,1,36]{2,1,0,3:T(2,128)(2,1)S(1)} %get-tuple-element.1213), channel_id=3, replica_groups=mesh['dp'=4,'seq'=4,'tensor'=2] {'dp','seq'}, dimensions={3}, use_global_device_ids=true | all-gather | bytes 2448 | tf_op jit(solution)/shard_map/while/body/eval_jaxpr/all_gather | solution.py:391
  1198.5 38.8 %all-gather.41 = bf16[1,2,1,576]{2,1,0,3:T(2,128)(2,1)S(1)} all-gather(bf16[1,2,1,36]{2,1,0,3:T(2,128)(2,1)S(1)} %get-tuple-element.1216), channel_id=11, replica_groups=mesh['dp'=4,'seq'=4,'tensor'=2] {'dp','seq'}, dimensions={3}, use_global_device_ids=true | all-gather | bytes 2448 | tf_op jit(solution)/shard_map/while/body/eval_jaxpr/all_gather | solution.py:391
  1247.2 48.5 %all-gather.63.cloned.1.call-done = bf16[1,576,1152]{1,2,0:T(8,128)(2,1)} async-done(((bf16[1,576,72]{1,2,0:T(8,128)(2,1)}), bf16[1,576,1152]{1,2,0:T(8,128)(2,1)}) %all-gather.63.cloned.1.call-update) | async-done | bytes 1327120 | tf_op jit(solution)/shard_map/while/body/eval_jaxpr/all_gather | solution.py:392
  1306.4 75.8 %all-reduce.18 = (bf16[2304]{0:T(1024)(128)(2,1)}, bf16[1152]{0:T(1024)(128)(2,1)S(1)}, bf16[2304]{0:T(1024)(128)(2,1)S(1)}, bf16[1152]{0:T(1024)(128)(2,1)S(1)}...) all-reduce(bf16[2304]{0:T(1024)(128)(2,1)S(1)} %dynamic-update-slic, ...), channel_id=16, replica_groups=mesh['dp'=4,'seq'=4,'tensor'=2] {'dp','seq'}, use_global_device_ids=true, to_apply=%add.4 | all-reduce | flops 9216 | bytes 36864 | tf_op jit(solution)/shard_map/while
  1385.2 23.1 all-gather.67.cloned.1.call-done
  1414.4 81.5 %all-gather.65.cloned.1.call-done = bf16[1,2304,1152]{1,2,0:T(8,128)(2,1)} async-done(((bf16[1,2304,72]{1,2,0:T(8,128)(2,1)}), bf16[1,2304,1152]{1,2,0:T(8,128)(2,1)}) %all-gather.65.cloned.1.call-update) | async-done | bytes 5308432 | tf_op jit(solution)/shard_map/while/body/eval_jaxpr/all_gather | solution.py:396
  1504.3 16.4 all-reduce.34.cloned.1.call-done
  1523.9 79.4 %all-gather.69.cloned.1.call-done = bf16[1,1152,3,576]{3,1,2,0:T(8,128)(2,1)} async-done(((bf16[1,72,3,576]{3,1,2,0:T(8,128)(2,1)}), bf16[1,1152,3,576]{3,1,2,0:T(8,128)(2,1)}) %all-gather.69.cloned.1.call-update) | async-done | bytes 3981328 | tf_op jit(solution)/shard_map/while/body/eval_jaxpr/all_gather | solution.py:390
  1686.0 15.3 all-reduce.36.cloned.1.call-done
  1704.4 86.3 %all-gather.59.cloned.1.call-done = bf16[1,1152,2304]{2,1,0:T(8,128)(2,1)} async-done(((bf16[1,72,2304]{2,1,0:T(8,128)(2,1)}), bf16[1,1152,2304]{2,1,0:T(8,128)(2,1)}) %all-gather.59.cloned.1.call-update) | async-done | bytes 5308432 | tf_op jit(solution)/shard_map/while/body/eval_jaxpr/all_gather | solution.py:394
  1797.0 81.4 %all-gather.57.cloned.1.call-done = bf16[1,2304,1152]{1,2,0:T(8,128)(2,1)} async-done(((bf16[1,2304,72]{1,2,0:T(8,128)(2,1)}), bf16[1,2304,1152]{1,2,0:T(8,128)(2,1)}) %all-gather.57.cloned.1.call-update) | async-done | bytes 5308432 | tf_op jit(solution)/shard_map/while/body/eval_jaxpr/all_gather | solution.py:396
  2143.7 18.4 copy.161
  2162.2 22.5 copy.163
  2187.5 45.9 %all-reduce.47 = bf16[8,2,6912]{2,0,1:T(8,128)(2,1)S(1)} all-reduce(f32[8,2,6912]{2,0,1:T(8,128)S(1)} %bitcast_dynamic-update-slice_fusion.1), channel_id=1, replica_groups=mesh['dp'=4,'seq'=4,'tensor'=2] {'dp','seq','tensor'}, use_global_device_ids=true, to_apply=%region_55.56 | all-reduce | flops 110592 | bytes 663552 | tf_op jit(solution)/shard_map/psum | solution.py:460
  2236.3 75.2 %all-reduce.16 = (f32[2,2,1,576]{3,2,1,0:T(1,128)S(1)}, f32[2,1152]{1,0:T(2,128)S(1)}, f32[2,1152]{1,0:T(2,128)S(1)}) all-reduce(f32[2,2,1,576]{3,2,1,0:T(1,128)S(1)} %copy-done.81, f32[2,1152]{1,0:T(2,128)S(1)} %copy-done.89, f32[2,1152]{1,0:T(2,128)S(1)} %copy-done.92), channel_id=19, replica_groups=mesh['dp'=4,'seq'=4,'tensor'=2] {'dp','seq'}, use_global_device_ids=true, to_apply=%region_58.59.clone | all-reduce | flops 6912 | bytes 55296
  2316.4 95.8 %reduce-scatter.13.cloned.1.call-done = f32[2,576,72]{1,2,0:T(8,128)} async-done(((f32[2,576,1152]{1,2,0:T(8,128)}), f32[2,576,72]{1,2,0:T(8,128)}) %reduce-scatter.13.cloned.1.call-update) | async-done | bytes 331792 | tf_op jit(solution)/shard_map/reduce_scatter | solution.py:444
  2412.2 276.8 %reduce-scatter.11.cloned.1.call-done = f32[2,72,3,576]{3,1,2,0:T(8,128)} async-done(((f32[2,1152,3,576]{3,1,2,0:T(8,128)}), f32[2,72,3,576]{3,1,2,0:T(8,128)}) %reduce-scatter.11.cloned.1.call-update) | async-done | bytes 995344 | tf_op jit(solution)/shard_map/reduce_scatter | solution.py:442
  2689.1 320.8 %reduce-scatter.17.cloned.1.call-done = f32[2,2304,72]{1,2,0:T(8,128)} async-done(((f32[2,2304,1152]{1,2,0:T(8,128)}), f32[2,2304,72]{1,2,0:T(8,128)}) %reduce-scatter.17.cloned.1.call-update) | async-done | bytes 1327120 | tf_op jit(solution)/shard_map/reduce_scatter | solution.py:448
  3009.9 319.6 %reduce-scatter.15.cloned.1.call-done = f32[2,72,2304]{2,1,0:T(8,128)} async-done(((f32[2,1152,2304]{2,1,0:T(8,128)}), f32[2,72,2304]{2,1,0:T(8,128)}) %reduce-scatter.15.cloned.1.call-update) | async-done | bytes 1327120 | tf_op jit(solution)/shard_map/reduce_scatter | solution.py:446
  (1053 shorter events, 821.9 us)
Async XLA Ops:
  7.2 135.3 %all-reduce.30.cloned.1.call-start = ((), (), s32[]{:S(2)}) async-start(), calls=%async_computation.13 | async-start | bytes 884736 | tf_op jit(solution)/shard_map/psum | solution.py:376
  172.6 93.6 %all-gather.61.cloned.1.call-start = ((), (), s32[]{:S(2)}) async-start(), calls=%async_computation.22 | async-start | bytes 4700160 | tf_op jit(solution)/shard_map/while/body/eval_jaxpr/all_gather | solution.py:390
  174.5 146.4 %all-gather.63.cloned.1.call-start = ((), (), s32[]{:S(2)}) async-start(), calls=%async_computation.23 | async-start | bytes 1566720 | tf_op jit(solution)/shard_map/while/body/eval_jaxpr/all_gather | solution.py:392
  176.2 231.2 %all-reduce.32.cloned.1.call-start = ((), (), s32[]{:S(2)}) async-start(), calls=%async_computation.24 | async-start | bytes 2359296 | tf_op jit(solution)/shard_map/while/body/eval_jaxpr/psum | solution.py:43
  324.1 109.4 %all-gather.67.cloned.1.call-start = ((), (), s32[]{:S(2)}) async-start(), calls=%async_computation.26 | async-start | bytes 5640192 | tf_op jit(solution)/shard_map/while/body/eval_jaxpr/all_gather | solution.py:394
  326.1 194.8 %all-gather.65.cloned.1.call-start = ((), (), s32[]{:S(2)}) async-start(), calls=%async_computation.25 | async-start | bytes 5640192 | tf_op jit(solution)/shard_map/while/body/eval_jaxpr/all_gather | solution.py:396
  328.1 217.6 %all-reduce.34.cloned.1.call-start = ((), (), s32[]{:S(2)}) async-start(), calls=%async_computation.27 | async-start | bytes 2359296 | tf_op jit(solution)/shard_map/while/body/eval_jaxpr/psum | solution.py:43
  527.3 101.2 %all-gather.69.cloned.1.call-start = ((), (), s32[]{:S(2)}) async-start(), calls=%async_computation.28 | async-start | bytes 4700160 | tf_op jit(solution)/shard_map/while/body/eval_jaxpr/all_gather | solution.py:390
  528.0 171.4 %all-gather.55.cloned.1.call-start = ((), (), s32[]{:S(2)}) async-start(), calls=%async_computation.19 | async-start | bytes 1566720 | tf_op jit(solution)/shard_map/while/body/eval_jaxpr/all_gather | solution.py:392
  707.8 108.2 %all-gather.59.cloned.1.call-start = ((), (), s32[]{:S(2)}) async-start(), calls=%async_computation.21 | async-start | bytes 5640192 | tf_op jit(solution)/shard_map/while/body/eval_jaxpr/all_gather | solution.py:394
  708.6 194.9 %all-gather.57.cloned.1.call-start = ((), (), s32[]{:S(2)}) async-start(), calls=%async_computation.20 | async-start | bytes 5640192 | tf_op jit(solution)/shard_map/while/body/eval_jaxpr/all_gather | solution.py:396
  709.2 233.9 %all-reduce.40.cloned.1.call-start = ((), (), s32[]{:S(2)}) async-start(), calls=%async_computation.31 | async-start | bytes 1179648 | tf_op jit(solution)/shard_map/while/body/eval_jaxpr/psum | solution.py:47
  1044.8 59.1 %all-reduce.44.cloned.1.call-start = ((), (), s32[]{:S(2)}) async-start(), calls=%async_computation.33 | async-start | bytes 1179648 | tf_op jit(solution)/shard_map/while/body/eval_jaxpr/psum | solution.py:47
  1081.2 60.1 %all-reduce.46.cloned.1.call-start = ((), (), s32[]{:S(2)}) async-start(), calls=%async_computation.34 | async-start | bytes 1179648 | tf_op jit(solution)/shard_map/while/body/eval_jaxpr/psum | solution.py:47
  1147.3 93.8 %all-gather.61.cloned.1.call-start = ((), (), s32[]{:S(2)}) async-start(), calls=%async_computation.22 | async-start | bytes 4700160 | tf_op jit(solution)/shard_map/while/body/eval_jaxpr/all_gather | solution.py:390
  1149.2 146.5 %all-gather.63.cloned.1.call-start = ((), (), s32[]{:S(2)}) async-start(), calls=%async_computation.23 | async-start | bytes 1566720 | tf_op jit(solution)/shard_map/while/body/eval_jaxpr/all_gather | solution.py:392
  1150.9 231.3 %all-reduce.32.cloned.1.call-start = ((), (), s32[]{:S(2)}) async-start(), calls=%async_computation.24 | async-start | bytes 2359296 | tf_op jit(solution)/shard_map/while/body/eval_jaxpr/psum | solution.py:43
  1298.9 109.4 %all-gather.67.cloned.1.call-start = ((), (), s32[]{:S(2)}) async-start(), calls=%async_computation.26 | async-start | bytes 5640192 | tf_op jit(solution)/shard_map/while/body/eval_jaxpr/all_gather | solution.py:394
  1300.9 195.0 %all-gather.65.cloned.1.call-start = ((), (), s32[]{:S(2)}) async-start(), calls=%async_computation.25 | async-start | bytes 5640192 | tf_op jit(solution)/shard_map/while/body/eval_jaxpr/all_gather | solution.py:396
  1302.9 217.8 %all-reduce.34.cloned.1.call-start = ((), (), s32[]{:S(2)}) async-start(), calls=%async_computation.27 | async-start | bytes 2359296 | tf_op jit(solution)/shard_map/while/body/eval_jaxpr/psum | solution.py:43
  1502.3 101.0 %all-gather.69.cloned.1.call-start = ((), (), s32[]{:S(2)}) async-start(), calls=%async_computation.28 | async-start | bytes 4700160 | tf_op jit(solution)/shard_map/while/body/eval_jaxpr/all_gather | solution.py:390
  1502.9 171.5 %all-gather.55.cloned.1.call-start = ((), (), s32[]{:S(2)}) async-start(), calls=%async_computation.19 | async-start | bytes 1566720 | tf_op jit(solution)/shard_map/while/body/eval_jaxpr/all_gather | solution.py:392
  1682.7 108.0 %all-gather.59.cloned.1.call-start = ((), (), s32[]{:S(2)}) async-start(), calls=%async_computation.21 | async-start | bytes 5640192 | tf_op jit(solution)/shard_map/while/body/eval_jaxpr/all_gather | solution.py:394
  1683.3 195.0 %all-gather.57.cloned.1.call-start = ((), (), s32[]{:S(2)}) async-start(), calls=%async_computation.20 | async-start | bytes 5640192 | tf_op jit(solution)/shard_map/while/body/eval_jaxpr/all_gather | solution.py:396
  1684.1 233.9 %all-reduce.40.cloned.1.call-start = ((), (), s32[]{:S(2)}) async-start(), calls=%async_computation.31 | async-start | bytes 1179648 | tf_op jit(solution)/shard_map/while/body/eval_jaxpr/psum | solution.py:47
  2019.7 59.1 %all-reduce.44.cloned.1.call-start = ((), (), s32[]{:S(2)}) async-start(), calls=%async_computation.33 | async-start | bytes 1179648 | tf_op jit(solution)/shard_map/while/body/eval_jaxpr/psum | solution.py:47
  2056.1 60.1 %all-reduce.46.cloned.1.call-start = ((), (), s32[]{:S(2)}) async-start(), calls=%async_computation.34 | async-start | bytes 1179648 | tf_op jit(solution)/shard_map/while/body/eval_jaxpr/psum | solution.py:47
  2127.4 187.2 %reduce-scatter.19.cloned.1.call-start = ((), (), s32[]{:S(2)}) async-start(), calls=%async_computation.18 | async-start | bytes 1253376
  2137.1 275.1 %reduce-scatter.13.cloned.1.call-start = ((), (), s32[]{:S(2)}) async-start(), calls=%async_computation.15 | async-start | bytes 6266880 | tf_op jit(solution)/shard_map/reduce_scatter | solution.py:444
  2143.7 545.4 %reduce-scatter.11.cloned.1.call-start = ((), (), s32[]{:S(2)}) async-start(), calls=%async_computation.14 | async-start | bytes 18800640 | tf_op jit(solution)/shard_map/reduce_scatter | solution.py:442
  2162.2 847.7 %reduce-scatter.17.cloned.1.call-start = ((), (), s32[]{:S(2)}) async-start(), calls=%async_computation.17 | async-start | bytes 22560768 | tf_op jit(solution)/shard_map/reduce_scatter | solution.py:448
  2184.8 1144.7 %reduce-scatter.15.cloned.1.call-start = ((), (), s32[]{:S(2)}) async-start(), calls=%async_computation.16 | async-start | bytes 22560768 | tf_op jit(solution)/shard_map/reduce_scatter | solution.py:446
  (262 other events, 4042.8 us)
Sparse Core Ops, SparseCore 0:
  13.9 128.5 all-reduce.29
  177.1 81.9 all-gather.60
  262.8 58.0 all-gather.62
  324.2 18.5 all-reduce.31
  346.0 87.3 all-gather.66
  436.7 84.2 all-gather.64
  549.4 78.9 all-gather.68
  631.5 57.8 all-gather.54
  708.0 18.3 all-reduce.35
  729.2 86.8 all-gather.58
  819.3 84.1 all-gather.56
  1045.0 20.4 all-reduce.41
  1081.3 20.0 all-reduce.43
  1121.3 20.0 all-reduce.45
  1151.5 83.1 all-gather.60
  1238.3 57.3 all-gather.62
  1299.0 18.5 all-reduce.31
  1321.0 87.3 all-gather.66
  1411.7 84.2 all-gather.64
  1524.3 78.9 all-gather.68
  1606.4 57.8 all-gather.54
  1682.8 18.3 all-reduce.35
  1703.9 86.8 all-gather.58
  1794.1 84.1 all-gather.56
  2019.8 20.4 all-reduce.41
  2056.2 20.0 all-reduce.43
  2096.2 20.0 all-reduce.45
  2137.2 125.5 reduce-scatter.18
  2269.6 142.6 reduce-scatter.12
  2419.6 269.3 reduce-scatter.10
  2696.5 313.2 reduce-scatter.16
  3016.4 312.9 reduce-scatter.14
  (6 shorter events, 107.0 us)
where the time goes:
time: 3350 us; the launch traced here: 3340 us
  waiting for transfers between devices  2090 us (62%)
  blocking collectives  437 us (13%)
  matrix products  304 us (9%)
  local copies, waits for them, and re-layouts  293 us (9%)
  other arithmetic  114 us (3%)
  starting transfers between devices  70 us (2%)
    all_gather x4, waiting for transfers between devices, gather_layer(): lax.all_gather(output_weight[layer_idx], ('dp', 'seq'), axis=1, tiled=True)  326 us
    reduce_scatter x1, waiting for transfers between devices, shards(): lax.psum_scatter(summed[6], ('dp', 'seq'), scatter_dimension=2, tiled=True)  321 us
    reduce_scatter x1, waiting for transfers between devices, shards(): lax.psum_scatter(summed[4], ('dp', 'seq'), scatter_dimension=1, tiled=True)  320 us
    reduce_scatter x1, waiting for transfers between devices, shards(): lax.psum_scatter(summed[0], ('dp', 'seq'), scatter_dimension=1, tiled=True)  277 us
    all_gather x4, waiting for transfers between devices, gather_layer(): lax.all_gather(hidden_weight[layer_idx], ('dp', 'seq'), axis=0, tiled=True)  219 us
    all_gather x4, blocking collectives, gather_layer(): lax.all_gather(pair_bias[layer_idx], ('dp', 'seq'), axis=2, tiled=True)  164 us
    all_gather x4, waiting for transfers between devices, gather_layer(): lax.all_gather(triple_weight[layer_idx], ('dp', 'seq'), axis=0, tiled=True)  159 us
    while x2, blocking collectives  152 us
  transfers between devices with their start and end apart: 54, of which 33 were waited for; matrix products, arithmetic and copies ran while one was open for 14% of the time, Pallas kernels for 0%

commit v1 on v0

v1 whole, which is shorter than its diff:
```python
from functools import partial

import jax
import jax.numpy as jnp
from jax import lax
from jax.experimental import pallas as pl
from jax.experimental.pallas import tpu as pltpu
from jax.sharding import PartitionSpec as P

HEAD_DIM = 72
LANES = 128
EPSILON = 1e-06
VMEM_LIMIT = 48 * 1024 * 1024
f32 = jnp.float32
bf16 = jnp.bfloat16


def bits_of(size):
    return max(size.bit_length() - 1, 0)


def pxor(value, axis, flip):
    size = lax.axis_size(axis)
    return lax.ppermute(value, axis, [(i, i ^ flip) for i in range(size)])


def swap(value):
    return pxor(value, "tensor", 1)


def take(value, axis, index):
    return lax.dynamic_index_in_dim(value, index, axis, keepdims=False)


def gather_tree(block, axis, order):
    blocks = {0: block}
    for bit in order:
        for rel in list(blocks):
            blocks[rel | (1 << bit)] = pxor(blocks[rel], axis, 1 << bit)
    return [blocks[rel] for rel in range(len(blocks))]


def place_kernel(idx_ref, *refs):
    blocks, out_ref = refs[:-1], refs[-1]
    for rel, block in enumerate(blocks):
        out_ref[0, jnp.bitwise_xor(idx_ref[1], rel)] = block[0]


def place(blocks, outer_index, inner_index):
    outer, rows, cols = blocks[0].shape
    inner = len(blocks)
    start = jnp.int32(0) if outer_index is None else outer_index
    index = jnp.stack([start, inner_index]).astype(jnp.int32)
    return pl.pallas_call(
        place_kernel,
        grid_spec=pltpu.PrefetchScalarGridSpec(
            num_scalar_prefetch=1,
            grid=(outer,),
            in_specs=[pl.BlockSpec((1, rows, cols), lambda o, idx: (o, 0, 0))] * inner,
            out_specs=pl.BlockSpec(
                (1, inner, rows, cols), lambda o, idx: (jnp.bitwise_xor(idx[0], o), 0, 0, 0)
            ),
        ),
        out_shape=jax.ShapeDtypeStruct((outer, inner, rows, cols), blocks[0].dtype),
        compiler_params=pltpu.CompilerParams(vmem_limit_bytes=VMEM_LIMIT),
        name="place",
    )(index, *blocks)


def finish_gather(halves, dp_index, seq_index):
    count = bits_of(lax.axis_size("seq"))
    whole = []
    for which, half in enumerate(halves):
        order = list(range(count))
        if which % 2:
            order.reverse()
        placed = place(gather_tree(half, "seq", order), dp_index, seq_index)
        whole.append(placed.reshape(-1, half.shape[-1]))
    return whole


def scatter_bits(value, axis, order, first_dim):
    index = lax.axis_index(axis)
    left = list(reversed(range(bits_of(lax.axis_size(axis)))))
    for bit in order:
        dim = first_dim + left.index(bit)
        mine = (index >> bit) & 1
        other = pxor(take(value, dim, 1 - mine), axis, 1 << bit)
        value = (take(value, dim, mine).astype(f32) + other.astype(f32)).astype(value.dtype)
        left.remove(bit)
    return value


def scatter_seq(grad, which):
    parts, clusters = lax.axis_size("seq"), lax.axis_size("dp")
    count = bits_of(parts)
    rows = grad.shape[0] // (parts * clusters)
    order = list(range(count))
    if which % 2 == 0:
        order.reverse()
    view = grad.reshape((clusters,) + (2,) * count + (rows, grad.shape[1]))
    return scatter_bits(view, "seq", order, 1)


def scatter_dp_tree(value):
    count = bits_of(lax.axis_size("dp"))
    view = value.reshape((2,) * count + value.shape[1:])
    return scatter_bits(view, "dp", list(range(count)), 0)


def gather_small(value, axis):
    size, index = lax.axis_size(axis), lax.axis_index(axis)
    out = jnp.zeros((size,) + value.shape, value.dtype)
    for rel in range(size):
        part = value if rel == 0 else pxor(value, axis, rel)
        out = lax.dynamic_update_slice_in_dim(out, part[None], index ^ rel, 0)
    return out


def scatter_small(value, axis):
    size, index = lax.axis_size(axis), lax.axis_index(axis)
    total = take(value, 0, index)
    for rel in range(1, size):
        total = total + pxor(take(value, 0, index ^ rel), axis, rel)
    return total


def sum_small(value, axis):
    total = value
    for rel in range(1, lax.axis_size(axis)):
        total = total + pxor(value, axis, rel)
    return total


def dispatch(rows):
    size, index = lax.axis_size("seq"), lax.axis_index("seq")
    view = rows.reshape(rows.shape[0], size, rows.shape[1] // size, rows.shape[2])
    parts = []
    for rel in range(size):
        part = take(view, 1, index ^ rel)
        parts.append(part if rel == 0 else pxor(part, "seq", rel))
    return jnp.stack(parts, axis=1)


def collect(parts):
    size, index = lax.axis_size("seq"), lax.axis_index("seq")
    blocks = []
    for rel in range(size):
        block = parts[:, rel]
        blocks.append(block if rel == 0 else pxor(block, "seq", rel))
    placed = place(blocks, None, index)
    return placed.reshape(placed.shape[0], -1, placed.shape[-1])


def head_windows(width):
    spans = []
    for first in range(0, width, HEAD_DIM):
        low = first // LANES * LANES
        high = min(-(-(first + HEAD_DIM) // LANES) * LANES, width)
        spans.append((first, low, high))
    return spans


def head_mask(first, low, high):
    lane = lax.broadcasted_iota(jnp.int32, (1, high - low), 1) + low
    return jnp.where((lane >= first) & (lane < first + HEAD_DIM), 1.0, 0.0).astype(bf16)


def row_dot(left, right):
    return lax.dot_general(left, right, (((1,), (1,)), ((), ())), preferred_element_type=f32)


def col_dot(left, right):
    return lax.dot_general(left, right, (((0,), (0,)), ((), ())), preferred_element_type=f32)


def softmax_probs(queries, key_rows, apart):
    scores = row_dot(queries, key_rows) * (HEAD_DIM ** (-0.5))
    if apart is not None:
        scores = jnp.where(apart, -1e30, scores)
    top = jnp.max(scores, axis=-1, keepdims=True)
    weights = jnp.exp(scores - top)
    return weights * (1.0 / jnp.sum(weights, axis=-1, keepdims=True))


def tokens_apart(rows, period):
    if period is None:
        return None
    one = lax.broadcasted_iota(jnp.int32, (rows, rows), 0)
    two = lax.broadcasted_iota(jnp.int32, (rows, rows), 1)
    return lax.rem(one, period) != lax.rem(two, period)


def attend_kernel(period, qk_ref, v_ref, out_ref, acc_ref):
    rows, width = v_ref.shape[1], v_ref.shape[2]
    apart = tokens_apart(rows, period)
    queries, key_rows, value_rows = qk_ref[0, :, :width], qk_ref[0, :, width:], v_ref[0]
    acc_ref[...] = jnp.zeros_like(acc_ref)
    for first, low, high in head_windows(width):
        mask = head_mask(first, low, high)
        probs = softmax_probs(queries[:, low:high] * mask, key_rows[:, low:high], apart)
        acc_ref[:, low:high] += jnp.dot(
            probs.astype(bf16), value_rows[:, low:high] * mask, preferred_element_type=f32
        )
    out_ref[0] = acc_ref[...].astype(bf16)


def attend(qk, values, period):
    blocks, rows, width = values.shape
    return pl.pallas_call(
        partial(attend_kernel, period),
        grid=(blocks,),
        out_shape=jax.ShapeDtypeStruct(values.shape, bf16),
        in_specs=[
            pl.BlockSpec((1, rows, 2 * width), lambda b: (b, 0, 0)),
            pl.BlockSpec((1, rows, width), lambda b: (b, 0, 0)),
        ],
        out_specs=pl.BlockSpec((1, rows, width), lambda b: (b, 0, 0)),
        scratch_shapes=[pltpu.VMEM((rows, width), f32)],
        compiler_params=pltpu.CompilerParams(vmem_limit_bytes=VMEM_LIMIT),
        name="attend",
    )(qk, values)


def attend_grad_kernel(period, qk_ref, v_ref, da_ref, dqk_ref, dv_ref, acc_q, acc_k, acc_v):
    rows, width = v_ref.shape[1], v_ref.shape[2]
    apart = tokens_apart(rows, period)
    queries, key_rows, value_rows = qk_ref[0, :, :width], qk_ref[0, :, width:], v_ref[0]
    grad_att = da_ref[0]
    factor = HEAD_DIM ** (-0.5)
    for acc in (acc_q, acc_k, acc_v):
        acc[...] = jnp.zeros_like(acc)
    for first, low, high in head_windows(width):
        mask = head_mask(first, low, high)
        q_own = queries[:, low:high] * mask
        k_own = key_rows[:, low:high] * mask
        g_own = grad_att[:, low:high] * mask
        probs = softmax_probs(q_own, k_own, apart)
        grad_probs = row_dot(g_own, value_rows[:, low:high])
        inner = jnp.sum(grad_probs * probs, axis=-1, keepdims=True)
        grad_scores = (probs * (grad_probs - inner)).astype(bf16)
        acc_q[:, low:high] += jnp.dot(grad_scores, k_own, preferred_element_type=f32)
        acc_k[:, low:high] += col_dot(grad_scores, q_own)
        acc_v[:, low:high] += col_dot(probs.astype(bf16), g_own)
    dqk_ref[0, :, :width] = (acc_q[...] * factor).astype(bf16)
    dqk_ref[0, :, width:] = (acc_k[...] * factor).astype(bf16)
    dv_ref[0] = acc_v[...].astype(bf16)


def attend_grad(qk, values, grad_att, period):
    blocks, rows, width = values.shape
    wide = pl.BlockSpec((1, rows, 2 * width), lambda b: (b, 0, 0))
    thin = pl.BlockSpec((1, rows, width), lambda b: (b, 0, 0))
    return pl.pallas_call(
        partial(attend_grad_kernel, period),
        grid=(blocks,),
        out_shape=(
            jax.ShapeDtypeStruct(qk.shape, bf16),
            jax.ShapeDtypeStruct(values.shape, bf16),
        ),
        in_specs=[wide, thin, thin],
        out_specs=(wide, thin),
        scratch_shapes=[pltpu.VMEM((rows, width), f32)] * 3,
        compiler_params=pltpu.CompilerParams(vmem_limit_bytes=VMEM_LIMIT),
        name="attend_grad",
    )(qk, values, grad_att)


def normalize(values):
    average = jnp.mean(values, axis=-1, keepdims=True)
    centered = values - average
    variance = jnp.mean(centered * centered, axis=-1, keepdims=True)
    return centered * lax.rsqrt(variance + EPSILON)


def modulate(values, shift_row, scale_row):
    return normalize(values) * (1.0 + scale_row) + shift_row


def both_clips(own):
    return jnp.concatenate([own, swap(own)], axis=0)


def own_total(partial_sum):
    rows = partial_sum.shape[0] // 2
    return partial_sum[:rows] + swap(partial_sum[rows:])


def mm(left, right):
    return jnp.dot(left, right, preferred_element_type=f32)


def layer_forward(x, mods, weights, biases, temporal):
    (w_qk, w_vo), (w_up_a, w_up_b), (w_down_a, w_down_b) = weights
    bias_q, bias_v, bias_out, bias_up, bias_down = biases
    width = bias_q.shape[0]
    half = w_up_a.shape[1]
    patches = x.shape[0]
    normed_one = both_clips(modulate(x, mods[0], mods[1]).astype(bf16))
    qk = (mm(normed_one, w_qk) + jnp.concatenate([bias_q, jnp.zeros_like(bias_q)])).astype(bf16)
    values = (mm(normed_one, w_vo[:, :width]) + bias_v).astype(bf16)
    clips = normed_one.shape[0] // patches
    qk = qk.reshape(clips, patches, -1)
    values = values.reshape(clips, patches, -1)
    if temporal:
        period = patches // lax.axis_size("seq")
        qk = dispatch(qk).reshape(qk.shape)
        values = dispatch(values).reshape(values.shape)
        attended = attend(qk, values, period)
        attended = collect(attended.reshape(clips, -1, period, width))
    else:
        attended = attend(qk, values, None)
    attended = attended.reshape(clips * patches, width)
    w_out = w_vo[:, width:]
    branch = own_total(row_dot(attended, w_out)) + bias_out
    x_mid = x + mods[2] * branch
    normed_two = both_clips(modulate(x_mid, mods[3], mods[4]).astype(bf16))
    pre_a = mm(normed_two, w_up_a) + bias_up[:half]
    pre_b = mm(normed_two, w_up_b) + bias_up[half:]
    hidden_a = jax.nn.gelu(pre_a, approximate=True).astype(bf16)
    hidden_b = jax.nn.gelu(pre_b, approximate=True).astype(bf16)
    mlp = own_total(row_dot(hidden_a, w_down_a) + row_dot(hidden_b, w_down_b)) + bias_down
    x_next = x_mid + mods[5] * mlp
    saved = (
        x, normed_one, qk, values, attended, branch, x_mid, normed_two, pre_a, pre_b,
        hidden_a, hidden_b, mlp, w_out,
    )
    return x_next, saved


def total(rows):
    return jnp.sum(rows, axis=0, dtype=f32)


def layer_backward(g, mods, weights, saved, temporal):
    (w_qk, w_vo), (w_up_a, w_up_b), (w_down_a, w_down_b) = weights
    (
        x, normed_one, qk, values, attended, branch, x_mid, normed_two, pre_a, pre_b,
        hidden_a, hidden_b, mlp, w_out,
    ) = saved
    patches = x.shape[0]
    width = values.shape[-1]
    grad_gate_two = total(g * mlp)
    grad_mlp = both_clips((mods[5] * g).astype(bf16))
    down_grads = [col_dot(grad_mlp, hidden_a).astype(bf16), col_dot(grad_mlp, hidden_b).astype(bf16)]
    pres = []
    for pre, w_down in ((pre_a, w_down_a), (pre_b, w_down_b)):
        back = jax.vjp(partial(jax.nn.gelu, approximate=True), pre)[1]
        pres.append(back(mm(grad_mlp, w_down))[0].astype(bf16))
    up_grads = [col_dot(normed_two, pres[0]).astype(bf16), col_dot(normed_two, pres[1]).astype(bf16)]
    grad_normed_two = own_total(row_dot(pres[0], w_up_a) + row_dot(pres[1], w_up_b))
    back_two = jax.vjp(modulate, x_mid, mods[3], mods[4])[1]
    grad_norm, grad_shift_two, grad_scale_two = back_two(grad_normed_two)
    g_mid = g + grad_norm
    grad_gate_one = total(g_mid * branch)
    grad_branch = both_clips((mods[2] * g_mid).astype(bf16))
    out_grad = col_dot(grad_branch, attended).astype(bf16)
    grad_att = mm(grad_branch, w_out).astype(bf16)
    clips = grad_att.shape[0] // patches
    grad_att = grad_att.reshape(clips, patches, width)
    if temporal:
        period = patches // lax.axis_size("seq")
        grad_att = dispatch(grad_att).reshape(grad_att.shape)
        grad_qk, grad_v = attend_grad(qk, values, grad_att, period)
        pair_grad = jnp.stack([total(grad_qk.reshape(-1, 2 * width)[:, :width]), total(grad_v.reshape(-1, width))])
        grad_qk = collect(grad_qk.reshape(clips, -1, period, 2 * width))
        grad_v = collect(grad_v.reshape(clips, -1, period, width))
    else:
        grad_qk, grad_v = attend_grad(qk, values, grad_att, None)
        pair_grad = jnp.stack([total(grad_qk.reshape(-1, 2 * width)[:, :width]), total(grad_v.reshape(-1, width))])
    grad_qk = grad_qk.reshape(clips * patches, 2 * width)
    grad_v = grad_v.reshape(clips * patches, width)
    qk_grad = col_dot(normed_one, grad_qk).astype(bf16)
    v_grad = col_dot(normed_one, grad_v).astype(bf16)
    grad_normed_one = own_total(row_dot(grad_qk, w_qk) + row_dot(grad_v, w_vo[:, :width]))
    back_one = jax.vjp(modulate, x, mods[0], mods[1])[1]
    grad_norm, grad_shift_one, grad_scale_one = back_one(grad_normed_one)
    g_below = g_mid + grad_norm
    mod_grads = jnp.stack(
        [grad_shift_one, grad_scale_one, grad_gate_one, grad_shift_two, grad_scale_two, grad_gate_two]
    )
    bias_grads = (
        pair_grad,
        total(grad_branch),
        jnp.concatenate([total(pres[0]), total(pres[1])]),
        total(grad_mlp),
    )
    grads = (down_grads, up_grads, [qk_grad, jnp.concatenate([v_grad, out_grad], axis=1)])
    return g_below, mod_grads, bias_grads, grads


def shards(
    tokens,
    conditioning,
    cotangent,
    modulation_weight,
    modulation_bias,
    triple_weight,
    pair_bias,
    out_weight,
    out_bias,
    hidden_weight,
    hidden_bias,
    output_weight,
    output_bias,
):
    layers, _, _, width = triple_weight.shape
    model = tokens.shape[3]
    patches = tokens.shape[2]
    own_clips = tokens.shape[0] // lax.axis_size("tensor")
    all_clips = conditioning.shape[0]
    assert own_clips == 1 and tokens.shape[1] == 1 and layers == 2
    units = hidden_weight.shape[2]
    half = units // 2
    dp_index, seq_index = lax.axis_index("dp"), lax.axis_index("seq")
    core = lax.axis_index("tensor")
    n_dp, n_seq, n_core = lax.axis_size("dp"), lax.axis_size("seq"), lax.axis_size("tensor")

    def unit(layer, which):
        if which == 0:
            triple = triple_weight[layer]
            first = jnp.concatenate([triple[:, 0], triple[:, 1]], axis=1)
            second = jnp.concatenate([triple[:, 2], out_weight[layer].T], axis=1)
        else:
            rows = hidden_weight[layer] if which == 1 else output_weight[layer].T
            first, second = rows[:, :half], rows[:, half:]
        return jnp.stack([first, second])

    shard = [[unit(layer, which) for which in range(3)] for layer in range(layers)]
    gathered = [[None] * 3 for _ in range(layers)]
    dp_order = list(reversed(range(bits_of(n_dp))))
    first_blocks = jnp.stack(gather_tree(shard[0][0], "dp", dp_order), axis=1)
    gathered[0][0] = finish_gather([first_blocks[0], first_blocks[1]], dp_index, seq_index)

    act_cond, silu_back = jax.vjp(jax.nn.silu, conditioning)
    act_low = act_cond.astype(bf16)
    local_term = jnp.einsum("cd,lde->cle", act_low, modulation_weight, preferred_element_type=f32)
    bias_cols = modulation_bias.shape[1]
    offset = ((dp_index * n_seq + seq_index) * n_core + core) * bias_cols
    bias_full = lax.dynamic_update_slice(
        jnp.zeros((layers, local_term.shape[2]), f32), modulation_bias.astype(f32), (jnp.int32(0), offset)
    )
    contribution = (local_term + bias_full[None]).reshape(n_dp, n_core, -1)
    contribution = take(contribution, 1, core) + swap(take(contribution, 1, 1 - core))
    mods = sum_small(scatter_small(contribution, "dp"), "seq").reshape(layers, 6, model)

    packed = jnp.concatenate(
        [pair_bias.reshape(layers, -1), out_bias, hidden_bias.reshape(layers, -1), output_bias], axis=1
    )
    spread = gather_small(gather_small(packed, "seq"), "dp").reshape(n_dp * n_seq, layers, -1)
    cuts, at = [], 0
    for size in (pair_bias.shape[3], pair_bias.shape[3], out_bias.shape[1], hidden_bias.shape[2], output_bias.shape[1]):
        cuts.append(spread[:, :, at : at + size].transpose(1, 0, 2).reshape(layers, -1).astype(f32))
        at += size

    late = [[(0, 1), (0, 2)], [(1, 0), (1, 1), (1, 2)]]
    for group in late:
        stacked = jnp.concatenate([shard[layer][which] for layer, which in group])
        blocks = lax.all_gather(stacked, "dp", axis=1)
        for pos, (layer, which) in enumerate(group):
            gathered[layer][which] = finish_gather([blocks[2 * pos], blocks[2 * pos + 1]], None, seq_index)

    x = take(tokens, 0, core).reshape(patches, model).astype(f32)
    kept = []
    for layer in range(layers):
        biases = [cut[layer] for cut in cuts]
        x, saved = layer_forward(x, mods[layer], gathered[layer], biases, layer == 1)
        kept.append(saved)

    def to_both(own):
        other = swap(own)
        pair = jnp.stack([jnp.where(core == 0, own, other), jnp.where(core == 0, other, own)])
        return pair.reshape((2, 1) + own.shape)

    activations = to_both(x.astype(bf16))
    g = take(cotangent, 0, core).reshape(patches, model).astype(f32)
    mod_grads, bias_grads = [None] * layers, [None] * layers
    done = [[None] * 3 for _ in range(layers)]

    def reduce_units(pairs, tree):
        blocks = [scatter_seq(grad, which) for pair in pairs for which, grad in enumerate(pair)]
        stacked = jnp.stack(blocks, axis=1)
        if tree:
            return scatter_dp_tree(stacked)
        return lax.psum_scatter(stacked, "dp", scatter_dimension=0)

    for layer in reversed(range(layers)):
        g, mod_grads[layer], bias_grads[layer], grads = layer_backward(
            g, mods[layer], gathered[layer], kept[layer], layer == 1
        )
        mlp_units = reduce_units(grads[:2], False)
        done[layer][2] = mlp_units[:2]
        done[layer][1] = mlp_units[2:]
        done[layer][0] = reduce_units(grads[2:], layer == 0)
    input_grad = to_both(g)

    def stack_layers(which, build):
        return jnp.stack([build(done[layer][which].astype(f32)) for layer in range(layers)])

    triple_grad = stack_layers(
        0, lambda u: jnp.stack([u[0][:, :width], u[0][:, width:], u[1][:, :width]], axis=1)
    )
    out_grad = stack_layers(0, lambda u: u[1][:, width:].T)
    hidden_grad = stack_layers(1, lambda u: jnp.concatenate([u[0], u[1]], axis=1))
    output_grad = stack_layers(2, lambda u: jnp.concatenate([u[0], u[1]], axis=1).T)

    def cut_rows(rows):
        return rows.reshape(rows.shape[:-1] + (n_dp * n_seq, -1))

    packed_grads = []
    for layer in range(layers):
        pair_grad, grad_out_bias, grad_up_bias, grad_down_bias = (cut_rows(b) for b in bias_grads[layer])
        packed_grads.append(
            jnp.concatenate([pair_grad[0], pair_grad[1], grad_out_bias, grad_up_bias, grad_down_bias], axis=1)
        )
    bias_rows = jnp.stack(packed_grads, axis=1).reshape(n_dp, n_seq, layers, -1)
    bias_rows = scatter_small(scatter_small(bias_rows.transpose(1, 0, 2, 3), "seq"), "dp")
    sizes = (2 * pair_bias.shape[3], out_bias.shape[1], hidden_bias.shape[2], output_bias.shape[1])
    ends = [sum(sizes[: i + 1]) for i in range(4)]
    pair_out = bias_rows[:, : ends[0]].reshape(layers, 2, 1, -1)
    out_bias_grad = bias_rows[:, ends[0] : ends[1]]
    hidden_bias_grad = bias_rows[:, ends[1] : ends[2]].reshape(layers, 1, -1)
    output_bias_grad = bias_rows[:, ends[2] : ends[3]]

    own_mods = sum_small(jnp.stack(mod_grads).reshape(-1), "seq").astype(bf16)
    grad_mods = gather_small(gather_small(own_mods, "tensor"), "dp").reshape(all_clips, layers, -1)
    modulation_weight_grad = jnp.einsum("cd,cle->lde", act_low, grad_mods, preferred_element_type=f32)
    modulation_bias_grad = lax.dynamic_slice_in_dim(
        jnp.sum(grad_mods, axis=0, dtype=f32), offset, bias_cols, 1
    )
    grad_act = jnp.einsum("cle,lde->cd", grad_mods, modulation_weight, preferred_element_type=f32)
    cond_grad = silu_back(grad_act)[0]
    return (
        activations,
        input_grad,
        cond_grad,
        modulation_weight_grad,
        modulation_bias_grad,
        triple_grad,
        pair_out,
        out_grad,
        out_bias_grad,
        hidden_grad,
        hidden_bias_grad,
        output_grad,
        output_bias_grad,
    )


def solution(mesh):
    owners = ("dp", "seq")
    everyone = ("dp", "seq", "tensor")
    rows = P("dp", "seq", None, None)
    weights = (
        P(None, everyone, None),
        P(None, everyone),
        P(None, owners, None, "tensor"),
        P(None, None, "tensor", owners),
        P(None, "tensor", owners),
        P(None, owners),
        P(None, owners, "tensor"),
        P(None, "tensor", owners),
        P(None, "tensor", owners),
        P(None, owners),
    )
    return jax.shard_map(
        shards,
        mesh=mesh,
        in_specs=(rows, P(None, everyone), rows) + weights,
        out_specs=(rows, rows, P(None, everyone)) + weights,
        check_vma=False,
    )
```

time: 3350 us -> 1020 us (0.30)
  waiting for transfers between devices: 2090 us -> 449 us
  blocking collectives: 437 us -> 0 us
  local copies, waits for them, and re-layouts: 293 us -> 121 us
  matrix products: 304 us -> 137 us
  Pallas kernels: 0 us -> 74.4 us
  starting transfers between devices: 70 us -> 131 us
    reduce_scatter x4 -> x3, waiting for transfers between devices: 1010 us -> 0.02 us  [reduce_units(): return lax.psum_scatter(stacked, 'dp', scatter_dimension=0)]
    all_gather x16 -> x2, waiting for transfers between devices: 800 us -> 0.02 us  [shards(): blocks = lax.all_gather(stacked, 'dp', axis=1)]
    ppermute x0 -> x127, waiting for transfers between devices: none -> 449 us  [pxor(): return lax.ppermute(value, axis, [(i, i ^ flip) for i in range(size)])]
    psum x17 -> x0, waiting for transfers between devices: 251 us -> none  [the longest x1 132 us: shards(): lax.psum(local_term + bias_full[None], ('dp', 'seq', 'tensor'))]
    dot_general x74 -> x44, matrix products: 302 us -> 136 us  [the longest x14 55.3 us: mm(): return jnp.dot(left, right, preferred_element_type=f32)]
    all_gather x4 -> x0, blocking collectives: 164 us -> none  [gather_layer(): lax.all_gather(pair_bias[layer_idx], ('dp', 'seq'), axis=2, tiled=True)]
    while x2 -> x0, blocking collectives: 152 us -> none
    ppermute x0 -> x127, starting transfers between devices: none -> 130 us  [pxor(): return lax.ppermute(value, axis, [(i, i ^ flip) for i in range(size)])]
  transfers between devices with their start and end apart: 54 -> 132, of which waited for: 33 -> 48; matrix products, arithmetic and copies ran while one was open for 14% -> 27% of each run, Pallas kernels for 0% -> 7%
where the time goes in v1:
time: 1020 us
  waiting for transfers between devices  449 us (44%)
  matrix products  137 us (13%)
  starting transfers between devices  131 us (13%)
  local copies, waits for them, and re-layouts  121 us (12%)
  other arithmetic  88.9 us (9%)
  Pallas kernels  74.4 us (7%)
  between operations  17.7 us (2%)
    ppermute x127, waiting for transfers between devices, pxor(): return lax.ppermute(value, axis, [(i, i ^ flip) for i in range(size)])  449 us
    ppermute x127, starting transfers between devices, pxor(): return lax.ppermute(value, axis, [(i, i ^ flip) for i in range(size)])  130 us
    dot_general x14, matrix products, mm(): return jnp.dot(left, right, preferred_element_type=f32)  55.3 us
    unnamed x399, local copies, waits for them, and re-layouts  42.3 us
    dot_general x14, matrix products, col_dot(): lax.dot_general(left, right, (((0,), (0,)), ((), ())), preferred_element_...  41.7 us
    dot_general x14, matrix products, row_dot(): lax.dot_general(left, right, (((1,), (1,)), ((), ())), preferred_element_...  36.9 us
    pallas_call x15, Pallas kernels, place(): pl.pallas_call(place_kernel, grid_spec=pltpu.PrefetchScalarGridSpec(num_s...  36.1 us
    pallas_call x2, Pallas kernels, attend_grad(): pl.pallas_call(partial(attend_grad_kernel, period), grid=(blocks,), out_s...  21.1 us
  transfers between devices with their start and end apart: 132, of which 48 were waited for; matrix products, arithmetic and copies ran while one was open for 27% of the time, Pallas kernels for 7%

profile of v1, /device:TPU:0, one launch (start us, length us, event | category | flops | bytes accessed | tf_op | source)
XLA Modules:
  0.0 1018.2 jit_solution(873372649376765195)
XLA Ops:
  31.5 17.3 %collective-permute-done.17 = bf16[4,2,360]{2,1,0:T(2,128)(2,1)S(1)} collective-permute-done((bf16[4,2,360]{2,1,0:T(2,128)(2,1)}, bf16[4,2,360]{2,1,0:T(2,128)(2,1)S(1)}, u32[]{:S(2)}, u32[]{:S(2)}) %collective-permute-start.17) | collective-permute-done | bytes 5792 | tf_op jit(solution)/shard_map/ppermute | solution.py:24
  69.7 18.0 %collective-permute-done.10 = bf16[2,72,1152]{2,1,0:T(8,128)(2,1)S(1)} collective-permute-done((bf16[2,72,1152]{2,1,0:T(8,128)(2,1)}, bf16[2,72,1152]{2,1,0:T(8,128)(2,1)S(1)}, u32[]{:S(2)}, u32[]{:S(2)}) %collective-permute-start.10) | collective-permute-done | bytes 331808 | tf_op jit(solution)/shard_map/ppermute | solution.py:24
  93.9 10.7 %collective-permute-done.21.refs_2_ = bf16[4,72,1152]{2,1,0:T(8,128)(2,1)} collective-permute-done((bf16[4,72,1152]{2,1,0:T(8,128)(2,1)S(1)}, bf16[4,72,1152]{2,1,0:T(8,128)(2,1)}, u32[]{:S(2)}, u32[]{:S(2)}) %collective-permute-start.21) | collective-permute-done | bytes 663584 | tf_op jit(solution)/shard_map/ppermute | solution.py:24
  110.6 13.0 %collective-permute-done.20.refs_1_ = bf16[4,72,1152]{2,1,0:T(8,128)(2,1)} collective-permute-done((bf16[4,72,1152]{2,1,0:T(8,128)(2,1)S(1)}, bf16[4,72,1152]{2,1,0:T(8,128)(2,1)}, u32[]{:S(2)}, u32[]{:S(2)}) %collective-permute-start.20) | collective-permute-done | bytes 663584 | tf_op jit(solution)/shard_map/ppermute | solution.py:24
  123.6 11.2 %collective-permute-done.22.refs_3_ = bf16[4,72,1152]{2,1,0:T(8,128)(2,1)} collective-permute-done((bf16[4,72,1152]{2,1,0:T(8,128)(2,1)}, bf16[4,72,1152]{2,1,0:T(8,128)(2,1)}, u32[]{:S(2)}, u32[]{:S(2)}) %collective-permute-start.22) | collective-permute-done | bytes 663584 | tf_op jit(solution)/shard_map/ppermute | solution.py:24
  148.6 13.7 %attend.2 = bf16[2,256,576]{2,1,0:T(8,128)(2,1)S(1)} custom-call(bf16[2,256,1152]{2,1,0:T(8,128)(2,1)S(1)} %bitcast.664, bf16[2,256,576]{2,1,0:T(8,128)(2,1)S(1)} %bitcast.660), custom_call_target="tpu_custom_call" | custom-call | tf_op jit(solution)/shard_map/attend/pallas_call | solution.py:210
  174.6 11.6 %collective-permute-done.32.refs_2_ = bf16[4,72,1152]{2,1,0:T(8,128)(2,1)} collective-permute-done((bf16[4,72,1152]{2,1,0:T(8,128)(2,1)}, bf16[4,72,1152]{2,1,0:T(8,128)(2,1)}, u32[]{:S(2)}, u32[]{:S(2)}) %collective-permute-start.32) | collective-permute-done | bytes 663584 | tf_op jit(solution)/shard_map/ppermute | solution.py:24
  191.0 10.0 collective-permute-done.25.refs_1_
  204.7 10.6 %collective-permute-done.28.refs_1_ = bf16[4,72,1152]{2,1,0:T(8,128)(2,1)} collective-permute-done((bf16[4,72,1152]{2,1,0:T(8,128)(2,1)S(1)}, bf16[4,72,1152]{2,1,0:T(8,128)(2,1)}, u32[]{:S(2)}, u32[]{:S(2)}) %collective-permute-start.28) | collective-permute-done | bytes 663584 | tf_op jit(solution)/shard_map/ppermute | solution.py:24
  218.3 11.2 %collective-permute-done.33.refs_3_ = bf16[4,72,1152]{2,1,0:T(8,128)(2,1)S(1)} collective-permute-done((bf16[4,72,1152]{2,1,0:T(8,128)(2,1)}, bf16[4,72,1152]{2,1,0:T(8,128)(2,1)S(1)}, u32[]{:S(2)}, u32[]{:S(2)}) %collective-permute-start.33) | collective-permute-done | bytes 663584 | tf_op jit(solution)/shard_map/ppermute | solution.py:24
  243.1 13.8 %collective-permute-done.30.refs_3_ = bf16[4,72,1152]{2,1,0:T(8,128)(2,1)} collective-permute-done((bf16[4,72,1152]{2,1,0:T(8,128)(2,1)}, bf16[4,72,1152]{2,1,0:T(8,128)(2,1)}, u32[]{:S(2)}, u32[]{:S(2)}) %collective-permute-start.30) | collective-permute-done | bytes 663584 | tf_op jit(solution)/shard_map/ppermute | solution.py:24
  286.9 12.8 %collective-permute-done.46.refs_2_ = bf16[4,72,1152]{2,1,0:T(8,128)(2,1)} collective-permute-done((bf16[4,72,1152]{2,1,0:T(8,128)(2,1)S(1)}, bf16[4,72,1152]{2,1,0:T(8,128)(2,1)}, u32[]{:S(2)}, u32[]{:S(2)}) %collective-permute-start.46) | collective-permute-done | bytes 663584 | tf_op jit(solution)/shard_map/ppermute | solution.py:24
  303.2 11.8 %collective-permute-done.39.refs_1_ = bf16[4,72,1152]{2,1,0:T(8,128)(2,1)} collective-permute-done((bf16[4,72,1152]{2,1,0:T(8,128)(2,1)S(1)}, bf16[4,72,1152]{2,1,0:T(8,128)(2,1)}, u32[]{:S(2)}, u32[]{:S(2)}) %collective-permute-start.39) | collective-permute-done | bytes 663584 | tf_op jit(solution)/shard_map/ppermute | solution.py:24
  316.6 11.8 %collective-permute-done.47.refs_3_ = bf16[4,72,1152]{2,1,0:T(8,128)(2,1)} collective-permute-done((bf16[4,72,1152]{2,1,0:T(8,128)(2,1)}, bf16[4,72,1152]{2,1,0:T(8,128)(2,1)}, u32[]{:S(2)}, u32[]{:S(2)}) %collective-permute-start.47) | collective-permute-done | bytes 663584 | tf_op jit(solution)/shard_map/ppermute | solution.py:24
  352.1 13.5 %collective-permute-done.49 = bf16[2,64,576]{2,1,0:T(8,128)(2,1)S(1)} collective-permute-done((bf16[2,64,576]{2,1,0:T(8,128)(2,1)S(1)}, bf16[2,64,576]{2,1,0:T(8,128)(2,1)S(1)}, u32[]{:S(2)}, u32[]{:S(2)}) %collective-permute-start.49) | collective-permute-done | bytes 147488 | tf_op jit(solution)/shard_map/ppermute | solution.py:24
  390.0 11.3 %collective-permute-done.63.refs_2_ = bf16[4,72,1152]{2,1,0:T(8,128)(2,1)} collective-permute-done((bf16[4,72,1152]{2,1,0:T(8,128)(2,1)}, bf16[4,72,1152]{2,1,0:T(8,128)(2,1)}, u32[]{:S(2)}, u32[]{:S(2)}) %collective-permute-start.63) | collective-permute-done | bytes 663584 | tf_op jit(solution)/shard_map/ppermute | solution.py:24
  407.4 9.5 collective-permute-done.56.refs_1_
  420.6 10.6 %collective-permute-done.59.refs_1_ = bf16[4,72,1152]{2,1,0:T(8,128)(2,1)} collective-permute-done((bf16[4,72,1152]{2,1,0:T(8,128)(2,1)}, bf16[4,72,1152]{2,1,0:T(8,128)(2,1)}, u32[]{:S(2)}, u32[]{:S(2)}) %collective-permute-start.59) | collective-permute-done | bytes 663584 | tf_op jit(solution)/shard_map/ppermute | solution.py:24
  433.0 12.3 %collective-permute-done.64.refs_3_ = bf16[4,72,1152]{2,1,0:T(8,128)(2,1)S(1)} collective-permute-done((bf16[4,72,1152]{2,1,0:T(8,128)(2,1)}, bf16[4,72,1152]{2,1,0:T(8,128)(2,1)S(1)}, u32[]{:S(2)}, u32[]{:S(2)}) %collective-permute-start.64) | collective-permute-done | bytes 663584 | tf_op jit(solution)/shard_map/ppermute | solution.py:24
  459.2 12.8 %collective-permute-done.61.refs_3_ = bf16[4,72,1152]{2,1,0:T(8,128)(2,1)} collective-permute-done((bf16[4,72,1152]{2,1,0:T(8,128)(2,1)}, bf16[4,72,1152]{2,1,0:T(8,128)(2,1)}, u32[]{:S(2)}, u32[]{:S(2)}) %collective-permute-start.61) | collective-permute-done | bytes 663584 | tf_op jit(solution)/shard_map/ppermute | solution.py:24
  544.8 13.8 %collective-permute-done.119 = bf16[4,2,72,1152]{3,2,0,1:T(8,128)(2,1)S(1)} collective-permute-done((bf16[4,2,72,1152]{3,2,0,1:T(8,128)(2,1)S(1)}, bf16[4,2,72,1152]{3,2,0,1:T(8,128)(2,1)S(1)}, u32[]{:S(2)}, u32[]{:S(2)}) %collective-permute-start.119) | collective-permute-done | bytes 1327136 | tf_op jit(solution)/shard_map/ppermute | solution.py:24
  566.5 20.5 %collective-permute-done.123 = bf16[4,2,72,1152]{3,2,0,1:T(8,128)(2,1)S(1)} collective-permute-done((bf16[4,2,72,1152]{3,2,0,1:T(8,128)(2,1)S(1)}, bf16[4,2,72,1152]{3,2,0,1:T(8,128)(2,1)S(1)}, u32[]{:S(2)}, u32[]{:S(2)}) %collective-permute-start.123) | collective-permute-done | bytes 1327136 | tf_op jit(solution)/shard_map/ppermute | solution.py:24
  608.7 10.3 %attend_grad.2 = (bf16[2,256,1152]{2,1,0:T(8,128)(2,1)S(1)}, bf16[2,256,576]{2,1,0:T(8,128)(2,1)S(1)}) custom-call(bf16[2,256,1152]{2,1,0:T(8,128)(2,1)S(1)} %bitcast.659, bf16[2,256,576]{2,1,0:T(8,128)(2,1)S(1)} %bitcast.663, bf16[2,256,576]{2,1,0:T(8,128)(2,1)S(1)} %bitcast.718), custom_call_target="tpu_custom_call" | custom-call | tf_op jit(solution)/shard_map/attend_grad/pallas_call | solution.py:254
  660.0 20.9 %collective-permute-done.103 = bf16[4,2,72,1152]{3,2,0,1:T(8,128)(2,1)S(1)} collective-permute-done((bf16[4,2,72,1152]{3,2,0,1:T(8,128)(2,1)S(1)}, bf16[4,2,72,1152]{3,2,0,1:T(8,128)(2,1)S(1)}, u32[]{:S(2)}, u32[]{:S(2)}) %collective-permute-start.103) | collective-permute-done | bytes 1327136 | tf_op jit(solution)/shard_map/ppermute | solution.py:24
  770.5 12.5 %collective-permute-done.111 = bf16[4,2,72,1152]{3,2,0,1:T(8,128)(2,1)S(1)} collective-permute-done((bf16[4,2,72,1152]{3,2,0,1:T(8,128)(2,1)S(1)}, bf16[4,2,72,1152]{3,2,0,1:T(8,128)(2,1)S(1)}, u32[]{:S(2)}, u32[]{:S(2)}) %collective-permute-start.111) | collective-permute-done | bytes 1327136 | tf_op jit(solution)/shard_map/ppermute | solution.py:24
  786.9 24.5 %collective-permute-done.115 = bf16[4,2,72,1152]{3,2,0,1:T(8,128)(2,1)S(1)} collective-permute-done((bf16[4,2,72,1152]{3,2,0,1:T(8,128)(2,1)S(1)}, bf16[4,2,72,1152]{3,2,0,1:T(8,128)(2,1)S(1)}, u32[]{:S(2)}, u32[]{:S(2)}) %collective-permute-start.115) | collective-permute-done | bytes 1327136 | tf_op jit(solution)/shard_map/ppermute | solution.py:24
  822.7 10.7 %attend_grad.3 = (bf16[2,256,1152]{2,1,0:T(8,128)(2,1)S(1)}, bf16[2,256,576]{2,1,0:T(8,128)(2,1)S(1)}) custom-call(bf16[2,256,1152]{2,1,0:T(8,128)(2,1)S(1)} %bitcast.665, bf16[2,256,576]{2,1,0:T(8,128)(2,1)S(1)} %bitcast.661, bf16[2,256,576]{2,1,0:T(8,128)(2,1)S(1)} %bitcast.719), custom_call_target="tpu_custom_call" | custom-call | tf_op jit(solution)/shard_map/attend_grad/pallas_call | solution.py:254
  880.3 9.4 collective-permute-done.116
  905.8 9.6 collective-permute-done.90
  931.7 9.4 collective-permute-done.93
  973.1 15.6 %collective-permute-done.99 = bf16[2,2,72,1152]{3,2,0,1:T(8,128)(2,1)S(1)} collective-permute-done((bf16[2,2,72,1152]{3,2,0,1:T(8,128)(2,1)S(1)}, bf16[2,2,72,1152]{3,2,0,1:T(8,128)(2,1)S(1)}, u32[]{:S(2)}, u32[]{:S(2)}) %collective-permute-start.99) | collective-permute-done | bytes 663584 | tf_op jit(solution)/shard_map/ppermute | solution.py:24
  993.4 11.3 %collective-permute-done.100 = bf16[2,72,1152]{2,1,0:T(8,128)(2,1)S(1)} collective-permute-done((bf16[2,72,1152]{2,1,0:T(8,128)(2,1)S(1)}, bf16[2,72,1152]{2,1,0:T(8,128)(2,1)S(1)}, u32[]{:S(2)}, u32[]{:S(2)}) %collective-permute-start.100) | collective-permute-done | bytes 331808 | tf_op jit(solution)/shard_map/ppermute | solution.py:24
  (986 shorter events, 584.3 us)
Async XLA Ops:
  7.2 158.3 %all-gather.5.cloned.1.call-start = ((), (), s32[]{:S(2)}) async-start(), calls=%async_computation.6 | async-start | bytes 3317760 | tf_op jit(solution)/shard_map/all_gather | solution.py:459
  10.4 268.3 %all-gather.7.cloned.1.call-start = ((), (), s32[]{:S(2)}) async-start(), calls=%async_computation.7 | async-start | bytes 4976640 | tf_op jit(solution)/shard_map/all_gather | solution.py:459
  17.5 52.2 %collective-permute-start.8 = (bf16[2,72,1152]{2,1,0:T(8,128)(2,1)}, bf16[2,72,1152]{2,1,0:T(8,128)(2,1)}, u32[]{:S(2)}, u32[]{:S(2)}) collective-permute-start(bf16[2,72,1152]{2,1,0:T(8,128)(2,1)} %get-tuple-element.207), channel_id=1, source_target_pairs={{0,8},{8,0},{16,24},{24,16},{1,9},{9,1},{17,25},{25,17},{2,10},{10... | collective-permute-start | bytes 995336 | tf_op jit(solution)/shard_map/ppermute | solution.py:24
  19.5 45.2 %collective-permute-start.9 = (bf16[2,72,1152]{2,1,0:T(8,128)(2,1)}, bf16[2,72,1152]{2,1,0:T(8,128)(2,1)}, u32[]{:S(2)}, u32[]{:S(2)}) collective-permute-start(bf16[2,72,1152]{2,1,0:T(8,128)(2,1)} %get-tuple-element.207), channel_id=1, source_target_pairs={{0,16},{8,24},{16,0},{24,8},{1,17},{9,25},{17,1},{25,9},{2,18},{10... | collective-permute-start | bytes 995336 | tf_op jit(solution)/shard_map/ppermute | solution.py:24
  23.5 870.8 %reduce-scatter.4.cloned.1.call-start = ((), (), s32[]{:S(2)}) async-start(), calls=%async_computation.3 | async-start | bytes 1658880 | tf_op jit(solution)/shard_map/reduce_scatter | solution.py:485
  64.7 41.6 %collective-permute-start.19 = (bf16[4,2,360]{2,1,0:T(2,128)(2,1)}, bf16[4,2,360]{2,1,0:T(2,128)(2,1)S(1)}, u32[]{:S(2)}, u32[]{:S(2)}) collective-permute-start(bf16[4,2,360]{2,1,0:T(2,128)(2,1)} %constant_dynamic-update-slice_fusion.4), channel_id=1, source_target_pairs={{0,24},{8,16},{16,8},{24,0},{1,25},{9,17},{17,9},{25,1},{2,26},{10... | collective-permute-start | bytes 17288 | tf_op jit(solution)/shard_map/ppermute | solution.py:24
  93.2 44.7 %collective-permute-start.7 = (bf16[256,1152]{1,0:T(8,128)(2,1)S(1)}, bf16[256,1152]{1,0:T(8,128)(2,1)}, u32[]{:S(2)}, u32[]{:S(2)}) collective-permute-start(bf16[256,1152]{1,0:T(8,128)(2,1)S(1)} %fusion.78), channel_id=1, source_target_pairs={{0,1},{1,0},{2,3},{3,2},{4,5},{5,4},{6,7},{7,6},{8,9},{9,8},{10,11... | collective-permute-start | bytes 1769480 | tf_op jit(solution)/shard_map/ppermute | solution.py:24
  173.1 42.2 %collective-permute-start.28 = (bf16[4,72,1152]{2,1,0:T(8,128)(2,1)S(1)}, bf16[4,72,1152]{2,1,0:T(8,128)(2,1)}, u32[]{:S(2)}, u32[]{:S(2)}) collective-permute-start(bf16[4,72,1152]{2,1,0:T(8,128)(2,1)S(1)} %bitcast.697), channel_id=1, source_target_pairs={{0,2},{2,0},{4,6},{6,4},{1,3},{3,1},{5,7},{7,5},{8,10},{10,8},{12,... | collective-permute-start | bytes 1990664 | tf_op jit(solution)/shard_map/ppermute | solution.py:24
  186.9 42.6 %collective-permute-start.33 = (bf16[4,72,1152]{2,1,0:T(8,128)(2,1)}, bf16[4,72,1152]{2,1,0:T(8,128)(2,1)S(1)}, u32[]{:S(2)}, u32[]{:S(2)}) collective-permute-start(bf16[4,72,1152]{2,1,0:T(8,128)(2,1)} %collective-permute-done.32.refs_2_), channel_id=1, source_target_pairs={{0,2},{2,0},{4,6},{6,4},{1,3},{3,1},{5,7},{7,5},{8,10},{10,8},{12,... | collective-permute-start | bytes 1990664 | tf_op jit(solution)/shard_map/ppermute | solution.py:24
  215.3 44.8 %collective-permute-start.34 = (bf16[4,72,1152]{2,1,0:T(8,128)(2,1)S(1)}, bf16[4,72,1152]{2,1,0:T(8,128)(2,1)}, u32[]{:S(2)}, u32[]{:S(2)}) collective-permute-start(bf16[4,72,1152]{2,1,0:T(8,128)(2,1)S(1)} %bitcast.695), channel_id=1, source_target_pairs={{0,2},{2,0},{4,6},{6,4},{1,3},{3,1},{5,7},{7,5},{8,10},{10,8},{12,... | collective-permute-start | bytes 1990664 | tf_op jit(solution)/shard_map/ppermute | solution.py:24
  217.0 39.9 %collective-permute-start.30 = (bf16[4,72,1152]{2,1,0:T(8,128)(2,1)}, bf16[4,72,1152]{2,1,0:T(8,128)(2,1)}, u32[]{:S(2)}, u32[]{:S(2)}) collective-permute-start(bf16[4,72,1152]{2,1,0:T(8,128)(2,1)} %collective-permute-done.28.refs_1_), channel_id=1, source_target_pairs={{0,4},{2,6},{4,0},{6,2},{1,5},{3,7},{5,1},{7,3},{8,12},{10,14},{12... | collective-permute-start | bytes 1990664 | tf_op jit(solution)/shard_map/ppermute | solution.py:24
  403.4 42.0 %collective-permute-start.64 = (bf16[4,72,1152]{2,1,0:T(8,128)(2,1)}, bf16[4,72,1152]{2,1,0:T(8,128)(2,1)S(1)}, u32[]{:S(2)}, u32[]{:S(2)}) collective-permute-start(bf16[4,72,1152]{2,1,0:T(8,128)(2,1)} %collective-permute-done.63.refs_2_), channel_id=1, source_target_pairs={{0,2},{2,0},{4,6},{6,4},{1,3},{3,1},{5,7},{7,5},{8,10},{10,8},{12,... | collective-permute-start | bytes 1990664 | tf_op jit(solution)/shard_map/ppermute | solution.py:24
  419.2 40.0 %collective-permute-start.60 = (bf16[4,72,1152]{2,1,0:T(8,128)(2,1)}, bf16[4,72,1152]{2,1,0:T(8,128)(2,1)}, u32[]{:S(2)}, u32[]{:S(2)}) collective-permute-start(bf16[4,72,1152]{2,1,0:T(8,128)(2,1)} %bitcast.100.refs_0_), channel_id=1, source_target_pairs={{0,4},{2,6},{4,0},{6,2},{1,5},{3,7},{5,1},{7,3},{8,12},{10,14},{12... | collective-permute-start | bytes 1990664 | tf_op jit(solution)/shard_map/ppermute | solution.py:24
  431.2 45.5 %collective-permute-start.65 = (bf16[4,72,1152]{2,1,0:T(8,128)(2,1)S(1)}, bf16[4,72,1152]{2,1,0:T(8,128)(2,1)}, u32[]{:S(2)}, u32[]{:S(2)}) collective-permute-start(bf16[4,72,1152]{2,1,0:T(8,128)(2,1)S(1)} %bitcast.689), channel_id=1, source_target_pairs={{0,2},{2,0},{4,6},{6,4},{1,3},{3,1},{5,7},{7,5},{8,10},{10,8},{12,... | collective-permute-start | bytes 1990664 | tf_op jit(solution)/shard_map/ppermute | solution.py:24
  431.6 40.5 %collective-permute-start.61 = (bf16[4,72,1152]{2,1,0:T(8,128)(2,1)}, bf16[4,72,1152]{2,1,0:T(8,128)(2,1)}, u32[]{:S(2)}, u32[]{:S(2)}) collective-permute-start(bf16[4,72,1152]{2,1,0:T(8,128)(2,1)} %collective-permute-done.59.refs_1_), channel_id=1, source_target_pairs={{0,4},{2,6},{4,0},{6,2},{1,5},{3,7},{5,1},{7,3},{8,12},{10,14},{12... | collective-permute-start | bytes 1990664 | tf_op jit(solution)/shard_map/ppermute | solution.py:24
  500.6 40.9 %collective-permute-start.121 = (bf16[4,2,72,1152]{3,2,0,1:T(8,128)(2,1)}, bf16[4,2,72,1152]{3,2,0,1:T(8,128)(2,1)}, u32[]{:S(2)}, u32[]{:S(2)}) collective-permute-start(bf16[4,2,72,1152]{3,2,0,1:T(8,128)(2,1)} %bitcast.634), channel_id=1, source_target_pairs={{0,2},{2,0},{4,6},{6,4},{1,3},{3,1},{5,7},{7,5},{8,10},{10,8},{12,... | collective-permute-start | bytes 3981320 | tf_op jit(solution)/shard_map/ppermute | solution.py:24
  522.0 186.4 %collective-permute-start.68 = (f32[256,1152]{1,0:T(8,128)}, f32[256,1152]{1,0:T(8,128)}, u32[]{:S(2)}, u32[]{:S(2)}) collective-permute-start(f32[256,1152]{1,0:T(8,128)} %slice.663), channel_id=1, source_target_pairs={{0,1},{1,0},{2,3},{3,2},{4,5},{5,4},{6,7},{7,6},{8,9},{9,8},{10,11... | collective-permute-start | bytes 3538952 | tf_op jit(solution)/shard_map/ppermute | solution.py:24
  536.8 50.3 %collective-permute-start.123 = (bf16[4,2,72,1152]{3,2,0,1:T(8,128)(2,1)S(1)}, bf16[4,2,72,1152]{3,2,0,1:T(8,128)(2,1)S(1)}, u32[]{:S(2)}, u32[]{:S(2)}) collective-permute-start(bf16[4,2,72,1152]{3,2,0,1:T(8,128)(2,1)S(1)} %bitcast.750), channel_id=1, source_target_pairs={{0,4},{2,6},{4,0},{6,2},{1,5},{3,7},{5,1},{7,3},{8,12},{10,14},{12... | collective-permute-start | bytes 3981320 | tf_op jit(solution)/shard_map/ppermute | solution.py:24
  541.5 48.7 %collective-permute-start.72 = (bf16[256,1152]{1,0:T(8,128)(2,1)S(1)}, bf16[256,1152]{1,0:T(8,128)(2,1)S(1)}, u32[]{:S(2)}, u32[]{:S(2)}) collective-permute-start(bf16[256,1152]{1,0:T(8,128)(2,1)S(1)} %multiply_convert_fusion.6), channel_id=1, source_target_pairs={{0,1},{1,0},{2,3},{3,2},{4,5},{5,4},{6,7},{7,6},{8,9},{9,8},{10,11... | collective-permute-start | bytes 1769480 | tf_op jit(solution)/shard_map/ppermute | solution.py:24
  558.6 64.2 %collective-permute-start.122 = (bf16[4,72,1152]{2,1,0:T(8,128)(2,1)}, bf16[4,72,1152]{2,1,0:T(8,128)(2,1)}, u32[]{:S(2)}, u32[]{:S(2)}) collective-permute-start(bf16[4,72,1152]{2,1,0:T(8,128)(2,1)} %dynamic-slice_bitcast_fusion.3), channel_id=1, source_target_pairs={{0,4},{2,6},{4,0},{6,2},{1,5},{3,7},{5,1},{7,3},{8,12},{10,14},{12... | collective-permute-start | bytes 1990664 | tf_op jit(solution)/shard_map/ppermute | solution.py:24
  651.7 62.4 %collective-permute-start.124 = (bf16[4,72,1152]{2,1,0:T(8,128)(2,1)}, bf16[4,72,1152]{2,1,0:T(8,128)(2,1)}, u32[]{:S(2)}, u32[]{:S(2)}) collective-permute-start(bf16[4,72,1152]{2,1,0:T(8,128)(2,1)} %dynamic-slice_bitcast_fusion.2), channel_id=1, source_target_pairs={{0,2},{2,0},{4,6},{6,4},{1,3},{3,1},{5,7},{7,5},{8,10},{10,8},{12,... | collective-permute-start | bytes 1990664 | tf_op jit(solution)/shard_map/ppermute | solution.py:24
  705.9 250.1 %reduce-scatter.8.cloned.1.call-start = ((), (), s32[]{:S(2)}) async-start(), calls=%async_computation.5 | async-start | bytes 3317760 | tf_op jit(solution)/shard_map/reduce_scatter | solution.py:485
  718.5 289.3 %reduce-scatter.6.cloned.1.call-start = ((), (), s32[]{:S(2)}) async-start(), calls=%async_computation.4 | async-start | bytes 3317760 | tf_op jit(solution)/shard_map/reduce_scatter | solution.py:485
  719.6 40.2 %collective-permute-start.69 = (bf16[256,1152]{1,0:T(8,128)(2,1)S(1)}, bf16[256,1152]{1,0:T(8,128)(2,1)}, u32[]{:S(2)}, u32[]{:S(2)}) collective-permute-start(bf16[256,1152]{1,0:T(8,128)(2,1)S(1)} %copy-done.99), channel_id=1, source_target_pairs={{0,1},{1,0},{2,3},{3,2},{4,5},{5,4},{6,7},{7,6},{8,9},{9,8},{10,11... | collective-permute-start | bytes 1769480 | tf_op jit(solution)/shard_map/ppermute | solution.py:24
  758.9 52.4 %collective-permute-start.115 = (bf16[4,2,72,1152]{3,2,0,1:T(8,128)(2,1)S(1)}, bf16[4,2,72,1152]{3,2,0,1:T(8,128)(2,1)S(1)}, u32[]{:S(2)}, u32[]{:S(2)}) collective-permute-start(bf16[4,2,72,1152]{3,2,0,1:T(8,128)(2,1)S(1)} %bitcast.749), channel_id=1, source_target_pairs={{0,4},{2,6},{4,0},{6,2},{1,5},{3,7},{5,1},{7,3},{8,12},{10,14},{12... | collective-permute-start | bytes 3981320 | tf_op jit(solution)/shard_map/ppermute | solution.py:24
  759.8 51.9 %collective-permute-start.117 = (bf16[4,2,72,1152]{3,2,0,1:T(8,128)(2,1)S(1)}, bf16[4,2,72,1152]{3,2,0,1:T(8,128)(2,1)S(1)}, u32[]{:S(2)}, u32[]{:S(2)}) collective-permute-start(bf16[4,2,72,1152]{3,2,0,1:T(8,128)(2,1)S(1)} %bitcast.747), channel_id=1, source_target_pairs={{0,2},{2,0},{4,6},{6,4},{1,3},{3,1},{5,7},{7,5},{8,10},{10,8},{12,... | collective-permute-start | bytes 3981320 | tf_op jit(solution)/shard_map/ppermute | solution.py:24
  770.4 44.2 %collective-permute-start.85 = (bf16[256,1152]{1,0:T(8,128)(2,1)S(1)}, bf16[256,1152]{1,0:T(8,128)(2,1)S(1)}, u32[]{:S(2)}, u32[]{:S(2)}) collective-permute-start(bf16[256,1152]{1,0:T(8,128)(2,1)S(1)} %multiply_convert_fusion.4), channel_id=1, source_target_pairs={{0,1},{1,0},{2,3},{3,2},{4,5},{5,4},{6,7},{7,6},{8,9},{9,8},{10,11... | collective-permute-start | bytes 1769480 | tf_op jit(solution)/shard_map/ppermute | solution.py:24
  784.2 90.9 %collective-permute-start.112 = (bf16[4,72,1152]{2,1,0:T(8,128)(2,1)}, bf16[4,72,1152]{2,1,0:T(8,128)(2,1)}, u32[]{:S(2)}, u32[]{:S(2)}) collective-permute-start(bf16[4,72,1152]{2,1,0:T(8,128)(2,1)} %dynamic-slice_bitcast_fusion.8), channel_id=1, source_target_pairs={{0,2},{2,0},{4,6},{6,4},{1,3},{3,1},{5,7},{7,5},{8,10},{10,8},{12,... | collective-permute-start | bytes 1990664 | tf_op jit(solution)/shard_map/ppermute | solution.py:24
  785.5 92.4 %collective-permute-start.114 = (bf16[4,72,1152]{2,1,0:T(8,128)(2,1)}, bf16[4,72,1152]{2,1,0:T(8,128)(2,1)}, u32[]{:S(2)}, u32[]{:S(2)}) collective-permute-start(bf16[4,72,1152]{2,1,0:T(8,128)(2,1)} %dynamic-slice_bitcast_fusion.7), channel_id=1, source_target_pairs={{0,4},{2,6},{4,0},{6,2},{1,5},{3,7},{5,1},{7,3},{8,12},{10,14},{12... | collective-permute-start | bytes 1990664 | tf_op jit(solution)/shard_map/ppermute | solution.py:24
  875.1 72.6 %collective-permute-start.97 = (bf16[4,2,72,1152]{3,2,1,0:T(8,128)(2,1)}, bf16[4,2,72,1152]{3,2,1,0:T(8,128)(2,1)}, u32[]{:S(2)}, u32[]{:S(2)}) collective-permute-start(bf16[4,2,72,1152]{3,2,1,0:T(8,128)(2,1)} %dynamic-slice_bitcast_fusion), channel_id=1, source_target_pairs={{0,2},{2,0},{4,6},{6,4},{1,3},{3,1},{5,7},{7,5},{8,10},{10,8},{12,... | collective-permute-start | bytes 3981320 | tf_op jit(solution)/shard_map/ppermute | solution.py:24
  877.9 73.1 %collective-permute-start.95 = (bf16[4,2,72,1152]{3,2,0,1:T(8,128)(2,1)}, bf16[4,2,72,1152]{3,2,0,1:T(8,128)(2,1)}, u32[]{:S(2)}, u32[]{:S(2)}) collective-permute-start(bf16[4,2,72,1152]{3,2,0,1:T(8,128)(2,1)} %bitcast.745), channel_id=1, source_target_pairs={{0,4},{2,6},{4,0},{6,2},{1,5},{3,7},{5,1},{7,3},{8,12},{10,14},{12... | collective-permute-start | bytes 3981320 | tf_op jit(solution)/shard_map/ppermute | solution.py:24
  919.0 71.1 %collective-permute-start.87 = (f32[256,1152]{1,0:T(8,128)}, f32[256,1152]{1,0:T(8,128)}, u32[]{:S(2)}, u32[]{:S(2)}) collective-permute-start(f32[256,1152]{1,0:T(8,128)} %add_add_fusion.4), channel_id=1, source_target_pairs={{0,1},{1,0},{2,3},{3,2},{4,5},{5,4},{6,7},{7,6},{8,9},{9,8},{10,11... | collective-permute-start | bytes 3538952 | tf_op jit(solution)/shard_map/ppermute | solution.py:24
  (294 other events, 3836.7 us)
Sparse Core Ops, SparseCore 0:
  10.5 76.5 all-gather.4
  89.3 78.6 all-gather.6
  706.0 30.3 reduce-scatter.3
  738.5 51.4 reduce-scatter.7
  894.4 54.6 reduce-scatter.5

commit v2 on v1

v2 whole, which is shorter than its diff:
```python
from functools import partial

import jax
import jax.numpy as jnp
from jax import lax
from jax.experimental import pallas as pl
from jax.experimental.pallas import tpu as pltpu
from jax.sharding import PartitionSpec as P

HEAD_DIM = 72
LANES = 128
EPSILON = 1e-06
MIB = 1024 * 1024
f32 = jnp.float32
bf16 = jnp.bfloat16
LIGHT = pl.CostEstimate(flops=1, bytes_accessed=1, transcendentals=0)
GELU_C = 0.7978845608028654


class Flow:
    RATE = 0.0435
    SEND = 1.5

    def __init__(self):
        self.now = 0.0
        self.busy = {}
        self.queues = {}
        self.fresh = []
        self.before = None
        self.latest = []
        self.last = {}
        self.depth = 1
        self.held = False

    def post(self, value, axis, bit, then, rank, weight=1.0):
        line = (axis, bit) if axis == "seq" else (axis, 0)
        size = value.size * value.dtype.itemsize * weight / (self.RATE * 1e6)
        queue = self.queues.setdefault(line, [])
        queue.append((value, axis, bit, size, then, rank))
        queue.sort(key=lambda entry: entry[-1])
        self.begin()

    def begin(self):
        for line, queue in self.queues.items():
            busy = self.busy.setdefault(line, [])
            depth = self.depth if line[0] == "seq" else 1
            while queue and len(busy) < depth and not (self.held and line[0] == "seq"):
                value, axis, bit, duration, then, _ = queue.pop(0)
                ahead = self.last.get(line, []) + (self.latest if axis == "seq" else [])
                if ahead:
                    value = lax.optimization_barrier((value, ahead))[0]
                self.now += self.SEND
                start = max([self.now] + [entry[0] for entry in busy])
                busy.append((start + duration, pxor(value, axis, 1 << bit), then))

    def pump(self):
        while True:
            lines = [line for line, busy in self.busy.items() if busy]
            line = min(lines, key=lambda entry: self.busy[entry][0][0], default=None)
            if line is None or self.busy[line][0][0] > self.now:
                break
            _, got, then = self.busy[line].pop(0)
            self.last[line] = [got]
            self.fresh.append(got)
            then(got)
            self.begin()

    def hold(self, cost):
        self.pump()
        self.held = True
        left = [entry[0] for line, busy in self.busy.items() if line[0] == "seq" for entry in busy]
        self.now = max([self.now] + left) + cost

    def release(self, got):
        self.held = False
        self.latest = [got]
        self.begin()
        self.latest = []

    def until(self, ready):
        self.pump()
        while not ready():
            self.now = max(self.now, min(busy[0][0] for busy in self.busy.values() if busy))
            self.pump()

    def step(self, cost, value):
        self.pump()
        if self.before is not None:
            self.fresh.append(self.before)
            self.before = None
        if self.fresh:
            value = lax.optimization_barrier((value, self.fresh))[0]
            self.fresh = []
        self.now += cost
        return value

    def note(self, *arrays):
        self.fresh.extend(arrays)

    def ran(self, outputs):
        self.before = outputs[0]
        return outputs


def bits_of(size):
    return max(size.bit_length() - 1, 0)


def pxor(value, axis, flip):
    size = lax.axis_size(axis)
    return lax.ppermute(value, axis, [(i, i ^ flip) for i in range(size)])


def swap(value):
    return pxor(value, "tensor", 1)


def take(value, axis, index):
    return lax.dynamic_index_in_dim(value, index, axis, keepdims=False)


def place_kernel(cuts, idx_ref, *refs):
    inner = len(refs) - len(cuts)
    blocks, outs = refs[:inner], refs[inner:]
    for rel, block in enumerate(blocks):
        at = jnp.bitwise_xor(idx_ref[1], rel)
        for (top, rows, left, cols, before, after), out_ref in zip(cuts, outs):
            part = block[0, top : top + rows, left : left + cols]
            sides = [part]
            if before:
                sides.insert(0, jnp.zeros((rows, before), part.dtype))
            if after:
                sides.append(jnp.zeros((rows, after), part.dtype))
            out_ref[0, at] = jnp.concatenate(sides, axis=1) if len(sides) > 1 else part


def place(blocks, outer_index, inner_index, cuts=None):
    outer, rows, cols = blocks[0].shape
    inner = len(blocks)
    cuts = cuts or ((0, rows, 0, cols, 0, 0),)
    start = jnp.int32(0) if outer_index is None else outer_index
    index = jnp.stack([start, inner_index]).astype(jnp.int32)
    sizes = [(cut[1], cut[3] + cut[4] + cut[5]) for cut in cuts]
    return pl.pallas_call(
        partial(place_kernel, cuts),
        grid_spec=pltpu.PrefetchScalarGridSpec(
            num_scalar_prefetch=1,
            grid=(outer,),
            in_specs=[pl.BlockSpec((1, rows, cols), lambda o, idx: (o, 0, 0))] * inner,
            out_specs=[
                pl.BlockSpec((1, inner) + size, lambda o, idx: (jnp.bitwise_xor(idx[0], o), 0, 0, 0))
                for size in sizes
            ],
        ),
        out_shape=[jax.ShapeDtypeStruct((outer, inner) + size, blocks[0].dtype) for size in sizes],
        compiler_params=pltpu.CompilerParams(vmem_limit_bytes=12 * MIB),
        cost_estimate=LIGHT,
        name="place",
    )(index, *blocks)


class Gather:
    def __init__(self, flow, rank, halves, dp_index, seq_index, cuts, cost):
        self.rank = rank
        self.flow, self.index, self.cuts, self.cost = flow, (dp_index, seq_index), cuts, cost
        self.count, self.outer = bits_of(lax.axis_size("seq")), bits_of(lax.axis_size("dp"))
        self.blocks = {}
        self.trees = [{}, {}]
        self.along_dp(0, self.outer, halves)

    def along_dp(self, rel, below, block):
        self.blocks[rel] = block
        for bit in reversed(range(below)):
            self.flow.post(
                block, "dp", bit, partial(self.along_dp, rel | 1 << bit, bit), self.rank, 1.0 + bit
            )
        if len(self.blocks) == 1 << self.outer:
            ordered = [self.blocks[r] for r in range(1 << self.outer)]
            self.flow.now += 2.0
            for which in range(2):
                stacked = jnp.stack([block[which] for block in ordered])
                self.along_seq(which, 0, 0, stacked)

    def along_seq(self, which, rel, first, block):
        self.trees[which][rel] = block
        for step in range(first, self.count):
            bit = step if which == 0 else self.count - 1 - step
            self.flow.post(block, "seq", bit, partial(self.along_seq, which, rel | 1 << bit, step + 1), self.rank)

    def ready(self):
        return all(len(tree) == 1 << self.count for tree in self.trees)

    def result(self):
        self.flow.until(self.ready)
        results = []
        for which in range(2):
            ordered = [self.trees[which][rel] for rel in range(1 << self.count)]
            ordered[0] = self.flow.step(self.cost, ordered[0])
            placed = self.flow.ran(place(ordered, *self.index, self.cuts[which]))
            results.append([p.reshape(-1, p.shape[-1]) for p in placed])
        return results


def add_up(parts):
    return sum(part.astype(f32) for part in parts[1:]) + parts[0].astype(f32)


class Scatter:
    def __init__(self, flow, rank):
        self.flow, self.rank = flow, rank
        self.count, self.outer = bits_of(lax.axis_size("seq")), bits_of(lax.axis_size("dp"))
        self.halves = [None, None]
        self.total = None

    def give(self, which, kept, sent):
        order = list(range(self.count))
        if which == 0:
            order.reverse()
        left = [bit for bit in reversed(range(self.count)) if bit != order[0]]
        shape = kept.shape[:1] + (2,) * (self.count - 1) + kept.shape[2:]
        self.flow.post(
            sent,
            "seq",
            order[0],
            lambda got: self.along_seq(which, order[1:], left, [kept.reshape(shape), got.reshape(shape)]),
            self.rank,
        )

    def split(self, parts, axis, bit, dim):
        mine = (lax.axis_index(axis) >> bit) & 1
        away = add_up([take(part, dim, 1 - mine) for part in parts]).astype(bf16)
        self.flow.note(away)
        kept = add_up([take(part, dim, mine) for part in parts]).astype(bf16)
        return kept, away

    def along_seq(self, which, order, left, parts):
        if not order:
            self.halves[which] = parts
            if all(half is not None for half in self.halves):
                both = [jnp.stack(pair) for pair in zip(*self.halves)]
                both = [v.reshape((2,) + (2,) * self.outer + v.shape[2:]) for v in both]
                self.along_dp(0, both)
            return
        self.flow.now += 2.0
        bit = order[0]
        kept, away = self.split(parts, "seq", bit, 1 + left.index(bit))
        rest = [b for b in left if b != bit]
        self.flow.post(away, "seq", bit, lambda got: self.along_seq(which, order[1:], rest, [kept, got]), self.rank)

    def along_dp(self, bit, parts):
        if bit == self.outer:
            self.total = add_up(parts)
            return
        self.flow.now += 2.0
        kept, away = self.split(parts, "dp", bit, self.outer - bit)
        self.flow.post(away, "dp", bit, lambda got: self.along_dp(bit + 1, [kept, got]), self.rank, 1.0 + bit)


def scatter_small(value, axis):
    count = bits_of(lax.axis_size(axis))
    value = value.reshape((2,) * count + value.shape[1:])
    for bit in reversed(range(count)):
        mine = (lax.axis_index(axis) >> bit) & 1
        value = take(value, 0, mine) + pxor(take(value, 0, 1 - mine), axis, 1 << bit)
    return value


def sum_small(value, axis):
    for bit in range(bits_of(lax.axis_size(axis))):
        value = value + pxor(value, axis, 1 << bit)
    return value


def gather_small(value, axis):
    for bit in range(bits_of(lax.axis_size(axis))):
        value = jnp.concatenate([value, pxor(value, axis, 1 << bit)], axis=0)
    return value


def dispatch(arrays):
    size, index = lax.axis_size("seq"), lax.axis_index("seq")
    parts = []
    for rel in range(size):
        views = [a.reshape(a.shape[0], size, a.shape[1] // size, a.shape[2]) for a in arrays]
        taken = [take(view, 1, index ^ rel) for view in views]
        part = jnp.concatenate(taken, axis=-1) if len(taken) > 1 else taken[0]
        parts.append(part if rel == 0 else pxor(part, "seq", rel))
    stacked = jnp.stack(parts, axis=1)
    return stacked.reshape(stacked.shape[0], -1, stacked.shape[-1])


def collect(rows, cuts):
    size, index = lax.axis_size("seq"), lax.axis_index("seq")
    parts = rows.reshape(rows.shape[0], size, rows.shape[1] // size, rows.shape[2])
    blocks = []
    for rel in range(size):
        block = parts[:, rel]
        blocks.append(block if rel == 0 else pxor(block, "seq", rel))
    return [p.reshape(-1, p.shape[-1]) for p in place(blocks, None, index, cuts)]


def head_windows(width):
    spans = []
    for first in range(0, width, HEAD_DIM):
        low = first // LANES * LANES
        high = min(-(-(first + HEAD_DIM) // LANES) * LANES, width)
        spans.append((first, low, high))
    return spans


def head_mask(first, low, high):
    lane = lax.broadcasted_iota(jnp.int32, (1, high - low), 1) + low
    return jnp.where((lane >= first) & (lane < first + HEAD_DIM), 1.0, 0.0).astype(bf16)


def row_dot(left, right):
    return lax.dot_general(left, right, (((1,), (1,)), ((), ())), preferred_element_type=f32)


def col_dot(left, right):
    return lax.dot_general(left, right, (((0,), (0,)), ((), ())), preferred_element_type=f32)


def softmax_probs(queries, key_rows, apart):
    scores = row_dot(queries, key_rows) * (HEAD_DIM ** (-0.5))
    if apart is not None:
        scores = jnp.where(apart, -1e30, scores)
    top = jnp.max(scores, axis=-1, keepdims=True)
    weights = jnp.exp(scores - top)
    return weights * (1.0 / jnp.sum(weights, axis=-1, keepdims=True))


def tokens_apart(rows, period):
    if period is None:
        return None
    one = lax.broadcasted_iota(jnp.int32, (rows, rows), 0)
    two = lax.broadcasted_iota(jnp.int32, (rows, rows), 1)
    return lax.rem(one, period) != lax.rem(two, period)


def attend_kernel(period, lead, qk_ref, v_ref, out_ref, acc_ref):
    rows, width = acc_ref.shape
    apart = tokens_apart(rows, period)
    queries, key_rows = qk_ref[0, :, :width], qk_ref[0, :, width : 2 * width]
    value_rows = v_ref[0, :, lead : lead + width]
    acc_ref[...] = jnp.zeros_like(acc_ref)
    for first, low, high in head_windows(width):
        mask = head_mask(first, low, high)
        probs = softmax_probs(queries[:, low:high] * mask, key_rows[:, low:high], apart)
        acc_ref[:, low:high] += jnp.dot(
            probs.astype(bf16), value_rows[:, low:high] * mask, preferred_element_type=f32
        )
    attended = acc_ref[...].astype(bf16)
    before = out_ref.shape[2] - width
    if before:
        attended = jnp.concatenate([jnp.zeros((rows, before), bf16), attended], axis=1)
    out_ref[0] = attended


def attend(qk, values, lead, width, before, period):
    blocks, rows = qk.shape[:2]

    def whole(cols):
        return pl.BlockSpec((1, rows, cols), lambda b: (b, 0, 0))

    return pl.pallas_call(
        partial(attend_kernel, period, lead),
        grid=(blocks,),
        out_shape=jax.ShapeDtypeStruct((blocks, rows, before + width), bf16),
        in_specs=[whole(qk.shape[2]), whole(values.shape[2])],
        out_specs=whole(before + width),
        scratch_shapes=[pltpu.VMEM((rows, width), f32)],
        compiler_params=pltpu.CompilerParams(vmem_limit_bytes=24 * MIB),
        cost_estimate=LIGHT,
        name="attend",
    )(qk, values)


def attend_grad_kernel(period, lead, skip, qk_ref, v_ref, da_ref, *refs):
    outs, sum_ref, (acc_q, acc_k, acc_v) = refs[:-4], refs[-4], refs[-3:]
    rows, width = acc_q.shape
    apart = tokens_apart(rows, period)
    queries, key_rows = qk_ref[0, :, :width], qk_ref[0, :, width : 2 * width]
    value_rows = v_ref[0, :, lead : lead + width]
    grad_att = da_ref[0, :, skip : skip + width]
    factor = HEAD_DIM ** (-0.5)
    for acc in (acc_q, acc_k, acc_v):
        acc[...] = jnp.zeros_like(acc)
    for first, low, high in head_windows(width):
        mask = head_mask(first, low, high)
        q_own = queries[:, low:high] * mask
        k_own = key_rows[:, low:high] * mask
        g_own = grad_att[:, low:high] * mask
        probs = softmax_probs(q_own, k_own, apart)
        grad_probs = row_dot(g_own, value_rows[:, low:high])
        inner = jnp.sum(grad_probs * probs, axis=-1, keepdims=True)
        grad_scores = (probs * (grad_probs - inner)).astype(bf16)
        acc_q[:, low:high] += jnp.dot(grad_scores, k_own, preferred_element_type=f32)
        acc_k[:, low:high] += col_dot(grad_scores, q_own)
        acc_v[:, low:high] += col_dot(probs.astype(bf16), g_own)
    grad_q = (acc_q[...] * factor).astype(bf16)
    outs[0][0, :, :width] = grad_q
    outs[0][0, :, width : 2 * width] = (acc_k[...] * factor).astype(bf16)
    grad_v = acc_v[...].astype(bf16)
    if len(outs) == 1:
        outs[0][0, :, 2 * width :] = grad_v
    else:
        outs[1][0] = jnp.concatenate([grad_v, jnp.zeros_like(grad_v)], axis=1)
    sum_ref[0, 0:1, :] = jnp.sum(grad_q.astype(f32), axis=0, keepdims=True)
    sum_ref[0, 1:2, :] = jnp.sum(grad_v.astype(f32), axis=0, keepdims=True)


def attend_grad(qk, values, lead, grad_att, skip, width, period):
    blocks, rows = qk.shape[:2]

    def whole(cols):
        return pl.BlockSpec((1, rows, cols), lambda b: (b, 0, 0))

    cols = [3 * width] if period else [2 * width, 2 * width]
    return pl.pallas_call(
        partial(attend_grad_kernel, period, lead, skip),
        grid=(blocks,),
        out_shape=[jax.ShapeDtypeStruct((blocks, rows, c), bf16) for c in cols]
        + [jax.ShapeDtypeStruct((blocks, 2, width), f32)],
        in_specs=[whole(qk.shape[2]), whole(values.shape[2]), whole(grad_att.shape[2])],
        out_specs=[whole(c) for c in cols] + [pl.BlockSpec((1, 2, width), lambda b: (b, 0, 0))],
        scratch_shapes=[pltpu.VMEM((rows, width), f32)] * 3,
        compiler_params=pltpu.CompilerParams(vmem_limit_bytes=24 * MIB),
        cost_estimate=LIGHT,
        name="attend_grad",
    )(qk, values, grad_att)


def on_chip():
    return pl.BlockSpec(memory_space=pltpu.VMEM)


def in_place():
    return pl.BlockSpec(memory_space=pl.ANY)


def call(kernel, name, inputs, streamed, outs, scratch=(), limit=24, out_specs=None):
    buffers = [pltpu.VMEM(w.shape, w.dtype) for w in streamed]
    sems = [pltpu.SemaphoreType.DMA((len(streamed),))] if streamed else []
    n_in, n_w, n_out = len(inputs), len(streamed), len(outs)

    def body(*refs):
        ins, away = refs[:n_in], refs[n_in : n_in + n_w]
        results = refs[n_in + n_w : n_in + n_w + n_out]
        rest = refs[n_in + n_w + n_out :]
        here, rest = rest[:n_w], rest[n_w:]
        copies = []
        if n_w:
            sem, rest = rest[0], rest[1:]
            copies = [pltpu.make_async_copy(a, h, sem.at[i]) for i, (a, h) in enumerate(zip(away, here))]
            for copy in copies:
                copy.start()

        def fetch(i):
            copies[i].wait()
            return here[i]

        kernel(ins, fetch, results, rest)

    return pl.pallas_call(
        body,
        out_shape=[jax.ShapeDtypeStruct(shape, dtype) for shape, dtype in outs],
        in_specs=[on_chip()] * n_in + [in_place()] * n_w,
        out_specs=out_specs or [on_chip()] * n_out,
        scratch_shapes=buffers + sems + list(scratch),
        compiler_params=pltpu.CompilerParams(vmem_limit_bytes=limit * MIB),
        cost_estimate=LIGHT,
        name=name,
    )(*inputs, *streamed)


def norm_parts(values):
    average = jnp.mean(values, axis=-1, keepdims=True)
    centered = values - average
    variance = jnp.mean(centered * centered, axis=-1, keepdims=True)
    inverse = lax.rsqrt(variance + EPSILON)
    return centered * inverse, inverse


def both(one, two):
    return jnp.concatenate([one[...], two[...]], axis=0)


def modulated(values, mods_ref, shift, scale):
    normed, _ = norm_parts(values)
    return (normed * (1.0 + mods_ref[scale : scale + 1, :]) + mods_ref[shift : shift + 1, :]).astype(bf16)


def norm_forward(x, mods, shift, scale):
    def kernel(ins, fetch, outs, scratch):
        outs[0][...] = modulated(ins[0][...], ins[1], shift, scale)

    return call(kernel, "norm_forward", [x, mods], [], [(x.shape, bf16)])[0]


def project_heads(normed, w_qk, w_vo, biases, row):
    rows, cols = 2 * normed[0].shape[0], w_qk.shape[1]

    def kernel(ins, fetch, outs, scratch):
        tokens = both(ins[0], ins[1])
        for i in range(2):
            bias = ins[2][row + i : row + i + 1, :]
            outs[i][...] = (jnp.dot(tokens, fetch(i)[...], preferred_element_type=f32) + bias).astype(bf16)

    return call(kernel, "project_heads", [*normed, biases], [w_qk, w_vo], [((rows, cols), bf16)] * 2)


def project_back(pairs, dtype, name):
    rows, cols = pairs[0][0].shape[0] // 2, pairs[0][1].shape[0]
    count = len(pairs)

    def kernel(ins, fetch, outs, scratch):
        out = row_dot(ins[0][...], fetch(0)[...])
        for i in range(1, count):
            out = out + row_dot(ins[i][...], fetch(i)[...])
        outs[0][...] = out[:rows]
        outs[1][...] = out[rows:].astype(dtype)

    return call(
        kernel, name, [p[0] for p in pairs], [p[1] for p in pairs], [((rows, cols), f32), ((rows, cols), dtype)]
    )


def residual(x, own, other, biases, bias_row, mods, gate, following):
    def kernel(ins, fetch, outs, scratch):
        branch = ins[1][...] + ins[2][...].astype(f32) + ins[3][bias_row : bias_row + 1, :]
        value = ins[0][...] + ins[4][gate : gate + 1, :] * branch
        outs[0][...] = branch
        outs[1][...] = value
        if following is None:
            outs[2][...] = value.astype(bf16)
        else:
            outs[2][...] = modulated(value, ins[4], *following)

    return call(
        kernel, "residual", [x, own, other, biases, mods], [], [(x.shape, f32), (x.shape, f32), (x.shape, bf16)]
    )


def gelu_parts(pre):
    inner = jnp.tanh(GELU_C * (pre + 0.044715 * (pre * pre * pre)))
    return inner


def mlp_forward(normed, up_a, up_b, down_a, down_b, biases, row, dtype):
    patches, cols = normed[0].shape[0], up_a.shape[1]
    model = down_a.shape[0]
    rows = 2 * patches

    def kernel(ins, fetch, outs, scratch):
        tokens = both(ins[0], ins[1])
        out = None
        for i in range(2):
            bias = ins[2][row + i : row + i + 1, :]
            pre = jnp.dot(tokens, fetch(2 * i)[...], preferred_element_type=f32) + bias
            outs[i][...] = pre
            hidden = (0.5 * pre * (1.0 + gelu_parts(pre))).astype(bf16)
            outs[2 + i][...] = hidden
            part = row_dot(hidden, fetch(2 * i + 1)[...])
            out = part if out is None else out + part
        outs[4][...] = out[:patches]
        outs[5][...] = out[patches:].astype(dtype)

    return call(
        kernel,
        "mlp_forward",
        [*normed, biases],
        [up_a, down_a, up_b, down_b],
        [((rows, cols), f32)] * 2 + [((rows, cols), bf16)] * 2 + [((patches, model), f32), ((patches, model), dtype)],
        limit=48,
    )


def mlp_backward(grad, pre, up, down, so_far):
    patches, model = grad[0].shape
    rows, cols = pre.shape
    last = so_far is not None

    def kernel(ins, fetch, outs, scratch):
        tokens = both(ins[0], ins[1])
        grad_hidden = jnp.dot(tokens, fetch(0)[...], preferred_element_type=f32)
        value = fetch(1)[...]
        inner = gelu_parts(value)
        slope = 0.5 * (1.0 + inner) + 0.5 * value * (1.0 - inner * inner) * (
            GELU_C * (1.0 + 3.0 * 0.044715 * (value * value))
        )
        grad_pre = (grad_hidden * slope).astype(bf16)
        outs[0][...] = grad_pre
        outs[1][0:1, :] = jnp.sum(grad_pre.astype(f32), axis=0, keepdims=True)
        outs[1][1:2, :] = jnp.sum(tokens.astype(f32), axis=0, keepdims=True)
        out = row_dot(grad_pre, fetch(2)[...])
        if last:
            out = out + fetch(3)[...]
            outs[2][...] = out[:patches]
            outs[3][...] = out[patches:].astype(bf16)
        else:
            outs[2][...] = out

    tail = [((patches, model), f32), ((patches, model), bf16)] if last else [((rows, model), f32)]
    return call(
        kernel,
        "mlp_backward",
        list(grad),
        [down, pre, up] + ([so_far] if last else []),
        [((rows, cols), bf16), ((2, cols), f32)] + tail,
        limit=32,
    )


def grad_heads(grad, w_vo):
    patches, model = grad[0].shape
    cols = w_vo.shape[1]

    def kernel(ins, fetch, outs, scratch):
        tokens = both(ins[0], ins[1])
        outs[1][...] = jnp.sum(tokens.astype(f32), axis=0, keepdims=True)
        outs[0][...] = jnp.dot(tokens, fetch(0)[...], preferred_element_type=f32).astype(bf16)

    return call(kernel, "grad_heads", list(grad), [w_vo], [((2 * patches, cols), bf16), ((1, model), f32)])


def norm_backward(g, own, other, x, mods, scale, gate, branch):
    rows, model = x.shape

    def kernel(ins, fetch, outs, scratch):
        grad = ins[1][...] + ins[2][...].astype(f32)
        normed, inverse = norm_parts(ins[3][...])
        scaled = grad * (1.0 + ins[4][scale : scale + 1, :])
        mean_one = jnp.mean(scaled, axis=-1, keepdims=True)
        mean_two = jnp.mean(scaled * normed, axis=-1, keepdims=True)
        value = ins[0][...] + inverse * (scaled - mean_one - normed * mean_two)
        outs[0][...] = value
        outs[1][0:1, :] = jnp.sum(grad, axis=0, keepdims=True)
        outs[1][1:2, :] = jnp.sum(grad * normed, axis=0, keepdims=True)
        if gate is not None:
            outs[1][2:3, :] = jnp.sum(value * ins[5][...], axis=0, keepdims=True)
            outs[2][...] = (ins[4][gate : gate + 1, :] * value).astype(bf16)

    inputs = [g, own, other, x, mods] + ([] if gate is None else [branch])
    outs = [(x.shape, f32), ((3, model), f32)] + ([] if gate is None else [(x.shape, bf16)])
    return call(kernel, "norm_backward", inputs, [], outs)


def insert_bit(rest, bit):
    low = rest & ((1 << bit) - 1)
    return (rest - low) * 2 + low


def weight_grad(pairs, bit, name):
    clusters, parts = lax.axis_size("dp"), lax.axis_size("seq")
    model, cols = pairs[0][0].shape[1], pairs[0][1].shape[1]
    rows = model // (clusters * parts)
    mine = ((lax.axis_index("seq") >> bit) & 1).astype(jnp.int32).reshape(1)
    shape = (clusters, parts // 2, rows, cols)
    count = len(pairs)

    def body(mine_ref, *refs):
        ins, outs, (whole, sem) = refs[: 2 * count], refs[2 * count : 2 * count + 2], refs[2 * count + 2 :]
        out = col_dot(ins[0][...], ins[1][...])
        for i in range(1, count):
            out = out + col_dot(ins[2 * i][...], ins[2 * i + 1][...])
        copies = []
        for c in range(clusters):
            for part in range(parts):
                at = (c * parts + part) * rows
                whole[c * parts + part] = out[at : at + rows].astype(bf16)
        for c in range(clusters):
            for rest in range(parts // 2):
                start = c * parts + insert_bit(rest, bit)
                for which in range(2):
                    side = mine_ref[0] if which == 0 else 1 - mine_ref[0]
                    copy = pltpu.make_async_copy(
                        whole.at[start + (side << bit)],
                        outs[which].at[c, rest],
                        sem.at[(c * (parts // 2) + rest) * 2 + which],
                    )
                    copy.start()
                    copies.append(copy)
        for copy in copies:
            copy.wait()

    return pl.pallas_call(
        body,
        out_shape=[jax.ShapeDtypeStruct(shape, bf16)] * 2,
        in_specs=[pl.BlockSpec(memory_space=pltpu.SMEM)] + [on_chip()] * (2 * count),
        out_specs=[in_place()] * 2,
        scratch_shapes=[
            pltpu.VMEM((clusters * parts, rows, cols), bf16),
            pltpu.SemaphoreType.DMA((clusters * parts,)),
        ],
        compiler_params=pltpu.CompilerParams(vmem_limit_bytes=32 * MIB),
        cost_estimate=LIGHT,
        name=name,
    )(mine, *[array for pair in pairs for array in pair])


def with_other(flow, own):
    flow.now += 5.0
    return own, swap(own)


def dispatch_in(flow, arrays, cost, hold):
    arrays[0] = flow.step(2.0, arrays[0])
    if hold:
        flow.hold(cost)
        result = dispatch(arrays)
        flow.release(result)
        return result
    flow.now += 2.5 * cost
    return dispatch(arrays)


def collect_in(flow, rows, cuts, cost, hold):
    rows = flow.step(2.0, rows)
    if hold:
        flow.hold(cost)
        result = collect(rows, cuts)
        flow.release(result[0])
        return result
    flow.now += 2.5 * cost
    return collect(rows, cuts)


def layer_forward(flow, x, normed_one, mods, layer, units, biases_of, temporal, following):
    attention_unit, mlp_unit = units
    patches = x.shape[0]
    base = 6 * layer
    normed_one = with_other(flow, normed_one)
    w_qk, w_vo = attention_unit()
    width = w_qk.shape[1] // 2
    biases = biases_of()
    qk, vo = flow.ran(project_heads((flow.step(6.5, normed_one[0]), normed_one[1]), w_qk, w_vo, biases, base))
    qk = qk.reshape(2, patches, -1)
    vo = vo.reshape(2, patches, -1)
    if temporal:
        period = patches // lax.axis_size("seq")
        qkv = dispatch_in(flow, [qk, vo[:, :, :width]], 17.0, False)
        heads = (flow.step(3.5, qkv), qkv, 2 * width)
        attended = attend(*heads, width, 0, period)
        attended = collect_in(flow, attended, ((0, period, 0, width, width, 0),), 11.0, False)[0]
    else:
        heads = (flow.step(3.5, qk), vo, 0)
        attended = attend(*heads, width, width, None).reshape(2 * patches, -1)
    own, other = flow.ran(project_back([(flow.step(2.5, attended), w_vo)], f32, "project_out"))
    other = swap(other)
    flow.now += 5.0
    branch, x_mid, normed_two = flow.ran(
        residual(x, flow.step(2.0, own), other, biases, base + 2, mods, base + 2, (base + 3, base + 4))
    )
    normed_two = with_other(flow, normed_two)
    w_up_a, w_up_b, w_down_a, w_down_b = mlp_unit()
    tokens = (flow.step(11.0, normed_two[0]), normed_two[1])
    pre_a, pre_b, hidden_a, hidden_b, own, other = flow.ran(
        mlp_forward(tokens, w_up_a, w_up_b, w_down_a, w_down_b, biases, base + 3, f32)
    )
    other = swap(other)
    flow.now += 5.0
    mlp, x_next, after = flow.ran(
        residual(x_mid, flow.step(2.0, own), other, biases, base + 5, mods, base + 5, following)
    )
    saved = (x, normed_one, heads, attended, branch, x_mid, normed_two, pre_a, pre_b, hidden_a, hidden_b, mlp)
    weights = (w_qk, w_vo, w_up_a, w_up_b, w_down_a, w_down_b)
    return x_next, after, saved, weights


def layer_backward(flow, g, grad_mlp, mods, layer, weights, saved, temporal, below):
    w_qk, w_vo, w_up_a, w_up_b, w_down_a, w_down_b = weights
    x, normed_one, heads, attended, branch, x_mid, normed_two, pre_a, pre_b, hidden_a, hidden_b, _ = saved
    patches = x.shape[0]
    width = w_qk.shape[1] // 2
    base = 6 * layer
    done = [Scatter(flow, 10 - 4 * layer - unit) for unit in range(3)]
    bits = (bits_of(lax.axis_size("seq")) - 1, 0)

    def reduce_half(unit, which, pairs, name):
        first = flow.step(5.0, pairs[0][1])
        done[unit].give(which, *flow.ran(weight_grad([(pairs[0][0], first)] + pairs[1:], bits[which], name)))

    def joined(pair):
        return jnp.concatenate(pair, axis=0)

    grad_mlp = with_other(flow, grad_mlp)
    grad_mlp_rows = joined(grad_mlp)
    reduce_half(2, 0, [(grad_mlp_rows, hidden_a)], "down_grad")
    reduce_half(2, 1, [(grad_mlp_rows, hidden_b)], "down_grad")
    normed_rows = joined(normed_two)
    tokens = (flow.step(7.0, grad_mlp[0]), grad_mlp[1])
    grad_pre_a, sums_a, so_far = flow.ran(mlp_backward(tokens, pre_a, w_up_a, w_down_a, None))
    reduce_half(1, 0, [(normed_rows, grad_pre_a)], "up_grad")
    tokens = (flow.step(8.0, grad_mlp[0]), grad_mlp[1])
    grad_pre_b, sums_b, own, other = flow.ran(mlp_backward(tokens, pre_b, w_up_b, w_down_b, so_far))
    other = swap(other)
    reduce_half(1, 1, [(normed_rows, grad_pre_b)], "up_grad")
    g_mid, sums_two, grad_branch = flow.ran(
        norm_backward(g, flow.step(2.0, own), other, x_mid, mods, base + 4, base + 2, branch)
    )
    other_branch = swap(grad_branch)
    flow.now += 4.0
    grad_branch = (flow.step(2.5, grad_branch), other_branch)
    grad_att, sum_branch = flow.ran(grad_heads(grad_branch, w_vo))
    grad_att = grad_att.reshape(2, patches, -1)
    if temporal:
        period = patches // lax.axis_size("seq")
        grad_att = dispatch_in(flow, [grad_att[:, :, width:]], 10.0, True)
        grad_qkv, sums_pair = flow.ran(attend_grad(*heads, flow.step(10.5, grad_att), 0, width, period))
        cuts = ((0, period, 0, 2 * width, 0, 0), (0, period, 2 * width, width, 0, width))
        grad_qk, grad_v = collect_in(flow, grad_qkv, cuts, 18.0, True)
    else:
        grad_qk, grad_v, sums_pair = flow.ran(
            attend_grad(*heads, flow.step(10.5, grad_att), width, width, None)
        )
        grad_qk = grad_qk.reshape(2 * patches, -1)
        grad_v = grad_v.reshape(2 * patches, -1)
    own, other = flow.ran(
        project_back([(flow.step(5.0, grad_qk), w_qk), (grad_v, w_vo)], bf16, "grad_normed")
    )
    other = swap(other)
    rows_one = joined(normed_one)
    reduce_half(0, 0, [(rows_one, grad_qk)], "heads_grad")
    own = flow.step(2.0, own)
    if below is None:
        g_below, sums_one = flow.ran(norm_backward(g_mid, own, other, x, mods, base + 1, None, None))
        grad_below = None
    else:
        g_below, sums_one, grad_below = flow.ran(
            norm_backward(g_mid, own, other, x, mods, base + 1, base - 1, below)
        )
    reduce_half(0, 1, [(rows_one, grad_v), (joined(grad_branch), attended)], "heads_grad")
    mod_sums = [sums_one[0], sums_one[1], sums_two[2], sums_two[0], sums_two[1]]
    bias_sums = [
        jnp.sum(sums_pair, axis=0).reshape(-1),
        sum_branch.reshape(-1),
        sums_a[0],
        sums_b[0],
        sums_a[1],
    ]
    return g_below, grad_below, mod_sums, sums_one[2], bias_sums, done


def shards(
    tokens,
    conditioning,
    cotangent,
    modulation_weight,
    modulation_bias,
    triple_weight,
    pair_bias,
    out_weight,
    out_bias,
    hidden_weight,
    hidden_bias,
    output_weight,
    output_bias,
):
    layers, _, _, width = triple_weight.shape
    model = tokens.shape[3]
    patches = tokens.shape[2]
    own_clips = tokens.shape[0] // lax.axis_size("tensor")
    all_clips = conditioning.shape[0]
    assert own_clips == 1 and tokens.shape[1] == 1 and layers == 2
    assert model == 2 * width and hidden_weight.shape[2] == 2 * model
    units = hidden_weight.shape[2]
    half = units // 2
    dp_index, seq_index = lax.axis_index("dp"), lax.axis_index("seq")
    core = lax.axis_index("tensor")
    n_dp, n_seq, n_core = lax.axis_size("dp"), lax.axis_size("seq"), lax.axis_size("tensor")

    packed = jnp.concatenate(
        [pair_bias.reshape(layers, -1), out_bias, hidden_bias.reshape(layers, -1), output_bias], axis=1
    ).reshape(-1)
    rows = triple_weight.shape[1]

    def attention_unit(layer):
        triple = triple_weight[layer]
        first = jnp.concatenate([triple[:, 0], triple[:, 1]], axis=1)
        second = jnp.concatenate([triple[:, 2], out_weight[layer].T], axis=1)
        if layer == 0:
            extra = jnp.zeros((8 * 2 * width,), bf16).at[: packed.shape[0]].set(packed).reshape(8, -1)
            first = jnp.concatenate([first, extra])
            second = jnp.concatenate([second, jnp.zeros_like(extra)])
        return jnp.stack([first, second])

    def mlp_unit(layer):
        down = output_weight[layer].T
        up = hidden_weight[layer]
        return jnp.stack(
            [jnp.concatenate([up[:, part], down[:, part]], axis=1) for part in (slice(0, half), slice(half, None))]
        )

    flow = Flow()
    flow.now = 8.0
    gathers = []
    for layer in range(layers):
        whole = (0, rows, 0, 2 * width, 0, 0)
        first_cuts = (whole, (rows, 8, 0, 2 * width, 0, 0)) if layer == 0 else (whole,)
        attention = Gather(flow, 2 * layer, attention_unit(layer), dp_index, seq_index, (first_cuts, (whole,)), 2.0)
        pair_cuts = ((0, rows, 0, half, 0, 0), (0, rows, half, half, 0, 0))
        mlp = Gather(flow, 2 * layer + 1, mlp_unit(layer), dp_index, seq_index, (pair_cuts, pair_cuts), 3.5)
        gathers.append((attention, mlp))

    act_cond, silu_back = jax.vjp(jax.nn.silu, conditioning)
    act_low = act_cond.astype(bf16)
    local_term = jnp.einsum("cd,lde->cle", act_low, modulation_weight, preferred_element_type=f32)
    bias_cols = modulation_bias.shape[1]
    offset = ((dp_index * n_seq + seq_index) * n_core + core) * bias_cols
    bias_full = lax.dynamic_update_slice(
        jnp.zeros((layers, local_term.shape[2]), f32), modulation_bias.astype(f32), (jnp.int32(0), offset)
    )
    contribution = (local_term + bias_full[None]).reshape(n_dp, n_core, -1)
    contribution = take(contribution, 1, core) + swap(take(contribution, 1, 1 - core))
    contribution = flow.step(25.0, contribution)
    mods = sum_small(scatter_small(contribution, "dp"), "seq").reshape(layers * 6, model)

    def unpack(spread):
        spread = spread.reshape(n_dp * n_seq, -1)[:, : packed.shape[0]].reshape(n_dp * n_seq, layers, -1)
        spread = spread.transpose(1, 0, 2).astype(f32)
        cuts, at = [], 0
        for size in (pair_bias.shape[3], pair_bias.shape[3], out_bias.shape[1], hidden_bias.shape[2], output_bias.shape[1]):
            cuts.append(spread[:, :, at : at + size].reshape(layers, -1))
            at += size
        blank = jnp.zeros_like(cuts[0])
        return jnp.concatenate([cuts[0], blank, cuts[1], blank, *cuts[2:]], axis=1).reshape(6 * layers, model)

    found = {}

    def attention_weights(layer):
        first, second = gathers[layer][0].result()
        if layer == 0:
            found["biases"] = unpack(first[1])
        return first[0], second[0]

    def mlp_weights(layer):
        first, second = gathers[layer][1].result()
        return first[0], second[0], first[1], second[1]

    x = take(tokens, 0, core).reshape(patches, model).astype(f32)
    after = norm_forward(x, mods, 0, 1)
    kept, weights = [], []
    for layer in range(layers):
        following = (6 * layer + 6, 6 * layer + 7) if layer + 1 < layers else None
        pending = (partial(attention_weights, layer), partial(mlp_weights, layer))
        x, after, saved, layer_weights = layer_forward(
            flow, x, after, mods, layer, pending, lambda: found["biases"], layer == 1, following
        )
        kept.append(saved)
        weights.append(layer_weights)

    def to_both(own):
        other = swap(own)
        pair = jnp.stack([jnp.where(core == 0, own, other), jnp.where(core == 0, other, own)])
        return pair.reshape((2, 1) + own.shape)

    activations = to_both(after)
    g = take(cotangent, 0, core).reshape(patches, model).astype(f32)
    grad_mlp = (mods[6 * layers - 1] * g).astype(bf16)
    grad_gates = [None] * layers
    grad_gates[-1] = jnp.sum(g * kept[-1][-1], axis=0)
    mod_grads, bias_grads, done = [None] * layers, [None] * layers, [None] * layers
    flow.depth = 2
    for layer in reversed(range(layers)):
        below = kept[layer - 1][-1] if layer else None
        g, grad_mlp, mod_sums, grad_gate, bias_grads[layer], done[layer] = layer_backward(
            flow, g, grad_mlp, mods, layer, weights[layer], kept[layer], layer == 1, below
        )
        mod_grads[layer] = jnp.concatenate(mod_sums + [grad_gates[layer]])
        if layer:
            grad_gates[layer - 1] = grad_gate
    input_grad = to_both(g)
    flow.until(lambda: all(unit.total is not None for layer in range(layers) for unit in done[layer]))

    def stack_layers(which, build):
        return jnp.stack([build(done[layer][which].total) for layer in range(layers)])

    triple_grad = stack_layers(
        0, lambda u: jnp.stack([u[0][:, :width], u[0][:, width:], u[1][:, :width]], axis=1)
    )
    out_grad = stack_layers(0, lambda u: u[1][:, width:].T)
    hidden_grad = stack_layers(1, lambda u: jnp.concatenate([u[0], u[1]], axis=1))
    output_grad = stack_layers(2, lambda u: jnp.concatenate([u[0], u[1]], axis=1).T)

    flat = [part for layer in range(layers) for part in bias_grads[layer]]
    summed = sum_small(jnp.concatenate(mod_grads + flat), "seq").astype(bf16)
    mods_size = 6 * model * layers
    pair = jnp.concatenate([summed[:mods_size], swap(summed[:mods_size]), summed[mods_size:]])
    spread = gather_small(pair.reshape(1, -1, 128), "dp").reshape(n_dp, -1)
    spread = [spread[rel] for rel in range(n_dp)]
    grad_mods = jnp.stack([s[c * mods_size : (c + 1) * mods_size] for s in spread for c in range(n_core)])
    grad_mods = grad_mods.reshape(all_clips, layers, -1)
    clip = jnp.arange(all_clips)
    clip = (clip // n_core ^ dp_index) * n_core + (clip % n_core ^ core)
    bias_sums = add_up([s[n_core * mods_size :] for s in spread]).reshape(layers, -1)
    owner = dp_index * n_seq + seq_index
    bias_out, at = [], 0
    for size, shape in (
        (width, None),
        (width, None),
        (model, out_bias.shape),
        (units, hidden_bias.shape),
        (model, output_bias.shape),
    ):
        part = bias_sums[:, at : at + size].reshape(layers, n_dp * n_seq, -1)
        part = take(part, 1, owner)
        bias_out.append(part if shape is None else part.reshape(shape))
        at += size
    pair_out = jnp.stack(bias_out[:2], axis=1).reshape(pair_bias.shape)
    out_bias_grad, hidden_bias_grad, output_bias_grad = bias_out[2:]
    modulation_weight_grad = jnp.einsum("cd,cle->lde", act_low[clip], grad_mods, preferred_element_type=f32)
    modulation_bias_grad = lax.dynamic_slice_in_dim(
        jnp.sum(grad_mods, axis=0, dtype=f32), offset, bias_cols, 1
    )
    grad_act = jnp.einsum("cle,lde->cd", grad_mods, modulation_weight, preferred_element_type=f32)
    cond_grad = silu_back(grad_act[clip])[0]
    return (
        activations,
        input_grad,
        cond_grad,
        modulation_weight_grad,
        modulation_bias_grad,
        triple_grad,
        pair_out,
        out_grad,
        out_bias_grad,
        hidden_grad,
        hidden_bias_grad,
        output_grad,
        output_bias_grad,
    )


def solution(mesh):
    owners = ("dp", "seq")
    everyone = ("dp", "seq", "tensor")
    rows = P("dp", "seq", None, None)
    weights = (
        P(None, everyone, None),
        P(None, everyone),
        P(None, owners, None, "tensor"),
        P(None, None, "tensor", owners),
        P(None, "tensor", owners),
        P(None, owners),
        P(None, owners, "tensor"),
        P(None, "tensor", owners),
        P(None, "tensor", owners),
        P(None, owners),
    )
    return jax.shard_map(
        shards,
        mesh=mesh,
        in_specs=(rows, P(None, everyone), rows) + weights,
        out_specs=(rows, rows, P(None, everyone)) + weights,
        check_vma=False,
    )
```

time: 1020 us -> 912 us (0.89)
  matrix products: 137 us -> 1.18 us
  Pallas kernels: 74.4 us -> 199 us
  starting transfers between devices: 131 us -> 93.1 us
  local copies, waits for them, and re-layouts: 121 us -> 101 us
  waiting for transfers between devices: 449 us -> 430 us
  other arithmetic: 88.9 us -> 72.6 us
  between operations: 17.7 us -> 4.34 us
    dot_general x43 -> x1, matrix products: 135 us -> 0.48 us  [shards(): jnp.einsum('cd,cle->lde', act_low[clip], grad_mods, preferred_element_typ...]
    pallas_call x19 -> x49, Pallas kernels: 74.4 us -> 199 us  [the longest x23 93.9 us: call(): pl.pallas_call(body, out_shape=[jax.ShapeDtypeStruct(shape, dtype) for sh...]
    ppermute x127 -> x112, starting transfers between devices: 130 us -> 93.1 us  [pxor(): return lax.ppermute(value, axis, [(i, i ^ flip) for i in range(size)])]
    unnamed x399 -> x470, local copies, waits for them, and re-layouts: 42.3 us -> 69.8 us
    reduce_sum x26 -> x3, other arithmetic: 26.3 us -> 0.83 us  [the longest x2 0.62 us: layer_backward(): jnp.sum(sums_pair, axis=0).reshape(-1)]
    ppermute x127 -> x112, waiting for transfers between devices: 449 us -> 430 us  [pxor(): return lax.ppermute(value, axis, [(i, i ^ flip) for i in range(size)])]
    concatenate x21 -> x6, local copies, waits for them, and re-layouts: 15.6 us -> 1.45 us  [the longest x4 1.34 us: joined(): return jnp.concatenate(pair, axis=0)]
    convert_element_type x31 -> x36, other arithmetic: 19.2 us -> 31.4 us  [the longest x16 17.6 us: split(): kept = add_up([take(part, dim, mine) for part in parts]).astype(bf16)]
  transfers between devices with their start and end apart: 132 -> 112, of which waited for: 48 -> 50; matrix products, arithmetic and copies ran while one was open for 27% -> 11% of each run, Pallas kernels for 7% -> 19%
where the time goes in v2:
time: 912 us; the launch traced here: 901 us
  waiting for transfers between devices  430 us (47%)
  Pallas kernels  199 us (22%)
  local copies, waits for them, and re-layouts  101 us (11%)
  starting transfers between devices  93.1 us (10%)
  other arithmetic  72.6 us (8%)
    ppermute x112, waiting for transfers between devices, pxor(): return lax.ppermute(value, axis, [(i, i ^ flip) for i in range(size)])  430 us
    pallas_call x23, Pallas kernels, call(): pl.pallas_call(body, out_shape=[jax.ShapeDtypeStruct(shape, dtype) for sh...  93.9 us
    ppermute x112, starting transfers between devices, pxor(): return lax.ppermute(value, axis, [(i, i ^ flip) for i in range(size)])  93.1 us
    unnamed x470, local copies, waits for them, and re-layouts  69.8 us
    pallas_call x12, Pallas kernels, weight_grad(): pl.pallas_call(body, out_shape=[jax.ShapeDtypeStruct(shape, bf16)] * 2, i...  60.1 us
    pallas_call x2, Pallas kernels, attend_grad(): pl.pallas_call(partial(attend_grad_kernel, period, lead, skip), grid=(blo...  21.1 us
  transfers between devices with their start and end apart: 112, of which 50 were waited for; matrix products, arithmetic and copies ran while one was open for 11% of the time, Pallas kernels for 19%

profile of v2, /device:TPU:0, one launch (start us, length us, event | category | flops | bytes accessed | tf_op | source)
XLA Modules:
  0.0 901.3 jit_solution(6471498435522133641)
XLA Ops:
  29.6 8.0 collective-permute-done.6
  37.7 9.0 collective-permute-done.7
  56.1 10.7 %collective-permute-done.3 = f32[13824]{0:T(1024)S(1)} collective-permute-done((f32[13824]{0:T(1024)S(1)}, f32[13824]{0:T(1024)S(1)}, u32[]{:S(2)}, u32[]{:S(2)}) %collective-permute-start.3) | collective-permute-done | bytes 55328 | tf_op jit(solution)/shard_map/ppermute | solution.py:111
  67.3 14.1 %collective-permute-done.10 = bf16[2,72,2304]{2,1,0:T(8,128)(2,1)S(1)} collective-permute-done((bf16[2,72,2304]{2,1,0:T(8,128)(2,1)S(1)}, bf16[2,72,2304]{2,1,0:T(8,128)(2,1)S(1)}, u32[]{:S(2)}, u32[]{:S(2)}) %collective-permute-start.10) | collective-permute-done | bytes 663584 | tf_op jit(solution)/shard_map/ppermute | solution.py:111
  84.7 12.8 %collective-permute-done.13 = bf16[2,72,2304]{2,1,0:T(8,128)(2,1)S(1)} collective-permute-done((bf16[2,72,2304]{2,1,0:T(8,128)(2,1)S(1)}, bf16[2,72,2304]{2,1,0:T(8,128)(2,1)S(1)}, u32[]{:S(2)}, u32[]{:S(2)}) %collective-permute-start.13) | collective-permute-done | bytes 663584 | tf_op jit(solution)/shard_map/ppermute | solution.py:111
  102.4 10.4 %collective-permute-done.17 = bf16[2,72,2304]{2,1,0:T(8,128)(2,1)S(1)} collective-permute-done((bf16[2,72,2304]{2,1,0:T(8,128)(2,1)S(1)}, bf16[2,72,2304]{2,1,0:T(8,128)(2,1)S(1)}, u32[]{:S(2)}, u32[]{:S(2)}) %collective-permute-start.17) | collective-permute-done | bytes 663584 | tf_op jit(solution)/shard_map/ppermute | solution.py:111
  155.4 8.0 collective-permute-done.20
  164.1 8.8 collective-permute-done.23
  173.1 11.9 %collective-permute-done.24.refs_1_ = bf16[4,72,2304]{2,1,0:T(8,128)(2,1)S(1)} collective-permute-done((bf16[4,72,2304]{2,1,0:T(8,128)(2,1)S(1)}, bf16[4,72,2304]{2,1,0:T(8,128)(2,1)S(1)}, u32[]{:S(2)}, u32[]{:S(2)}) %collective-permute-start.24) | collective-permute-done | bytes 1327136 | tf_op jit(solution)/shard_map/ppermute | solution.py:111
  188.7 14.8 %collective-permute-done.26 = bf16[2,72,2304]{2,1,0:T(8,128)(2,1)S(1)} collective-permute-done((bf16[2,72,2304]{2,1,0:T(8,128)(2,1)S(1)}, bf16[2,72,2304]{2,1,0:T(8,128)(2,1)S(1)}, u32[]{:S(2)}, u32[]{:S(2)}) %collective-permute-start.26) | collective-permute-done | bytes 663584 | tf_op jit(solution)/shard_map/ppermute | solution.py:111
  204.4 15.8 %collective-permute-done.28 = bf16[2,72,2304]{2,1,0:T(8,128)(2,1)S(1)} collective-permute-done((bf16[2,72,2304]{2,1,0:T(8,128)(2,1)S(1)}, bf16[2,72,2304]{2,1,0:T(8,128)(2,1)S(1)}, u32[]{:S(2)}, u32[]{:S(2)}) %collective-permute-start.28) | collective-permute-done | bytes 663584 | tf_op jit(solution)/shard_map/ppermute | solution.py:111
  221.6 14.9 %collective-permute-done.32.refs_2_ = bf16[4,72,1152]{2,1,0:T(8,128)(2,1)S(1)} collective-permute-done((bf16[4,72,1152]{2,1,0:T(8,128)(2,1)S(1)}, bf16[4,72,1152]{2,1,0:T(8,128)(2,1)S(1)}, u32[]{:S(2)}, u32[]{:S(2)}) %collective-permute-start.32) | collective-permute-done | bytes 663584 | tf_op jit(solution)/shard_map/ppermute | solution.py:111
  238.0 13.5 %collective-permute-done.35.refs_2_ = bf16[4,72,1152]{2,1,0:T(8,128)(2,1)S(1)} collective-permute-done((bf16[4,72,1152]{2,1,0:T(8,128)(2,1)S(1)}, bf16[4,72,1152]{2,1,0:T(8,128)(2,1)S(1)}, u32[]{:S(2)}, u32[]{:S(2)}) %collective-permute-start.35) | collective-permute-done | bytes 663584 | tf_op jit(solution)/shard_map/ppermute | solution.py:111
  263.1 10.6 %mlp_forward.2 = (f32[512,1152]{1,0:T(8,128)}, f32[512,1152]{1,0:T(8,128)}, bf16[512,1152]{1,0:T(8,128)(2,1)S(1)}, bf16[512,1152]{1,0:T(8,128)(2,1)S(1)}, f32[25...) custom-call(bf16[256,1152]{1,0:T(8,128)(2,1)S(1)} %get-tuple-element.283.refs_0_, ...), custom_call_target="tpu_custom_call" | custom-call | flops 1 | bytes 1 | tf_op jit(solution)/shard_map/mlp_forward/pallas_call | solution.py:465
  285.0 20.3 %collective-permute-done.40.refs_2_ = bf16[4,72,2304]{2,1,0:T(8,128)(2,1)S(1)} collective-permute-done((bf16[4,72,2304]{2,1,0:T(8,128)(2,1)S(1)}, bf16[4,72,2304]{2,1,0:T(8,128)(2,1)S(1)}, u32[]{:S(2)}, u32[]{:S(2)}) %collective-permute-start.40) | collective-permute-done | bytes 1327136 | tf_op jit(solution)/shard_map/ppermute | solution.py:111
  325.8 13.0 %collective-permute-done.46.refs_2_ = bf16[4,72,2304]{2,1,0:T(8,128)(2,1)} collective-permute-done((bf16[4,72,2304]{2,1,0:T(8,128)(2,1)}, bf16[4,72,2304]{2,1,0:T(8,128)(2,1)}, u32[]{:S(2)}, u32[]{:S(2)}) %collective-permute-start.46) | collective-permute-done | bytes 1327136 | tf_op jit(solution)/shard_map/ppermute | solution.py:111
  350.6 37.1 %collective-permute-done.44 = bf16[2,64,1728]{2,1,0:T(8,128)(2,1)S(1)} collective-permute-done((bf16[2,64,1728]{2,1,0:T(8,128)(2,1)S(1)}, bf16[2,64,1728]{2,1,0:T(8,128)(2,1)S(1)}, u32[]{:S(2)}, u32[]{:S(2)}) %collective-permute-start.44) | collective-permute-done | bytes 442400 | tf_op jit(solution)/shard_map/ppermute | solution.py:111
  421.1 11.6 %mlp_forward.3 = (f32[512,1152]{1,0:T(8,128)}, f32[512,1152]{1,0:T(8,128)}, bf16[512,1152]{1,0:T(8,128)(2,1)S(1)}, bf16[512,1152]{1,0:T(8,128)(2,1)S(1)}, f32[256,1152]{1,0:T(8,128)S(1)}, /*index=5*/f32[256,1152]{1,0:T(8,128)}) custom-call(bf16[256,1152]{1,0:T(8,128)(2,1)S(1)} %get-tuple-element.320.refs_0_, ...), custom_call_target="tpu_custom_call" | custom-call | flops 1 | bytes 1 | tf_op jit(solution)/shard_map/mlp_forward/pallas_call | solution.py:465
  500.8 26.6 %collective-permute-done.65 = bf16[4,2,72,1152]{3,2,1,0:T(8,128)(2,1)S(1)} collective-permute-done((bf16[4,2,72,1152]{3,2,1,0:T(8,128)(2,1)S(1)}, bf16[4,2,72,1152]{3,2,1,0:T(8,128)(2,1)S(1)}, u32[]{:S(2)}, u32[]{:S(2)}) %collective-permute-start.65) | collective-permute-done | bytes 1327136 | tf_op jit(solution)/shard_map/ppermute | solution.py:111
  543.8 7.6 collective-permute-done.72
  563.0 10.3 %attend_grad.2 = (bf16[2,256,1728]{2,1,0:T(8,128)(2,1)S(1)}, f32[2,2,576]{2,1,0:T(2,128)S(1)}) custom-call(bf16[2,256,1728]{2,1,0:T(8,128)(2,1)S(1)} %bitcast.446, bf16[2,256,1728]{2,1,0:T(8,128)(2,1)S(1)} %bitcast.447, bf16[2,256,576]{2,1,0:T(8,128)(2,1)S(1)} %bitcast.484), custom_call_target="tpu_custom_call" | custom-call | flops 1 | bytes 1 | tf_op jit(solution)/shard_map/attend_grad/pallas_call | solution.py:420
  578.1 8.9 collective-permute-done.69.refs_1_
  587.0 8.9 collective-permute-done.71.refs_3_
  614.6 9.4 %collective-permute-done.76 = bf16[2,72,1152]{2,1,0:T(8,128)(2,1)} collective-permute-done((bf16[2,72,1152]{2,1,0:T(8,128)(2,1)}, bf16[2,72,1152]{2,1,0:T(8,128)(2,1)}, u32[]{:S(2)}, u32[]{:S(2)}) %collective-permute-start.76) | collective-permute-done | bytes 331808 | tf_op jit(solution)/shard_map/ppermute | solution.py:111
  718.3 10.8 %attend_grad.3 = (bf16[2,256,1152]{2,1,0:T(8,128)(2,1)S(1)}, bf16[2,256,1152]{2,1,0:T(8,128)(2,1)S(1)}, f32[2,2,576]{2,1,0:T(2,128)S(1)}) custom-call(bf16[2,256,1152]{2,1,0:T(8,128)(2,1)S(1)} %bitcast.473, bf16[2,256,1152]{2,1,0:T(8,128)(2,1)S(1)} %bitcast.475, bf16[2,256,1152]{2,1,0:T(8,128)(2,1)S(1)} %bitcast.487), custom_call_target="tpu_custom_call" | custom-call | flops 1 | bytes 1 | tf_op jit(solution)/shard_map/attend_grad/pallas_call | solution.py:420
  753.6 9.1 %collective-permute-done.105 = bf16[2,72,1152]{2,1,0:T(8,128)(2,1)S(1)} collective-permute-done((bf16[2,72,1152]{2,1,0:T(8,128)(2,1)S(1)}, bf16[2,72,1152]{2,1,0:T(8,128)(2,1)S(1)}, u32[]{:S(2)}, u32[]{:S(2)}) %collective-permute-start.105) | collective-permute-done | bytes 331808 | tf_op jit(solution)/shard_map/ppermute | solution.py:111
  787.3 8.2 collective-permute-done.94
  806.7 14.4 %collective-permute-done.107 = bf16[2,72,1152]{2,1,0:T(8,128)(2,1)S(1)} collective-permute-done((bf16[2,72,1152]{2,1,0:T(8,128)(2,1)S(1)}, bf16[2,72,1152]{2,1,0:T(8,128)(2,1)S(1)}, u32[]{:S(2)}, u32[]{:S(2)}) %collective-permute-start.107) | collective-permute-done | bytes 331808 | tf_op jit(solution)/shard_map/ppermute | solution.py:111
  834.9 7.4 collective-permute-done.108
  843.3 9.7 %collective-permute-done.101 = bf16[4,2,72,1152]{3,2,1,0:T(8,128)(2,1)S(1)} collective-permute-done((bf16[4,2,72,1152]{3,2,1,0:T(8,128)(2,1)S(1)}, bf16[4,2,72,1152]{3,2,1,0:T(8,128)(2,1)S(1)}, u32[]{:S(2)}, u32[]{:S(2)}) %collective-permute-start.101) | collective-permute-done | bytes 1327136 | tf_op jit(solution)/shard_map/ppermute | solution.py:111
  869.1 13.9 %collective-permute-done.110 = bf16[2,2,72,1152]{3,2,0,1:T(8,128)(2,1)S(1)} collective-permute-done((bf16[2,2,72,1152]{3,2,0,1:T(8,128)(2,1)S(1)}, bf16[2,2,72,1152]{3,2,0,1:T(8,128)(2,1)S(1)}, u32[]{:S(2)}, u32[]{:S(2)}) %collective-permute-start.110) | collective-permute-done | bytes 663584 | tf_op jit(solution)/shard_map/ppermute | solution.py:111
  885.6 11.7 %collective-permute-done.111 = bf16[2,72,1152]{2,1,0:T(8,128)(2,1)S(1)} collective-permute-done((bf16[2,72,1152]{2,1,0:T(8,128)(2,1)S(1)}, bf16[2,72,1152]{2,1,0:T(8,128)(2,1)S(1)}, u32[]{:S(2)}, u32[]{:S(2)}) %collective-permute-start.111) | collective-permute-done | bytes 331808 | tf_op jit(solution)/shard_map/ppermute | solution.py:111
  (944 shorter events, 494.6 us)
Async XLA Ops:
  46.9 34.6 %collective-permute-start.9 = (bf16[4,80,1152]{2,1,0:T(8,128)(2,1)S(1)}, bf16[4,80,1152]{2,1,0:T(8,128)(2,1)S(1)}, u32[]{:S(2)}, u32[]{:S(2)}) collective-permute-start(bf16[4,80,1152]{2,1,0:T(8,128)(2,1)S(1)} %pad_maximum_fusion.13.refs_0_), channel_id=1, source_target_pairs={{0,4},{2,6},{4,0},{6,2},{1,5},{3,7},{5,1},{7,3},{8,12},{10,14},{12... | collective-permute-start | bytes 2211848 | tf_op jit(solution)/shard_map/ppermute | solution.py:111
  66.8 53.8 %collective-permute-start.4 = (f32[13824]{0:T(1024)S(1)}, f32[13824]{0:T(1024)S(1)}, u32[]{:S(2)}, u32[]{:S(2)}) collective-permute-start(f32[13824]{0:T(1024)S(1)} %add.600), channel_id=1, source_target_pairs={{0,4},{2,6},{4,0},{6,2},{1,5},{3,7},{5,1},{7,3},{8,12},{10,14},{12... | collective-permute-start | bytes 165896 | tf_op jit(solution)/shard_map/ppermute | solution.py:111
  116.8 37.0 %collective-permute-start.22 = (bf16[4,72,2304]{2,1,0:T(8,128)(2,1)}, bf16[4,72,2304]{2,1,0:T(8,128)(2,1)}, u32[]{:S(2)}, u32[]{:S(2)}) collective-permute-start(bf16[4,72,2304]{2,1,0:T(8,128)(2,1)} %pad_maximum_fusion.2.refs_0_), channel_id=1, source_target_pairs={{0,4},{2,6},{4,0},{6,2},{1,5},{3,7},{5,1},{7,3},{8,12},{10,14},{12... | collective-permute-start | bytes 3981320 | tf_op jit(solution)/shard_map/ppermute | solution.py:111
  118.0 36.1 %collective-permute-start.21 = (bf16[4,72,2304]{2,1,0:T(8,128)(2,1)}, bf16[4,72,2304]{2,1,0:T(8,128)(2,1)}, u32[]{:S(2)}, u32[]{:S(2)}) collective-permute-start(bf16[4,72,2304]{2,1,0:T(8,128)(2,1)} %pad_maximum_fusion.2.refs_0_), channel_id=1, source_target_pairs={{0,2},{2,0},{4,6},{6,4},{1,3},{3,1},{5,7},{7,5},{8,10},{10,8},{12,... | collective-permute-start | bytes 3981320 | tf_op jit(solution)/shard_map/ppermute | solution.py:111
  152.9 34.1 %collective-permute-start.18 = (f32[256,1152]{1,0:T(8,128)S(1)}, f32[256,1152]{1,0:T(8,128)S(1)}, u32[]{:S(2)}, u32[]{:S(2)}) collective-permute-start(f32[256,1152]{1,0:T(8,128)S(1)} %get-tuple-element.261), channel_id=1, source_target_pairs={{0,1},{1,0},{2,3},{3,2},{4,5},{5,4},{6,7},{7,6},{8,9},{9,8},{10,11... | collective-permute-start | bytes 3538952 | tf_op jit(solution)/shard_map/ppermute | solution.py:111
  185.3 35.2 %collective-permute-start.29 = (bf16[4,72,2304]{2,1,0:T(8,128)(2,1)}, bf16[4,72,2304]{2,1,0:T(8,128)(2,1)S(1)}, u32[]{:S(2)}, u32[]{:S(2)}) collective-permute-start(bf16[4,72,2304]{2,1,0:T(8,128)(2,1)} %collective-permute-done.21.refs_1_), channel_id=1, source_target_pairs={{0,4},{2,6},{4,0},{6,2},{1,5},{3,7},{5,1},{7,3},{8,12},{10,14},{12... | collective-permute-start | bytes 3981320 | tf_op jit(solution)/shard_map/ppermute | solution.py:111
  188.7 74.4 %collective-permute-start.33 = (bf16[256,1152]{1,0:T(8,128)(2,1)S(1)}, bf16[256,1152]{1,0:T(8,128)(2,1)S(1)}, u32[]{:S(2)}, u32[]{:S(2)}) collective-permute-start(bf16[256,1152]{1,0:T(8,128)(2,1)S(1)} %get-tuple-element.283.refs_0_), channel_id=1, source_target_pairs={{0,1},{1,0},{2,3},{3,2},{4,5},{5,4},{6,7},{7,6},{8,9},{9,8},{10,11... | collective-permute-start | bytes 1769480 | tf_op jit(solution)/shard_map/ppermute | solution.py:111
  203.5 33.3 %collective-permute-start.31 = (bf16[4,72,2304]{2,1,0:T(8,128)(2,1)S(1)}, bf16[4,72,2304]{2,1,0:T(8,128)(2,1)S(1)}, u32[]{:S(2)}, u32[]{:S(2)}) collective-permute-start(bf16[4,72,2304]{2,1,0:T(8,128)(2,1)S(1)} %collective-permute-done.25.refs_2_), channel_id=1, source_target_pairs={{0,2},{2,0},{4,6},{6,4},{1,3},{3,1},{5,7},{7,5},{8,10},{10,8},{12,... | collective-permute-start | bytes 3981320 | tf_op jit(solution)/shard_map/ppermute | solution.py:111
  283.2 34.4 %collective-permute-start.41 = (bf16[256,1152]{1,0:T(8,128)(2,1)}, bf16[256,1152]{1,0:T(8,128)(2,1)}, u32[]{:S(2)}, u32[]{:S(2)}) collective-permute-start(bf16[256,1152]{1,0:T(8,128)(2,1)} %get-tuple-element.301.refs_0_), channel_id=1, source_target_pairs={{0,1},{1,0},{2,3},{3,2},{4,5},{5,4},{6,7},{7,6},{8,9},{9,8},{10,11... | collective-permute-start | bytes 1769480 | tf_op jit(solution)/shard_map/ppermute | solution.py:111
  338.8 63.8 %collective-permute-start.51 = (bf16[4,72,2304]{2,1,0:T(8,128)(2,1)S(1)}, bf16[4,72,2304]{2,1,0:T(8,128)(2,1)S(1)}, u32[]{:S(2)}, u32[]{:S(2)}) collective-permute-start(bf16[4,72,2304]{2,1,0:T(8,128)(2,1)S(1)} %copy-done.97), channel_id=1, source_target_pairs={{0,4},{2,6},{4,0},{6,2},{1,5},{3,7},{5,1},{7,3},{8,12},{10,14},{12... | collective-permute-start | bytes 3981320 | tf_op jit(solution)/shard_map/ppermute | solution.py:111
  340.9 61.7 %collective-permute-start.50 = (bf16[4,72,2304]{2,1,0:T(8,128)(2,1)}, bf16[4,72,2304]{2,1,0:T(8,128)(2,1)S(1)}, u32[]{:S(2)}, u32[]{:S(2)}) collective-permute-start(bf16[4,72,2304]{2,1,0:T(8,128)(2,1)} %collective-permute-done.46.refs_2_), channel_id=1, source_target_pairs={{0,2},{2,0},{4,6},{6,4},{1,3},{3,1},{5,7},{7,5},{8,10},{10,8},{12,... | collective-permute-start | bytes 3981320 | tf_op jit(solution)/shard_map/ppermute | solution.py:111
  343.0 44.8 %collective-permute-start.44 = (bf16[2,64,1728]{2,1,0:T(8,128)(2,1)S(1)}, bf16[2,64,1728]{2,1,0:T(8,128)(2,1)S(1)}, u32[]{:S(2)}, u32[]{:S(2)}) collective-permute-start(bf16[2,64,1728]{2,1,0:T(8,128)(2,1)S(1)} %pad_maximum_fusion.21), channel_id=1, source_target_pairs={{0,6},{2,4},{4,2},{6,0},{1,7},{3,5},{5,3},{7,1},{8,14},{10,12},{12... | collective-permute-start | bytes 1327112 | tf_op jit(solution)/shard_map/ppermute | solution.py:111
  452.9 41.0 %collective-permute-start.57 = (bf16[4,2,72,1152]{3,2,1,0:T(8,128)(2,1)}, bf16[4,2,72,1152]{3,2,1,0:T(8,128)(2,1)}, u32[]{:S(2)}, u32[]{:S(2)}) collective-permute-start(bf16[4,2,72,1152]{3,2,1,0:T(8,128)(2,1)} %get-tuple-element.343), channel_id=1, source_target_pairs={{0,4},{2,6},{4,0},{6,2},{1,5},{3,7},{5,1},{7,3},{8,12},{10,14},{12... | collective-permute-start | bytes 3981320 | tf_op jit(solution)/shard_map/ppermute | solution.py:111
  454.0 38.7 %collective-permute-start.55 = (bf16[256,1152]{1,0:T(8,128)(2,1)}, bf16[256,1152]{1,0:T(8,128)(2,1)S(1)}, u32[]{:S(2)}, u32[]{:S(2)}) collective-permute-start(bf16[256,1152]{1,0:T(8,128)(2,1)} %get-tuple-element.327), channel_id=1, source_target_pairs={{0,1},{1,0},{2,3},{3,2},{4,5},{5,4},{6,7},{7,6},{8,9},{9,8},{10,11... | collective-permute-start | bytes 1769480 | tf_op jit(solution)/shard_map/ppermute | solution.py:111
  487.8 39.6 %collective-permute-start.65 = (bf16[4,2,72,1152]{3,2,1,0:T(8,128)(2,1)S(1)}, bf16[4,2,72,1152]{3,2,1,0:T(8,128)(2,1)S(1)}, u32[]{:S(2)}, u32[]{:S(2)}) collective-permute-start(bf16[4,2,72,1152]{3,2,1,0:T(8,128)(2,1)S(1)} %get-tuple-element.358), channel_id=1, source_target_pairs={{0,2},{2,0},{4,6},{6,4},{1,3},{3,1},{5,7},{7,5},{8,10},{10,8},{12,... | collective-permute-start | bytes 3981320 | tf_op jit(solution)/shard_map/ppermute | solution.py:111
  490.9 36.9 %collective-permute-start.64 = (bf16[4,2,72,1152]{3,2,1,0:T(8,128)(2,1)S(1)}, bf16[4,2,72,1152]{3,2,1,0:T(8,128)(2,1)S(1)}, u32[]{:S(2)}, u32[]{:S(2)}) collective-permute-start(bf16[4,2,72,1152]{3,2,1,0:T(8,128)(2,1)S(1)} %get-tuple-element.356), channel_id=1, source_target_pairs={{0,4},{2,6},{4,0},{6,2},{1,5},{3,7},{5,1},{7,3},{8,12},{10,14},{12... | collective-permute-start | bytes 3981320 | tf_op jit(solution)/shard_map/ppermute | solution.py:111
  497.0 33.9 %collective-permute-start.60 = (bf16[256,1152]{1,0:T(8,128)(2,1)S(1)}, bf16[256,1152]{1,0:T(8,128)(2,1)S(1)}, u32[]{:S(2)}, u32[]{:S(2)}) collective-permute-start(bf16[256,1152]{1,0:T(8,128)(2,1)S(1)} %get-tuple-element.352.refs_0_), channel_id=1, source_target_pairs={{0,1},{1,0},{2,3},{3,2},{4,5},{5,4},{6,7},{7,6},{8,9},{9,8},{10,11... | collective-permute-start | bytes 1769480 | tf_op jit(solution)/shard_map/ppermute | solution.py:111
  499.3 42.3 %collective-permute-start.67 = (bf16[4,72,1152]{2,1,0:T(8,128)(2,1)S(1)}, bf16[4,72,1152]{2,1,0:T(8,128)(2,1)S(1)}, u32[]{:S(2)}, u32[]{:S(2)}) collective-permute-start(bf16[4,72,1152]{2,1,0:T(8,128)(2,1)S(1)} %get-tuple-element.360), channel_id=1, source_target_pairs={{0,2},{2,0},{4,6},{6,4},{1,3},{3,1},{5,7},{7,5},{8,10},{10,8},{12,... | collective-permute-start | bytes 1990664 | tf_op jit(solution)/shard_map/ppermute | solution.py:111
  499.5 43.1 %collective-permute-start.66 = (bf16[4,72,1152]{2,1,0:T(8,128)(2,1)S(1)}, bf16[4,72,1152]{2,1,0:T(8,128)(2,1)S(1)}, u32[]{:S(2)}, u32[]{:S(2)}) collective-permute-start(bf16[4,72,1152]{2,1,0:T(8,128)(2,1)S(1)} %get-tuple-element.359), channel_id=1, source_target_pairs={{0,4},{2,6},{4,0},{6,2},{1,5},{3,7},{5,1},{7,3},{8,12},{10,14},{12... | collective-permute-start | bytes 1990664 | tf_op jit(solution)/shard_map/ppermute | solution.py:111
  551.4 45.3 %collective-permute-start.73 = (bf16[2,2,72,1152]{3,2,0,1:T(8,128)(2,1)S(1)}, bf16[2,2,72,1152]{3,2,0,1:T(8,128)(2,1)S(1)}, u32[]{:S(2)}, u32[]{:S(2)}) collective-permute-start(bf16[2,2,72,1152]{3,2,0,1:T(8,128)(2,1)S(1)} %fusion.6), channel_id=1, source_target_pairs={{0,8},{8,0},{16,24},{24,16},{1,9},{9,1},{17,25},{25,17},{2,10},{10... | collective-permute-start | bytes 1990664 | tf_op jit(solution)/shard_map/ppermute | solution.py:111
  613.6 50.5 %collective-permute-start.78 = (bf16[4,2,72,1152]{3,2,1,0:T(8,128)(2,1)}, bf16[4,2,72,1152]{3,2,1,0:T(8,128)(2,1)}, u32[]{:S(2)}, u32[]{:S(2)}) collective-permute-start(bf16[4,2,72,1152]{3,2,1,0:T(8,128)(2,1)} %get-tuple-element.390), channel_id=1, source_target_pairs={{0,4},{2,6},{4,0},{6,2},{1,5},{3,7},{5,1},{7,3},{8,12},{10,14},{12... | collective-permute-start | bytes 3981320 | tf_op jit(solution)/shard_map/ppermute | solution.py:111
  645.8 43.9 %collective-permute-start.80 = (bf16[4,2,72,1152]{3,2,1,0:T(8,128)(2,1)S(1)}, bf16[4,2,72,1152]{3,2,1,0:T(8,128)(2,1)S(1)}, u32[]{:S(2)}, u32[]{:S(2)}) collective-permute-start(bf16[4,2,72,1152]{3,2,1,0:T(8,128)(2,1)S(1)} %get-tuple-element.400), channel_id=1, source_target_pairs={{0,4},{2,6},{4,0},{6,2},{1,5},{3,7},{5,1},{7,3},{8,12},{10,14},{12... | collective-permute-start | bytes 3981320 | tf_op jit(solution)/shard_map/ppermute | solution.py:111
  653.5 42.6 %collective-permute-start.83 = (bf16[4,2,72,1152]{3,2,1,0:T(8,128)(2,1)S(1)}, bf16[4,2,72,1152]{3,2,1,0:T(8,128)(2,1)S(1)}, u32[]{:S(2)}, u32[]{:S(2)}) collective-permute-start(bf16[4,2,72,1152]{3,2,1,0:T(8,128)(2,1)S(1)} %get-tuple-element.410), channel_id=1, source_target_pairs={{0,2},{2,0},{4,6},{6,4},{1,3},{3,1},{5,7},{7,5},{8,10},{10,8},{12,... | collective-permute-start | bytes 3981320 | tf_op jit(solution)/shard_map/ppermute | solution.py:111
  669.6 33.2 %collective-permute-start.84 = (bf16[4,72,1152]{2,1,0:T(8,128)(2,1)S(1)}, bf16[4,72,1152]{2,1,0:T(8,128)(2,1)S(1)}, u32[]{:S(2)}, u32[]{:S(2)}) collective-permute-start(bf16[4,72,1152]{2,1,0:T(8,128)(2,1)S(1)} %get-tuple-element.411), channel_id=1, source_target_pairs={{0,4},{2,6},{4,0},{6,2},{1,5},{3,7},{5,1},{7,3},{8,12},{10,14},{12... | collective-permute-start | bytes 1990664 | tf_op jit(solution)/shard_map/ppermute | solution.py:111
  696.1 42.9 %collective-permute-start.87 = (bf16[4,72,1152]{2,1,0:T(8,128)(2,1)}, bf16[4,72,1152]{2,1,0:T(8,128)(2,1)}, u32[]{:S(2)}, u32[]{:S(2)}) collective-permute-start(bf16[4,72,1152]{2,1,0:T(8,128)(2,1)} %get-tuple-element.420), channel_id=1, source_target_pairs={{0,2},{2,0},{4,6},{6,4},{1,3},{3,1},{5,7},{7,5},{8,10},{10,8},{12,... | collective-permute-start | bytes 1990664 | tf_op jit(solution)/shard_map/ppermute | solution.py:111
  697.4 66.5 %collective-permute-start.95 = (bf16[4,2,72,1152]{3,2,1,0:T(8,128)(2,1)}, bf16[4,2,72,1152]{3,2,1,0:T(8,128)(2,1)}, u32[]{:S(2)}, u32[]{:S(2)}) collective-permute-start(bf16[4,2,72,1152]{3,2,1,0:T(8,128)(2,1)} %get-tuple-element.440), channel_id=1, source_target_pairs={{0,4},{2,6},{4,0},{6,2},{1,5},{3,7},{5,1},{7,3},{8,12},{10,14},{12... | collective-permute-start | bytes 3981320 | tf_op jit(solution)/shard_map/ppermute | solution.py:111
  702.8 43.4 %collective-permute-start.102 = (bf16[4,72,1152]{2,1,0:T(8,128)(2,1)}, bf16[4,72,1152]{2,1,0:T(8,128)(2,1)}, u32[]{:S(2)}, u32[]{:S(2)}) collective-permute-start(bf16[4,72,1152]{2,1,0:T(8,128)(2,1)} %get-tuple-element.451), channel_id=1, source_target_pairs={{0,4},{2,6},{4,0},{6,2},{1,5},{3,7},{5,1},{7,3},{8,12},{10,14},{12... | collective-permute-start | bytes 1990664 | tf_op jit(solution)/shard_map/ppermute | solution.py:111
  714.6 62.9 %collective-permute-start.100 = (bf16[4,2,72,1152]{3,2,1,0:T(8,128)(2,1)}, bf16[4,2,72,1152]{3,2,1,0:T(8,128)(2,1)}, u32[]{:S(2)}, u32[]{:S(2)}) collective-permute-start(bf16[4,2,72,1152]{3,2,1,0:T(8,128)(2,1)} %get-tuple-element.448), channel_id=1, source_target_pairs={{0,2},{2,0},{4,6},{6,4},{1,3},{3,1},{5,7},{7,5},{8,10},{10,8},{12,... | collective-permute-start | bytes 3981320 | tf_op jit(solution)/shard_map/ppermute | solution.py:111
  762.7 41.5 %collective-permute-start.106 = (bf16[2,2,72,1152]{3,2,0,1:T(8,128)(2,1)}, bf16[2,2,72,1152]{3,2,0,1:T(8,128)(2,1)}, u32[]{:S(2)}, u32[]{:S(2)}) collective-permute-start(bf16[2,2,72,1152]{3,2,0,1:T(8,128)(2,1)} %fusion.19), channel_id=1, source_target_pairs={{0,8},{8,0},{16,24},{24,16},{1,9},{9,1},{17,25},{25,17},{2,10},{10... | collective-permute-start | bytes 1990664 | tf_op jit(solution)/shard_map/ppermute | solution.py:111
  762.8 65.4 %collective-permute-start.89 = (f32[256,1152]{1,0:T(8,128)}, f32[256,1152]{1,0:T(8,128)}, u32[]{:S(2)}, u32[]{:S(2)}) collective-permute-start(f32[256,1152]{1,0:T(8,128)} %get-tuple-element.425), channel_id=1, source_target_pairs={{0,1},{1,0},{2,3},{3,2},{4,5},{5,4},{6,7},{7,6},{8,9},{9,8},{10,11... | collective-permute-start | bytes 3538952 | tf_op jit(solution)/shard_map/ppermute | solution.py:111
  766.6 57.4 %collective-permute-start.97 = (bf16[4,72,1152]{2,1,0:T(8,128)(2,1)}, bf16[4,72,1152]{2,1,0:T(8,128)(2,1)}, u32[]{:S(2)}, u32[]{:S(2)}) collective-permute-start(bf16[4,72,1152]{2,1,0:T(8,128)(2,1)} %get-tuple-element.442), channel_id=1, source_target_pairs={{0,2},{2,0},{4,6},{6,4},{1,3},{3,1},{5,7},{7,5},{8,10},{10,8},{12,... | collective-permute-start | bytes 1990664 | tf_op jit(solution)/shard_map/ppermute | solution.py:111
  776.3 55.2 %collective-permute-start.96 = (bf16[4,2,72,1152]{3,2,1,0:T(8,128)(2,1)}, bf16[4,2,72,1152]{3,2,1,0:T(8,128)(2,1)}, u32[]{:S(2)}, u32[]{:S(2)}) collective-permute-start(bf16[4,2,72,1152]{3,2,1,0:T(8,128)(2,1)} %get-tuple-element.441), channel_id=1, source_target_pairs={{0,4},{2,6},{4,0},{6,2},{1,5},{3,7},{5,1},{7,3},{8,12},{10,14},{12... | collective-permute-start | bytes 3981320 | tf_op jit(solution)/shard_map/ppermute | solution.py:111
  (301 other events, 3535.9 us)

commit v3 on v2

--- a/solution.py
+++ b/solution.py
@@ -11,6 +11,16 @@
 LANES = 128
 EPSILON = 1e-06
 MIB = 1024 * 1024
+SCALE = 1.07
+SCALE_B = 1.11
+TRIP = 1.41
+ADD = 4.0
+SWAP = 6.0
+RATE = 0.0398
+SEND = 0.5
+DEPTH = 2
+HOLD = True
+HALF = 0.0
 f32 = jnp.float32
 bf16 = jnp.bfloat16
 LIGHT = pl.CostEstimate(flops=1, bytes_accessed=1, transcendentals=0)
@@ -18,9 +28,6 @@
 
 
 class Flow:
-    RATE = 0.0435
-    SEND = 1.5
-
     def __init__(self):
         self.now = 0.0
         self.busy = {}
@@ -30,11 +37,12 @@
         self.latest = []
         self.last = {}
         self.depth = 1
+        self.scale = SCALE
         self.held = False
 
     def post(self, value, axis, bit, then, rank, weight=1.0):
         line = (axis, bit) if axis == "seq" else (axis, 0)
-        size = value.size * value.dtype.itemsize * weight / (self.RATE * 1e6)
+        size = value.size * value.dtype.itemsize * weight / (RATE * 1e6)
         queue = self.queues.setdefault(line, [])
         queue.append((value, axis, bit, size, then, rank))
         queue.sort(key=lambda entry: entry[-1])
@@ -49,7 +57,7 @@
                 ahead = self.last.get(line, []) + (self.latest if axis == "seq" else [])
                 if ahead:
                     value = lax.optimization_barrier((value, ahead))[0]
-                self.now += self.SEND
+                self.now += SEND
                 start = max([self.now] + [entry[0] for entry in busy])
                 busy.append((start + duration, pxor(value, axis, 1 << bit), then))
 
@@ -91,7 +99,7 @@
         if self.fresh:
             value = lax.optimization_barrier((value, self.fresh))[0]
             self.fresh = []
-        self.now += cost
+        self.now += cost * self.scale
         return value
 
     def note(self, *arrays):
@@ -164,22 +172,22 @@
         self.rank = rank
         self.flow, self.index, self.cuts, self.cost = flow, (dp_index, seq_index), cuts, cost
         self.count, self.outer = bits_of(lax.axis_size("seq")), bits_of(lax.axis_size("dp"))
+        self.trees = [{}, {}]
         self.blocks = {}
-        self.trees = [{}, {}]
-        self.along_dp(0, self.outer, halves)
-
-    def along_dp(self, rel, below, block):
-        self.blocks[rel] = block
+        self.along_dp((0, 1), 0, self.outer, jnp.stack(halves))
+
+    def along_dp(self, which, rel, below, block):
+        blocks = self.blocks.setdefault(which, {})
+        blocks[rel] = block
         for bit in reversed(range(below)):
-            self.flow.post(
-                block, "dp", bit, partial(self.along_dp, rel | 1 << bit, bit), self.rank, 1.0 + bit
-            )
-        if len(self.blocks) == 1 << self.outer:
-            ordered = [self.blocks[r] for r in range(1 << self.outer)]
-            self.flow.now += 2.0
-            for which in range(2):
-                stacked = jnp.stack([block[which] for block in ordered])
-                self.along_seq(which, 0, 0, stacked)
+            then = partial(self.along_dp, which, rel | 1 << bit, bit)
+            self.flow.post(block, "dp", bit, then, self.rank, 1.0 + bit)
+        if len(blocks) == 1 << self.outer:
+            ordered = [blocks[r] for r in range(1 << self.outer)]
+            for half in which:
+                self.flow.now += HALF
+                part = ordered if len(which) == 1 else [block[half] for block in ordered]
+                self.along_seq(half, 0, 0, jnp.stack(part))
 
     def along_seq(self, which, rel, first, block):
         self.trees[which][rel] = block
@@ -241,7 +249,7 @@
                 both = [v.reshape((2,) + (2,) * self.outer + v.shape[2:]) for v in both]
                 self.along_dp(0, both)
             return
-        self.flow.now += 2.0
+        self.flow.now += ADD
         bit = order[0]
         kept, away = self.split(parts, "seq", bit, 1 + left.index(bit))
         rest = [b for b in left if b != bit]
@@ -251,7 +259,7 @@
         if bit == self.outer:
             self.total = add_up(parts)
             return
-        self.flow.now += 2.0
+        self.flow.now += ADD
         kept, away = self.split(parts, "dp", bit, self.outer - bit)
         self.flow.post(away, "dp", bit, lambda got: self.along_dp(bit + 1, [kept, got]), self.rank, 1.0 + bit)
 
@@ -576,6 +584,27 @@
     )
 
 
+def mlp_up(normed, up_a, up_b, biases, row):
+    rows, cols = 2 * normed[0].shape[0], up_a.shape[1]
+
+    def kernel(ins, fetch, outs, scratch):
+        tokens = both(ins[0], ins[1])
+        for i in range(2):
+            bias = ins[2][row + i : row + i + 1, :]
+            pre = jnp.dot(tokens, fetch(i)[...], preferred_element_type=f32) + bias
+            outs[i][...] = pre
+            outs[2 + i][...] = (0.5 * pre * (1.0 + gelu_parts(pre))).astype(bf16)
+
+    return call(
+        kernel,
+        "mlp_up",
+        [*normed, biases],
+        [up_a, up_b],
+        [((rows, cols), f32)] * 2 + [((rows, cols), bf16)] * 2,
+        limit=32,
+    )
+
+
 def mlp_backward(grad, pre, up, down, so_far):
     patches, model = grad[0].shape
     rows, cols = pre.shape
@@ -700,7 +729,7 @@
 
 
 def with_other(flow, own):
-    flow.now += 5.0
+    flow.now += SWAP
     return own, swap(own)
 
 
@@ -739,42 +768,62 @@
     vo = vo.reshape(2, patches, -1)
     if temporal:
         period = patches // lax.axis_size("seq")
-        qkv = dispatch_in(flow, [qk, vo[:, :, :width]], 17.0, False)
+        qkv = dispatch_in(flow, [qk, vo[:, :, :width]], 17.0 * TRIP, False)
         heads = (flow.step(3.5, qkv), qkv, 2 * width)
         attended = attend(*heads, width, 0, period)
-        attended = collect_in(flow, attended, ((0, period, 0, width, width, 0),), 11.0, False)[0]
+        attended = collect_in(flow, attended, ((0, period, 0, width, width, 0),), 11.0 * TRIP, False)[0]
     else:
         heads = (flow.step(3.5, qk), vo, 0)
         attended = attend(*heads, width, width, None).reshape(2 * patches, -1)
     own, other = flow.ran(project_back([(flow.step(2.5, attended), w_vo)], f32, "project_out"))
     other = swap(other)
-    flow.now += 5.0
+    flow.now += SWAP
     branch, x_mid, normed_two = flow.ran(
         residual(x, flow.step(2.0, own), other, biases, base + 2, mods, base + 2, (base + 3, base + 4))
     )
     normed_two = with_other(flow, normed_two)
-    w_up_a, w_up_b, w_down_a, w_down_b = mlp_unit()
-    tokens = (flow.step(11.0, normed_two[0]), normed_two[1])
-    pre_a, pre_b, hidden_a, hidden_b, own, other = flow.ran(
-        mlp_forward(tokens, w_up_a, w_up_b, w_down_a, w_down_b, biases, base + 3, f32)
-    )
-    other = swap(other)
-    flow.now += 5.0
-    mlp, x_next, after = flow.ran(
-        residual(x_mid, flow.step(2.0, own), other, biases, base + 5, mods, base + 5, following)
-    )
+    if following is not None:
+        w_up_a, w_down_a, w_up_b, w_down_b = mlp_unit()
+        tokens = (flow.step(11.0, normed_two[0]), normed_two[1])
+        pre_a, pre_b, hidden_a, hidden_b, own, other = flow.ran(
+            mlp_forward(tokens, w_up_a, w_up_b, w_down_a, w_down_b, biases, base + 3, f32)
+        )
+        other = swap(other)
+        flow.now += SWAP
+        mlp, x_next, after = flow.ran(
+            residual(x_mid, flow.step(2.0, own), other, biases, base + 5, mods, base + 5, following)
+        )
+        finish = None
+        downs = (w_down_a, w_down_b)
+    else:
+        w_up_a, w_down_a, w_up_b, w_down_b = mlp_unit()
+        tokens = (flow.step(8.0, normed_two[0]), normed_two[1])
+        pre_a, pre_b, hidden_a, hidden_b = flow.ran(mlp_up(tokens, w_up_a, w_up_b, biases, base + 3))
+        downs = (w_down_a, w_down_b)
+        mlp = x_next = after = None
+
+        def finish(down_a, down_b):
+            first = flow.step(4.0, hidden_a)
+            own, other = flow.ran(project_back([(first, down_a), (hidden_b, down_b)], f32, "project_down"))
+            other = swap(other)
+
+            def rest():
+                return flow.ran(residual(x_mid, flow.step(2.0, own), other, biases, base + 5, mods, base + 5, None))
+
+            return rest
+
     saved = (x, normed_one, heads, attended, branch, x_mid, normed_two, pre_a, pre_b, hidden_a, hidden_b, mlp)
-    weights = (w_qk, w_vo, w_up_a, w_up_b, w_down_a, w_down_b)
-    return x_next, after, saved, weights
-
-
-def layer_backward(flow, g, grad_mlp, mods, layer, weights, saved, temporal, below):
-    w_qk, w_vo, w_up_a, w_up_b, w_down_a, w_down_b = weights
+    weights = (w_qk, w_vo, w_up_a, w_up_b, downs)
+    return x_next, after, saved, weights, finish
+
+
+def layer_backward(flow, g, grad_mlp, mods, layer, weights, saved, temporal, below, finish):
+    w_qk, w_vo, w_up_a, w_up_b, downs = weights
     x, normed_one, heads, attended, branch, x_mid, normed_two, pre_a, pre_b, hidden_a, hidden_b, _ = saved
     patches = x.shape[0]
     width = w_qk.shape[1] // 2
     base = 6 * layer
-    done = [Scatter(flow, 10 - 4 * layer - unit) for unit in range(3)]
+    done = [Scatter(flow, 20 - 4 * layer - unit) for unit in range(3)]
     bits = (bits_of(lax.axis_size("seq")) - 1, 0)
 
     def reduce_half(unit, which, pairs, name):
@@ -788,6 +837,7 @@
     grad_mlp_rows = joined(grad_mlp)
     reduce_half(2, 0, [(grad_mlp_rows, hidden_a)], "down_grad")
     reduce_half(2, 1, [(grad_mlp_rows, hidden_b)], "down_grad")
+    w_down_a, w_down_b = downs
     normed_rows = joined(normed_two)
     tokens = (flow.step(7.0, grad_mlp[0]), grad_mlp[1])
     grad_pre_a, sums_a, so_far = flow.ran(mlp_backward(tokens, pre_a, w_up_a, w_down_a, None))
@@ -804,18 +854,23 @@
     grad_branch = (flow.step(2.5, grad_branch), other_branch)
     grad_att, sum_branch = flow.ran(grad_heads(grad_branch, w_vo))
     grad_att = grad_att.reshape(2, patches, -1)
+    rest = finished = None
+    if finish is not None:
+        rest = finish(w_down_a, w_down_b)
     if temporal:
         period = patches // lax.axis_size("seq")
-        grad_att = dispatch_in(flow, [grad_att[:, :, width:]], 10.0, True)
+        grad_att = dispatch_in(flow, [grad_att[:, :, width:]], 10.0 * TRIP, HOLD)
         grad_qkv, sums_pair = flow.ran(attend_grad(*heads, flow.step(10.5, grad_att), 0, width, period))
         cuts = ((0, period, 0, 2 * width, 0, 0), (0, period, 2 * width, width, 0, width))
-        grad_qk, grad_v = collect_in(flow, grad_qkv, cuts, 18.0, True)
+        grad_qk, grad_v = collect_in(flow, grad_qkv, cuts, 18.0 * TRIP, HOLD)
     else:
         grad_qk, grad_v, sums_pair = flow.ran(
             attend_grad(*heads, flow.step(10.5, grad_att), width, width, None)
         )
         grad_qk = grad_qk.reshape(2 * patches, -1)
         grad_v = grad_v.reshape(2 * patches, -1)
+    if rest is not None:
+        finished = rest()
     own, other = flow.ran(
         project_back([(flow.step(5.0, grad_qk), w_qk), (grad_v, w_vo)], bf16, "grad_normed")
     )
@@ -839,7 +894,7 @@
         sums_b[0],
         sums_a[1],
     ]
-    return g_below, grad_below, mod_sums, sums_one[2], bias_sums, done
+    return g_below, grad_below, mod_sums, sums_one[2], bias_sums, done, finished
 
 
 def shards(
@@ -883,14 +938,13 @@
             extra = jnp.zeros((8 * 2 * width,), bf16).at[: packed.shape[0]].set(packed).reshape(8, -1)
             first = jnp.concatenate([first, extra])
             second = jnp.concatenate([second, jnp.zeros_like(extra)])
-        return jnp.stack([first, second])
+        return first, second
 
     def mlp_unit(layer):
         down = output_weight[layer].T
         up = hidden_weight[layer]
-        return jnp.stack(
-            [jnp.concatenate([up[:, part], down[:, part]], axis=1) for part in (slice(0, half), slice(half, None))]
-        )
+        parts = (slice(0, half), slice(half, None))
+        return [[jnp.concatenate([up[:, part], down[:, part]], axis=1) for part in parts]]
 
     flow = Flow()
     flow.now = 8.0
@@ -900,7 +954,12 @@
         first_cuts = (whole, (rows, 8, 0, 2 * width, 0, 0)) if layer == 0 else (whole,)
         attention = Gather(flow, 2 * layer, attention_unit(layer), dp_index, seq_index, (first_cuts, (whole,)), 2.0)
         pair_cuts = ((0, rows, 0, half, 0, 0), (0, rows, half, half, 0, 0))
-        mlp = Gather(flow, 2 * layer + 1, mlp_unit(layer), dp_index, seq_index, (pair_cuts, pair_cuts), 3.5)
+        mlp = mlp_unit(layer)
+        mlp_cuts = (pair_cuts, pair_cuts) if len(mlp) == 1 else ((whole,), (whole,))
+        mlp = [
+            Gather(flow, 2 * layer + 1 + i, halves, dp_index, seq_index, mlp_cuts, 3.5 if len(mlp) == 1 else 2.0)
+            for i, halves in enumerate(mlp)
+        ]
         gathers.append((attention, mlp))
 
     act_cond, silu_back = jax.vjp(jax.nn.silu, conditioning)
@@ -935,8 +994,8 @@
         return first[0], second[0]
 
     def mlp_weights(layer):
-        first, second = gathers[layer][1].result()
-        return first[0], second[0], first[1], second[1]
+        first, second = gathers[layer][1][0].result()
+        return first + second
 
     x = take(tokens, 0, core).reshape(patches, model).astype(f32)
     after = norm_forward(x, mods, 0, 1)
@@ -944,7 +1003,7 @@
     for layer in range(layers):
         following = (6 * layer + 6, 6 * layer + 7) if layer + 1 < layers else None
         pending = (partial(attention_weights, layer), partial(mlp_weights, layer))
-        x, after, saved, layer_weights = layer_forward(
+        x, after, saved, layer_weights, finish = layer_forward(
             flow, x, after, mods, layer, pending, lambda: found["biases"], layer == 1, following
         )
         kept.append(saved)
@@ -955,18 +1014,21 @@
         pair = jnp.stack([jnp.where(core == 0, own, other), jnp.where(core == 0, other, own)])
         return pair.reshape((2, 1) + own.shape)
 
-    activations = to_both(after)
     g = take(cotangent, 0, core).reshape(patches, model).astype(f32)
     grad_mlp = (mods[6 * layers - 1] * g).astype(bf16)
     grad_gates = [None] * layers
-    grad_gates[-1] = jnp.sum(g * kept[-1][-1], axis=0)
+    top = g
     mod_grads, bias_grads, done = [None] * layers, [None] * layers, [None] * layers
-    flow.depth = 2
+    flow.depth, flow.scale = DEPTH, SCALE_B
     for layer in reversed(range(layers)):
         below = kept[layer - 1][-1] if layer else None
-        g, grad_mlp, mod_sums, grad_gate, bias_grads[layer], done[layer] = layer_backward(
-            flow, g, grad_mlp, mods, layer, weights[layer], kept[layer], layer == 1, below
+        g, grad_mlp, mod_sums, grad_gate, bias_grads[layer], done[layer], finished = layer_backward(
+            flow, g, grad_mlp, mods, layer, weights[layer], kept[layer], layer == 1, below, finish
         )
+        if finished is not None:
+            grad_gates[layer] = jnp.sum(top * finished[0], axis=0)
+            activations = to_both(finished[2])
+            finish = None
         mod_grads[layer] = jnp.concatenate(mod_sums + [grad_gates[layer]])
         if layer:
             grad_gates[layer - 1] = grad_gate

time: 912 us -> 895 us (0.981)
  waiting for transfers between devices: 430 us -> 408 us
  other arithmetic: 72.6 us -> 84.9 us
  local copies, waits for them, and re-layouts: 101 us -> 89.6 us
    ppermute x112, waiting for transfers between devices: 430 us -> 408 us  [pxor(): return lax.ppermute(value, axis, [(i, i ^ flip) for i in range(size)])]
    unnamed x470 -> x458, local copies, waits for them, and re-layouts: 69.8 us -> 58.4 us
    pallas_call x23 -> x24, Pallas kernels: 93.9 us -> 93 us  [call(): pl.pallas_call(body, out_shape=[jax.ShapeDtypeStruct(shape, dtype) for sh...]
  transfers between devices with their start and end apart: 112 -> 112, of which waited for: 50 -> 45; matrix products, arithmetic and copies ran while one was open for 11% -> 13% of each run, Pallas kernels for 19% -> 21%
where the time goes in v3:
time: 895 us; the launch traced here: 884 us
  waiting for transfers between devices  408 us (46%)
  Pallas kernels  200 us (22%)
  starting transfers between devices  96.1 us (11%)
  local copies, waits for them, and re-layouts  89.6 us (10%)
  other arithmetic  84.9 us (9%)
    ppermute x112, waiting for transfers between devices, pxor(): return lax.ppermute(value, axis, [(i, i ^ flip) for i in range(size)])  408 us
    ppermute x112, starting transfers between devices, pxor(): return lax.ppermute(value, axis, [(i, i ^ flip) for i in range(size)])  96.1 us
    pallas_call x24, Pallas kernels, call(): pl.pallas_call(body, out_shape=[jax.ShapeDtypeStruct(shape, dtype) for sh...  93 us
    pallas_call x12, Pallas kernels, weight_grad(): pl.pallas_call(body, out_shape=[jax.ShapeDtypeStruct(shape, bf16)] * 2, i...  61.1 us
    unnamed x458, local copies, waits for them, and re-layouts  58.4 us
    pallas_call x2, Pallas kernels, attend_grad(): pl.pallas_call(partial(attend_grad_kernel, period, lead, skip), grid=(blo...  21.1 us
    pallas_call x10, Pallas kernels, place(): pl.pallas_call(partial(place_kernel, cuts), grid_spec=pltpu.PrefetchScala...  18.1 us
  transfers between devices with their start and end apart: 112, of which 45 were waited for; matrix products, arithmetic and copies ran while one was open for 13% of the time, Pallas kernels for 21%

profile of v3, /device:TPU:0, one launch (start us, length us, event | category | flops | bytes accessed | tf_op | source)
XLA Modules:
  0.0 884.0 jit_solution(313188020027039638)
XLA Ops:
  30.3 8.0 collective-permute-done.6
  38.4 9.0 %collective-permute-done.7 = bf16[2,80,1152]{2,1,0:T(8,128)(2,1)S(1)} collective-permute-done((bf16[2,80,1152]{2,1,0:T(8,128)(2,1)}, bf16[2,80,1152]{2,1,0:T(8,128)(2,1)S(1)}, u32[]{:S(2)}, u32[]{:S(2)}) %collective-permute-start.7) | collective-permute-done | bytes 368672 | tf_op jit(solution)/shard_map/ppermute | solution.py:119
  56.7 10.7 %collective-permute-done.3 = f32[13824]{0:T(1024)S(1)} collective-permute-done((f32[13824]{0:T(1024)S(1)}, f32[13824]{0:T(1024)S(1)}, u32[]{:S(2)}, u32[]{:S(2)}) %collective-permute-start.3) | collective-permute-done | bytes 55328 | tf_op jit(solution)/shard_map/ppermute | solution.py:119
  68.0 14.1 %collective-permute-done.10 = bf16[2,72,2304]{2,1,0:T(8,128)(2,1)S(1)} collective-permute-done((bf16[2,72,2304]{2,1,0:T(8,128)(2,1)S(1)}, bf16[2,72,2304]{2,1,0:T(8,128)(2,1)S(1)}, u32[]{:S(2)}, u32[]{:S(2)}) %collective-permute-start.10) | collective-permute-done | bytes 663584 | tf_op jit(solution)/shard_map/ppermute | solution.py:119
  85.4 12.8 %collective-permute-done.13 = bf16[2,72,2304]{2,1,0:T(8,128)(2,1)S(1)} collective-permute-done((bf16[2,72,2304]{2,1,0:T(8,128)(2,1)S(1)}, bf16[2,72,2304]{2,1,0:T(8,128)(2,1)S(1)}, u32[]{:S(2)}, u32[]{:S(2)}) %collective-permute-start.13) | collective-permute-done | bytes 663584 | tf_op jit(solution)/shard_map/ppermute | solution.py:119
  103.0 10.3 %collective-permute-done.17 = bf16[2,72,2304]{2,1,0:T(8,128)(2,1)S(1)} collective-permute-done((bf16[2,72,2304]{2,1,0:T(8,128)(2,1)S(1)}, bf16[2,72,2304]{2,1,0:T(8,128)(2,1)S(1)}, u32[]{:S(2)}, u32[]{:S(2)}) %collective-permute-start.17) | collective-permute-done | bytes 663584 | tf_op jit(solution)/shard_map/ppermute | solution.py:119
  156.2 8.1 collective-permute-done.20
  164.9 8.8 collective-permute-done.23
  173.8 11.9 %collective-permute-done.24.refs_1_ = bf16[4,72,2304]{2,1,0:T(8,128)(2,1)S(1)} collective-permute-done((bf16[4,72,2304]{2,1,0:T(8,128)(2,1)S(1)}, bf16[4,72,2304]{2,1,0:T(8,128)(2,1)S(1)}, u32[]{:S(2)}, u32[]{:S(2)}) %collective-permute-start.24) | collective-permute-done | bytes 1327136 | tf_op jit(solution)/shard_map/ppermute | solution.py:119
  189.4 14.8 %collective-permute-done.26 = bf16[2,72,2304]{2,1,0:T(8,128)(2,1)S(1)} collective-permute-done((bf16[2,72,2304]{2,1,0:T(8,128)(2,1)S(1)}, bf16[2,72,2304]{2,1,0:T(8,128)(2,1)S(1)}, u32[]{:S(2)}, u32[]{:S(2)}) %collective-permute-start.26) | collective-permute-done | bytes 663584 | tf_op jit(solution)/shard_map/ppermute | solution.py:119
  205.2 15.8 %collective-permute-done.28 = bf16[2,72,2304]{2,1,0:T(8,128)(2,1)S(1)} collective-permute-done((bf16[2,72,2304]{2,1,0:T(8,128)(2,1)S(1)}, bf16[2,72,2304]{2,1,0:T(8,128)(2,1)S(1)}, u32[]{:S(2)}, u32[]{:S(2)}) %collective-permute-start.28) | collective-permute-done | bytes 663584 | tf_op jit(solution)/shard_map/ppermute | solution.py:119
  222.4 14.9 %collective-permute-done.32.refs_2_ = bf16[4,72,1152]{2,1,0:T(8,128)(2,1)S(1)} collective-permute-done((bf16[4,72,1152]{2,1,0:T(8,128)(2,1)S(1)}, bf16[4,72,1152]{2,1,0:T(8,128)(2,1)S(1)}, u32[]{:S(2)}, u32[]{:S(2)}) %collective-permute-start.32) | collective-permute-done | bytes 663584 | tf_op jit(solution)/shard_map/ppermute | solution.py:119
  238.7 13.6 %collective-permute-done.35.refs_2_ = bf16[4,72,1152]{2,1,0:T(8,128)(2,1)S(1)} collective-permute-done((bf16[4,72,1152]{2,1,0:T(8,128)(2,1)S(1)}, bf16[4,72,1152]{2,1,0:T(8,128)(2,1)S(1)}, u32[]{:S(2)}, u32[]{:S(2)}) %collective-permute-start.35) | collective-permute-done | bytes 663584 | tf_op jit(solution)/shard_map/ppermute | solution.py:119
  264.4 10.6 %mlp_forward.1 = (f32[512,1152]{1,0:T(8,128)}, f32[512,1152]{1,0:T(8,128)}, bf16[512,1152]{1,0:T(8,128)(2,1)S(1)}, bf16[512,1152]{1,0:T(8,128)(2,1)S(1)}, f32[25...) custom-call(bf16[256,1152]{1,0:T(8,128)(2,1)S(1)} %get-tuple-element.282.refs_0_, ...), custom_call_target="tpu_custom_call" | custom-call | flops 1 | bytes 1 | tf_op jit(solution)/shard_map/mlp_forward/pallas_call | solution.py:473
  285.8 21.8 %collective-permute-done.40.refs_2_ = bf16[4,72,2304]{2,1,0:T(8,128)(2,1)S(1)} collective-permute-done((bf16[4,72,2304]{2,1,0:T(8,128)(2,1)S(1)}, bf16[4,72,2304]{2,1,0:T(8,128)(2,1)S(1)}, u32[]{:S(2)}, u32[]{:S(2)}) %collective-permute-start.40) | collective-permute-done | bytes 1327136 | tf_op jit(solution)/shard_map/ppermute | solution.py:119
  325.5 15.5 %collective-permute-done.46.refs_2_ = bf16[4,72,2304]{2,1,0:T(8,128)(2,1)} collective-permute-done((bf16[4,72,2304]{2,1,0:T(8,128)(2,1)}, bf16[4,72,2304]{2,1,0:T(8,128)(2,1)}, u32[]{:S(2)}, u32[]{:S(2)}) %collective-permute-start.46) | collective-permute-done | bytes 1327136 | tf_op jit(solution)/shard_map/ppermute | solution.py:119
  345.6 7.5 collective-permute-done.42
  353.1 36.6 %collective-permute-done.44 = bf16[2,64,1728]{2,1,0:T(8,128)(2,1)S(1)} collective-permute-done((bf16[2,64,1728]{2,1,0:T(8,128)(2,1)S(1)}, bf16[2,64,1728]{2,1,0:T(8,128)(2,1)S(1)}, u32[]{:S(2)}, u32[]{:S(2)}) %collective-permute-start.44) | collective-permute-done | bytes 442400 | tf_op jit(solution)/shard_map/ppermute | solution.py:119
  448.2 7.9 mlp_backward.4
  464.3 8.4 mlp_backward.5
  490.0 16.3 %collective-permute-done.59 = bf16[4,2,72,1152]{3,2,1,0:T(8,128)(2,1)S(1)} collective-permute-done((bf16[4,2,72,1152]{3,2,1,0:T(8,128)(2,1)}, bf16[4,2,72,1152]{3,2,1,0:T(8,128)(2,1)S(1)}, u32[]{:S(2)}, u32[]{:S(2)}) %collective-permute-start.59) | collective-permute-done | bytes 1327136 | tf_op jit(solution)/shard_map/ppermute | solution.py:119
  546.7 10.3 %attend_grad.2 = (bf16[2,256,1728]{2,1,0:T(8,128)(2,1)S(1)}, f32[2,2,576]{2,1,0:T(2,128)S(1)}) custom-call(bf16[2,256,1728]{2,1,0:T(8,128)(2,1)S(1)} %bitcast.446, bf16[2,256,1728]{2,1,0:T(8,128)(2,1)S(1)} %bitcast.447, bf16[2,256,576]{2,1,0:T(8,128)(2,1)S(1)} %bitcast.484), custom_call_target="tpu_custom_call" | custom-call | flops 1 | bytes 1 | tf_op jit(solution)/shard_map/attend_grad/pallas_call | solution.py:428
  562.8 7.9 collective-permute-done.72.refs_1_
  570.7 8.6 collective-permute-done.73.refs_2_
  652.7 7.3 mlp_backward.7
  693.1 10.8 %attend_grad.3 = (bf16[2,256,1152]{2,1,0:T(8,128)(2,1)S(1)}, bf16[2,256,1152]{2,1,0:T(8,128)(2,1)S(1)}, f32[2,2,576]{2,1,0:T(2,128)S(1)}) custom-call(bf16[2,256,1152]{2,1,0:T(8,128)(2,1)S(1)} %bitcast.473, bf16[2,256,1152]{2,1,0:T(8,128)(2,1)S(1)} %bitcast.475, bf16[2,256,1152]{2,1,0:T(8,128)(2,1)S(1)} %bitcast.487), custom_call_target="tpu_custom_call" | custom-call | flops 1 | bytes 1 | tf_op jit(solution)/shard_map/attend_grad/pallas_call | solution.py:428
  760.9 7.6 collective-permute-done.94
  779.6 15.5 %collective-permute-done.107 = bf16[2,72,1152]{2,1,0:T(8,128)(2,1)S(1)} collective-permute-done((bf16[2,72,1152]{2,1,0:T(8,128)(2,1)S(1)}, bf16[2,72,1152]{2,1,0:T(8,128)(2,1)S(1)}, u32[]{:S(2)}, u32[]{:S(2)}) %collective-permute-start.107) | collective-permute-done | bytes 331808 | tf_op jit(solution)/shard_map/ppermute | solution.py:119
  797.2 14.6 %collective-permute-done.101 = bf16[4,72,1152]{2,1,0:T(8,128)(2,1)S(1)} collective-permute-done((bf16[4,72,1152]{2,1,0:T(8,128)(2,1)S(1)}, bf16[4,72,1152]{2,1,0:T(8,128)(2,1)S(1)}, u32[]{:S(2)}, u32[]{:S(2)}) %collective-permute-start.101) | collective-permute-done | bytes 663584 | tf_op jit(solution)/shard_map/ppermute | solution.py:119
  832.1 13.3 %collective-permute-done.109 = bf16[2,72,1152]{2,1,0:T(8,128)(2,1)S(1)} collective-permute-done((bf16[2,72,1152]{2,1,0:T(8,128)(2,1)S(1)}, bf16[2,72,1152]{2,1,0:T(8,128)(2,1)S(1)}, u32[]{:S(2)}, u32[]{:S(2)}) %collective-permute-start.109) | collective-permute-done | bytes 331808 | tf_op jit(solution)/shard_map/ppermute | solution.py:119
  848.4 15.6 %collective-permute-done.110 = bf16[2,2,72,1152]{3,2,0,1:T(8,128)(2,1)S(1)} collective-permute-done((bf16[2,2,72,1152]{3,2,0,1:T(8,128)(2,1)S(1)}, bf16[2,2,72,1152]{3,2,0,1:T(8,128)(2,1)S(1)}, u32[]{:S(2)}, u32[]{:S(2)}) %collective-permute-start.110) | collective-permute-done | bytes 663584 | tf_op jit(solution)/shard_map/ppermute | solution.py:119
  865.5 14.6 %collective-permute-done.111 = bf16[2,72,1152]{2,1,0:T(8,128)(2,1)S(1)} collective-permute-done((bf16[2,72,1152]{2,1,0:T(8,128)(2,1)S(1)}, bf16[2,72,1152]{2,1,0:T(8,128)(2,1)S(1)}, u32[]{:S(2)}, u32[]{:S(2)}) %collective-permute-start.111) | collective-permute-done | bytes 331808 | tf_op jit(solution)/shard_map/ppermute | solution.py:119
  (934 shorter events, 476.3 us)
Async XLA Ops:
  47.6 34.6 %collective-permute-start.9 = (bf16[4,80,1152]{2,1,0:T(8,128)(2,1)S(1)}, bf16[4,80,1152]{2,1,0:T(8,128)(2,1)S(1)}, u32[]{:S(2)}, u32[]{:S(2)}) collective-permute-start(bf16[4,80,1152]{2,1,0:T(8,128)(2,1)S(1)} %pad_maximum_fusion.13.refs_0_), channel_id=1, source_target_pairs={{0,4},{2,6},{4,0},{6,2},{1,5},{3,7},{5,1},{7,3},{8,12},{10,14},{12... | collective-permute-start | bytes 2211848 | tf_op jit(solution)/shard_map/ppermute | solution.py:119
  67.4 53.9 %collective-permute-start.4 = (f32[13824]{0:T(1024)S(1)}, f32[13824]{0:T(1024)S(1)}, u32[]{:S(2)}, u32[]{:S(2)}) collective-permute-start(f32[13824]{0:T(1024)S(1)} %add.600), channel_id=1, source_target_pairs={{0,4},{2,6},{4,0},{6,2},{1,5},{3,7},{5,1},{7,3},{8,12},{10,14},{12... | collective-permute-start | bytes 165896 | tf_op jit(solution)/shard_map/ppermute | solution.py:119
  117.5 37.1 %collective-permute-start.22 = (bf16[4,72,2304]{2,1,0:T(8,128)(2,1)}, bf16[4,72,2304]{2,1,0:T(8,128)(2,1)}, u32[]{:S(2)}, u32[]{:S(2)}) collective-permute-start(bf16[4,72,2304]{2,1,0:T(8,128)(2,1)} %pad_maximum_fusion.2.refs_0_), channel_id=1, source_target_pairs={{0,4},{2,6},{4,0},{6,2},{1,5},{3,7},{5,1},{7,3},{8,12},{10,14},{12... | collective-permute-start | bytes 3981320 | tf_op jit(solution)/shard_map/ppermute | solution.py:119
  118.6 36.2 %collective-permute-start.21 = (bf16[4,72,2304]{2,1,0:T(8,128)(2,1)}, bf16[4,72,2304]{2,1,0:T(8,128)(2,1)}, u32[]{:S(2)}, u32[]{:S(2)}) collective-permute-start(bf16[4,72,2304]{2,1,0:T(8,128)(2,1)} %pad_maximum_fusion.2.refs_0_), channel_id=1, source_target_pairs={{0,2},{2,0},{4,6},{6,4},{1,3},{3,1},{5,7},{7,5},{8,10},{10,8},{12,... | collective-permute-start | bytes 3981320 | tf_op jit(solution)/shard_map/ppermute | solution.py:119
  153.7 34.1 %collective-permute-start.18 = (f32[256,1152]{1,0:T(8,128)S(1)}, f32[256,1152]{1,0:T(8,128)S(1)}, u32[]{:S(2)}, u32[]{:S(2)}) collective-permute-start(f32[256,1152]{1,0:T(8,128)S(1)} %get-tuple-element.260), channel_id=1, source_target_pairs={{0,1},{1,0},{2,3},{3,2},{4,5},{5,4},{6,7},{7,6},{8,9},{9,8},{10,11... | collective-permute-start | bytes 3538952 | tf_op jit(solution)/shard_map/ppermute | solution.py:119
  186.1 35.2 %collective-permute-start.29 = (bf16[4,72,2304]{2,1,0:T(8,128)(2,1)}, bf16[4,72,2304]{2,1,0:T(8,128)(2,1)S(1)}, u32[]{:S(2)}, u32[]{:S(2)}) collective-permute-start(bf16[4,72,2304]{2,1,0:T(8,128)(2,1)} %collective-permute-done.21.refs_1_), channel_id=1, source_target_pairs={{0,4},{2,6},{4,0},{6,2},{1,5},{3,7},{5,1},{7,3},{8,12},{10,14},{12... | collective-permute-start | bytes 3981320 | tf_op jit(solution)/shard_map/ppermute | solution.py:119
  189.4 74.9 %collective-permute-start.33 = (bf16[256,1152]{1,0:T(8,128)(2,1)S(1)}, bf16[256,1152]{1,0:T(8,128)(2,1)S(1)}, u32[]{:S(2)}, u32[]{:S(2)}) collective-permute-start(bf16[256,1152]{1,0:T(8,128)(2,1)S(1)} %get-tuple-element.282.refs_0_), channel_id=1, source_target_pairs={{0,1},{1,0},{2,3},{3,2},{4,5},{5,4},{6,7},{7,6},{8,9},{9,8},{10,11... | collective-permute-start | bytes 1769480 | tf_op jit(solution)/shard_map/ppermute | solution.py:119
  204.3 33.3 %collective-permute-start.31 = (bf16[4,72,2304]{2,1,0:T(8,128)(2,1)S(1)}, bf16[4,72,2304]{2,1,0:T(8,128)(2,1)S(1)}, u32[]{:S(2)}, u32[]{:S(2)}) collective-permute-start(bf16[4,72,2304]{2,1,0:T(8,128)(2,1)S(1)} %collective-permute-done.25.refs_2_), channel_id=1, source_target_pairs={{0,2},{2,0},{4,6},{6,4},{1,3},{3,1},{5,7},{7,5},{8,10},{10,8},{12,... | collective-permute-start | bytes 3981320 | tf_op jit(solution)/shard_map/ppermute | solution.py:119
  284.3 34.9 %collective-permute-start.41 = (bf16[256,1152]{1,0:T(8,128)(2,1)S(1)}, bf16[256,1152]{1,0:T(8,128)(2,1)S(1)}, u32[]{:S(2)}, u32[]{:S(2)}) collective-permute-start(bf16[256,1152]{1,0:T(8,128)(2,1)S(1)} %get-tuple-element.300.refs_0_), channel_id=1, source_target_pairs={{0,1},{1,0},{2,3},{3,2},{4,5},{5,4},{6,7},{7,6},{8,9},{9,8},{10,11... | collective-permute-start | bytes 1769480 | tf_op jit(solution)/shard_map/ppermute | solution.py:119
  341.0 63.8 %collective-permute-start.51 = (bf16[4,72,2304]{2,1,0:T(8,128)(2,1)}, bf16[4,72,2304]{2,1,0:T(8,128)(2,1)S(1)}, u32[]{:S(2)}, u32[]{:S(2)}) collective-permute-start(bf16[4,72,2304]{2,1,0:T(8,128)(2,1)} %collective-permute-done.38.refs_1_), channel_id=1, source_target_pairs={{0,4},{2,6},{4,0},{6,2},{1,5},{3,7},{5,1},{7,3},{8,12},{10,14},{12... | collective-permute-start | bytes 3981320 | tf_op jit(solution)/shard_map/ppermute | solution.py:119
  343.4 62.6 %collective-permute-start.50 = (bf16[4,72,2304]{2,1,0:T(8,128)(2,1)}, bf16[4,72,2304]{2,1,0:T(8,128)(2,1)S(1)}, u32[]{:S(2)}, u32[]{:S(2)}) collective-permute-start(bf16[4,72,2304]{2,1,0:T(8,128)(2,1)} %collective-permute-done.46.refs_2_), channel_id=1, source_target_pairs={{0,2},{2,0},{4,6},{6,4},{1,3},{3,1},{5,7},{7,5},{8,10},{10,8},{12,... | collective-permute-start | bytes 3981320 | tf_op jit(solution)/shard_map/ppermute | solution.py:119
  345.4 44.3 %collective-permute-start.44 = (bf16[2,64,1728]{2,1,0:T(8,128)(2,1)S(1)}, bf16[2,64,1728]{2,1,0:T(8,128)(2,1)S(1)}, u32[]{:S(2)}, u32[]{:S(2)}) collective-permute-start(bf16[2,64,1728]{2,1,0:T(8,128)(2,1)S(1)} %pad_maximum_fusion.21), channel_id=1, source_target_pairs={{0,6},{2,4},{4,2},{6,0},{1,7},{3,5},{5,3},{7,1},{8,14},{10,12},{12... | collective-permute-start | bytes 1327112 | tf_op jit(solution)/shard_map/ppermute | solution.py:119
  445.0 41.1 %collective-permute-start.57 = (bf16[4,2,72,1152]{3,2,1,0:T(8,128)(2,1)}, bf16[4,2,72,1152]{3,2,1,0:T(8,128)(2,1)}, u32[]{:S(2)}, u32[]{:S(2)}) collective-permute-start(bf16[4,2,72,1152]{3,2,1,0:T(8,128)(2,1)} %get-tuple-element.344), channel_id=1, source_target_pairs={{0,2},{2,0},{4,6},{6,4},{1,3},{3,1},{5,7},{7,5},{8,10},{10,8},{12,... | collective-permute-start | bytes 3981320 | tf_op jit(solution)/shard_map/ppermute | solution.py:119
  445.7 36.1 %collective-permute-start.55 = (bf16[4,2,72,1152]{3,2,1,0:T(8,128)(2,1)}, bf16[4,2,72,1152]{3,2,1,0:T(8,128)(2,1)}, u32[]{:S(2)}, u32[]{:S(2)}) collective-permute-start(bf16[4,2,72,1152]{3,2,1,0:T(8,128)(2,1)} %get-tuple-element.337), channel_id=1, source_target_pairs={{0,4},{2,6},{4,0},{6,2},{1,5},{3,7},{5,1},{7,3},{8,12},{10,14},{12... | collective-permute-start | bytes 3981320 | tf_op jit(solution)/shard_map/ppermute | solution.py:119
  472.7 33.6 %collective-permute-start.59 = (bf16[4,2,72,1152]{3,2,1,0:T(8,128)(2,1)}, bf16[4,2,72,1152]{3,2,1,0:T(8,128)(2,1)S(1)}, u32[]{:S(2)}, u32[]{:S(2)}) collective-permute-start(bf16[4,2,72,1152]{3,2,1,0:T(8,128)(2,1)} %copy-done.143), channel_id=1, source_target_pairs={{0,4},{2,6},{4,0},{6,2},{1,5},{3,7},{5,1},{7,3},{8,12},{10,14},{12... | collective-permute-start | bytes 3981320 | tf_op jit(solution)/shard_map/ppermute | solution.py:119
  488.5 43.3 %collective-permute-start.64 = (bf16[4,72,1152]{2,1,0:T(8,128)(2,1)}, bf16[4,72,1152]{2,1,0:T(8,128)(2,1)}, u32[]{:S(2)}, u32[]{:S(2)}) collective-permute-start(bf16[4,72,1152]{2,1,0:T(8,128)(2,1)} %get-tuple-element.357), channel_id=1, source_target_pairs={{0,4},{2,6},{4,0},{6,2},{1,5},{3,7},{5,1},{7,3},{8,12},{10,14},{12... | collective-permute-start | bytes 1990664 | tf_op jit(solution)/shard_map/ppermute | solution.py:119
  489.6 43.4 %collective-permute-start.63 = (bf16[4,72,1152]{2,1,0:T(8,128)(2,1)}, bf16[4,72,1152]{2,1,0:T(8,128)(2,1)}, u32[]{:S(2)}, u32[]{:S(2)}) collective-permute-start(bf16[4,72,1152]{2,1,0:T(8,128)(2,1)} %get-tuple-element.356), channel_id=1, source_target_pairs={{0,2},{2,0},{4,6},{6,4},{1,3},{3,1},{5,7},{7,5},{8,10},{10,8},{12,... | collective-permute-start | bytes 1990664 | tf_op jit(solution)/shard_map/ppermute | solution.py:119
  537.9 43.7 %collective-permute-start.67 = (f32[256,1152]{1,0:T(8,128)S(1)}, f32[256,1152]{1,0:T(8,128)S(1)}, u32[]{:S(2)}, u32[]{:S(2)}) collective-permute-start(f32[256,1152]{1,0:T(8,128)S(1)} %copy-done.145), channel_id=1, source_target_pairs={{0,1},{1,0},{2,3},{3,2},{4,5},{5,4},{6,7},{7,6},{8,9},{9,8},{10,11... | collective-permute-start | bytes 3538952 | tf_op jit(solution)/shard_map/ppermute | solution.py:119
  597.4 38.3 %collective-permute-start.78 = (bf16[4,2,72,1152]{3,2,1,0:T(8,128)(2,1)S(1)}, bf16[4,2,72,1152]{3,2,1,0:T(8,128)(2,1)}, u32[]{:S(2)}, u32[]{:S(2)}) collective-permute-start(bf16[4,2,72,1152]{3,2,1,0:T(8,128)(2,1)S(1)} %get-tuple-element.389), channel_id=1, source_target_pairs={{0,4},{2,6},{4,0},{6,2},{1,5},{3,7},{5,1},{7,3},{8,12},{10,14},{12... | collective-permute-start | bytes 3981320 | tf_op jit(solution)/shard_map/ppermute | solution.py:119
  600.9 46.5 %collective-permute-start.79 = (bf16[2,72,1152]{2,1,0:T(8,128)(2,1)S(1)}, bf16[2,72,1152]{2,1,0:T(8,128)(2,1)S(1)}, u32[]{:S(2)}, u32[]{:S(2)}) collective-permute-start(bf16[2,72,1152]{2,1,0:T(8,128)(2,1)S(1)} %fusion.59), channel_id=1, source_target_pairs={{0,16},{8,24},{16,0},{24,8},{1,17},{9,25},{17,1},{25,9},{2,18},{10... | collective-permute-start | bytes 995336 | tf_op jit(solution)/shard_map/ppermute | solution.py:119
  620.6 45.5 %collective-permute-start.81 = (bf16[4,2,72,1152]{3,2,1,0:T(8,128)(2,1)S(1)}, bf16[4,2,72,1152]{3,2,1,0:T(8,128)(2,1)S(1)}, u32[]{:S(2)}, u32[]{:S(2)}) collective-permute-start(bf16[4,2,72,1152]{3,2,1,0:T(8,128)(2,1)S(1)} %get-tuple-element.400), channel_id=1, source_target_pairs={{0,4},{2,6},{4,0},{6,2},{1,5},{3,7},{5,1},{7,3},{8,12},{10,14},{12... | collective-permute-start | bytes 3981320 | tf_op jit(solution)/shard_map/ppermute | solution.py:119
  628.3 43.8 %collective-permute-start.83 = (bf16[4,2,72,1152]{3,2,1,0:T(8,128)(2,1)S(1)}, bf16[4,2,72,1152]{3,2,1,0:T(8,128)(2,1)S(1)}, u32[]{:S(2)}, u32[]{:S(2)}) collective-permute-start(bf16[4,2,72,1152]{3,2,1,0:T(8,128)(2,1)S(1)} %get-tuple-element.408), channel_id=1, source_target_pairs={{0,2},{2,0},{4,6},{6,4},{1,3},{3,1},{5,7},{7,5},{8,10},{10,8},{12,... | collective-permute-start | bytes 3981320 | tf_op jit(solution)/shard_map/ppermute | solution.py:119
  644.8 34.0 %collective-permute-start.85 = (bf16[4,72,1152]{2,1,0:T(8,128)(2,1)}, bf16[4,72,1152]{2,1,0:T(8,128)(2,1)S(1)}, u32[]{:S(2)}, u32[]{:S(2)}) collective-permute-start(bf16[4,72,1152]{2,1,0:T(8,128)(2,1)} %get-tuple-element.411), channel_id=1, source_target_pairs={{0,4},{2,6},{4,0},{6,2},{1,5},{3,7},{5,1},{7,3},{8,12},{10,14},{12... | collective-permute-start | bytes 1990664 | tf_op jit(solution)/shard_map/ppermute | solution.py:119
  645.8 40.4 %collective-permute-start.86 = (bf16[4,72,1152]{2,1,0:T(8,128)(2,1)}, bf16[4,72,1152]{2,1,0:T(8,128)(2,1)S(1)}, u32[]{:S(2)}, u32[]{:S(2)}) collective-permute-start(bf16[4,72,1152]{2,1,0:T(8,128)(2,1)} %get-tuple-element.414), channel_id=1, source_target_pairs={{0,2},{2,0},{4,6},{6,4},{1,3},{3,1},{5,7},{7,5},{8,10},{10,8},{12,... | collective-permute-start | bytes 1990664 | tf_op jit(solution)/shard_map/ppermute | solution.py:119
  672.1 40.2 %collective-permute-start.87 = (bf16[4,72,1152]{2,1,0:T(8,128)(2,1)}, bf16[4,72,1152]{2,1,0:T(8,128)(2,1)}, u32[]{:S(2)}, u32[]{:S(2)}) collective-permute-start(bf16[4,72,1152]{2,1,0:T(8,128)(2,1)} %get-tuple-element.418), channel_id=1, source_target_pairs={{0,2},{2,0},{4,6},{6,4},{1,3},{3,1},{5,7},{7,5},{8,10},{10,8},{12,... | collective-permute-start | bytes 1990664 | tf_op jit(solution)/shard_map/ppermute | solution.py:119
  673.5 71.1 %collective-permute-start.95 = (bf16[4,2,72,1152]{3,2,1,0:T(8,128)(2,1)}, bf16[4,2,72,1152]{3,2,1,0:T(8,128)(2,1)}, u32[]{:S(2)}, u32[]{:S(2)}) collective-permute-start(bf16[4,2,72,1152]{3,2,1,0:T(8,128)(2,1)} %get-tuple-element.438), channel_id=1, source_target_pairs={{0,4},{2,6},{4,0},{6,2},{1,5},{3,7},{5,1},{7,3},{8,12},{10,14},{12... | collective-permute-start | bytes 3981320 | tf_op jit(solution)/shard_map/ppermute | solution.py:119
  678.8 43.4 %collective-permute-start.102 = (bf16[4,72,1152]{2,1,0:T(8,128)(2,1)}, bf16[4,72,1152]{2,1,0:T(8,128)(2,1)}, u32[]{:S(2)}, u32[]{:S(2)}) collective-permute-start(bf16[4,72,1152]{2,1,0:T(8,128)(2,1)} %get-tuple-element.449), channel_id=1, source_target_pairs={{0,4},{2,6},{4,0},{6,2},{1,5},{3,7},{5,1},{7,3},{8,12},{10,14},{12... | collective-permute-start | bytes 1990664 | tf_op jit(solution)/shard_map/ppermute | solution.py:119
  690.0 60.9 %collective-permute-start.100 = (bf16[4,2,72,1152]{3,2,1,0:T(8,128)(2,1)}, bf16[4,2,72,1152]{3,2,1,0:T(8,128)(2,1)}, u32[]{:S(2)}, u32[]{:S(2)}) collective-permute-start(bf16[4,2,72,1152]{3,2,1,0:T(8,128)(2,1)} %get-tuple-element.447), channel_id=1, source_target_pairs={{0,2},{2,0},{4,6},{6,4},{1,3},{3,1},{5,7},{7,5},{8,10},{10,8},{12,... | collective-permute-start | bytes 3981320 | tf_op jit(solution)/shard_map/ppermute | solution.py:119
  736.7 40.5 %collective-permute-start.106 = (bf16[2,2,72,1152]{3,2,0,1:T(8,128)(2,1)}, bf16[2,2,72,1152]{3,2,0,1:T(8,128)(2,1)}, u32[]{:S(2)}, u32[]{:S(2)}) collective-permute-start(bf16[2,2,72,1152]{3,2,0,1:T(8,128)(2,1)} %fusion.19), channel_id=1, source_target_pairs={{0,8},{8,0},{16,24},{24,16},{1,9},{9,1},{17,25},{25,17},{2,10},{10... | collective-permute-start | bytes 1990664 | tf_op jit(solution)/shard_map/ppermute | solution.py:119
  737.4 78.5 %collective-permute-start.89 = (f32[256,1152]{1,0:T(8,128)}, f32[256,1152]{1,0:T(8,128)}, u32[]{:S(2)}, u32[]{:S(2)}) collective-permute-start(f32[256,1152]{1,0:T(8,128)} %get-tuple-element.423), channel_id=1, source_target_pairs={{0,1},{1,0},{2,3},{3,2},{4,5},{5,4},{6,7},{7,6},{8,9},{9,8},{10,11... | collective-permute-start | bytes 3538952 | tf_op jit(solution)/shard_map/ppermute | solution.py:119
  743.3 76.0 %collective-permute-start.97 = (bf16[4,2,72,1152]{3,2,1,0:T(8,128)(2,1)}, bf16[4,2,72,1152]{3,2,1,0:T(8,128)(2,1)}, u32[]{:S(2)}, u32[]{:S(2)}) collective-permute-start(bf16[4,2,72,1152]{3,2,1,0:T(8,128)(2,1)} %get-tuple-element.442), channel_id=1, source_target_pairs={{0,2},{2,0},{4,6},{6,4},{1,3},{3,1},{5,7},{7,5},{8,10},{10,8},{12,... | collective-permute-start | bytes 3981320 | tf_op jit(solution)/shard_map/ppermute | solution.py:119
  749.7 71.5 %collective-permute-start.96 = (bf16[4,2,72,1152]{3,2,1,0:T(8,128)(2,1)}, bf16[4,2,72,1152]{3,2,1,0:T(8,128)(2,1)}, u32[]{:S(2)}, u32[]{:S(2)}) collective-permute-start(bf16[4,2,72,1152]{3,2,1,0:T(8,128)(2,1)} %get-tuple-element.439), channel_id=1, source_target_pairs={{0,4},{2,6},{4,0},{6,2},{1,5},{3,7},{5,1},{7,3},{8,12},{10,14},{12... | collective-permute-start | bytes 3981320 | tf_op jit(solution)/shard_map/ppermute | solution.py:119
  (295 other events, 3690.7 us)

commit v4 on v3

--- a/solution.py
+++ b/solution.py
@@ -11,12 +11,12 @@
 LANES = 128
 EPSILON = 1e-06
 MIB = 1024 * 1024
-SCALE = 1.07
-SCALE_B = 1.11
-TRIP = 1.41
+SCALE = 1.12
+SCALE_B = 1.05
+TRIP = 1.13
 ADD = 4.0
-SWAP = 6.0
-RATE = 0.0398
+SWAP = 8.0
+RATE = 0.0392
 SEND = 0.5
 DEPTH = 2
 HOLD = True

time: 895 us -> 888 us (level)
    unnamed x458 -> x440, local copies, waits for them, and re-layouts: 58.4 us -> 52 us
  transfers between devices with their start and end apart: 112 -> 112, of which waited for: 45 -> 47; matrix products, arithmetic and copies ran while one was open for 13% -> 12% of each run, Pallas kernels for 21% -> 20%
where the time goes in v4:
time: 888 us; the launch traced here: 877 us
  waiting for transfers between devices  415 us (47%)
  Pallas kernels  202 us (23%)
  starting transfers between devices  90.6 us (10%)
  local copies, waits for them, and re-layouts  84.5 us (10%)
  other arithmetic  80.4 us (9%)
    ppermute x112, waiting for transfers between devices, pxor(): return lax.ppermute(value, axis, [(i, i ^ flip) for i in range(size)])  415 us
    pallas_call x24, Pallas kernels, call(): pl.pallas_call(body, out_shape=[jax.ShapeDtypeStruct(shape, dtype) for sh...  93.4 us
    ppermute x112, starting transfers between devices, pxor(): return lax.ppermute(value, axis, [(i, i ^ flip) for i in range(size)])  90.6 us
    pallas_call x12, Pallas kernels, weight_grad(): pl.pallas_call(body, out_shape=[jax.ShapeDtypeStruct(shape, bf16)] * 2, i...  62.2 us
    unnamed x440, local copies, waits for them, and re-layouts  52 us
    pallas_call x2, Pallas kernels, attend_grad(): pl.pallas_call(partial(attend_grad_kernel, period, lead, skip), grid=(blo...  21.1 us
    pallas_call x10, Pallas kernels, place(): pl.pallas_call(partial(place_kernel, cuts), grid_spec=pltpu.PrefetchScala...  18.1 us
  transfers between devices with their start and end apart: 112, of which 47 were waited for; matrix products, arithmetic and copies ran while one was open for 12% of the time, Pallas kernels for 20%

profile of v4, /device:TPU:0, one launch (start us, length us, event | category | flops | bytes accessed | tf_op | source)
XLA Modules:
  0.0 877.3 jit_solution(16486469213658402493)
XLA Ops:
  30.3 8.0 collective-permute-done.6
  38.4 9.0 %collective-permute-done.7 = bf16[2,80,1152]{2,1,0:T(8,128)(2,1)S(1)} collective-permute-done((bf16[2,80,1152]{2,1,0:T(8,128)(2,1)}, bf16[2,80,1152]{2,1,0:T(8,128)(2,1)S(1)}, u32[]{:S(2)}, u32[]{:S(2)}) %collective-permute-start.7) | collective-permute-done | bytes 368672 | tf_op jit(solution)/shard_map/ppermute | solution.py:119
  56.7 10.7 %collective-permute-done.3 = f32[13824]{0:T(1024)S(1)} collective-permute-done((f32[13824]{0:T(1024)S(1)}, f32[13824]{0:T(1024)S(1)}, u32[]{:S(2)}, u32[]{:S(2)}) %collective-permute-start.3) | collective-permute-done | bytes 55328 | tf_op jit(solution)/shard_map/ppermute | solution.py:119
  68.0 14.1 %collective-permute-done.10 = bf16[2,72,2304]{2,1,0:T(8,128)(2,1)S(1)} collective-permute-done((bf16[2,72,2304]{2,1,0:T(8,128)(2,1)S(1)}, bf16[2,72,2304]{2,1,0:T(8,128)(2,1)S(1)}, u32[]{:S(2)}, u32[]{:S(2)}) %collective-permute-start.10) | collective-permute-done | bytes 663584 | tf_op jit(solution)/shard_map/ppermute | solution.py:119
  85.4 12.8 %collective-permute-done.13 = bf16[2,72,2304]{2,1,0:T(8,128)(2,1)S(1)} collective-permute-done((bf16[2,72,2304]{2,1,0:T(8,128)(2,1)S(1)}, bf16[2,72,2304]{2,1,0:T(8,128)(2,1)S(1)}, u32[]{:S(2)}, u32[]{:S(2)}) %collective-permute-start.13) | collective-permute-done | bytes 663584 | tf_op jit(solution)/shard_map/ppermute | solution.py:119
  103.0 10.4 %collective-permute-done.17 = bf16[2,72,2304]{2,1,0:T(8,128)(2,1)S(1)} collective-permute-done((bf16[2,72,2304]{2,1,0:T(8,128)(2,1)S(1)}, bf16[2,72,2304]{2,1,0:T(8,128)(2,1)S(1)}, u32[]{:S(2)}, u32[]{:S(2)}) %collective-permute-start.17) | collective-permute-done | bytes 663584 | tf_op jit(solution)/shard_map/ppermute | solution.py:119
  156.1 8.1 collective-permute-done.22
  164.8 8.8 %collective-permute-done.23 = bf16[2,72,1152]{2,1,0:T(8,128)(2,1)S(1)} collective-permute-done((bf16[2,72,1152]{2,1,0:T(8,128)(2,1)}, bf16[2,72,1152]{2,1,0:T(8,128)(2,1)S(1)}, u32[]{:S(2)}, u32[]{:S(2)}) %collective-permute-start.23) | collective-permute-done | bytes 331808 | tf_op jit(solution)/shard_map/ppermute | solution.py:119
  173.7 11.9 %collective-permute-done.24.refs_1_ = bf16[4,72,2304]{2,1,0:T(8,128)(2,1)S(1)} collective-permute-done((bf16[4,72,2304]{2,1,0:T(8,128)(2,1)S(1)}, bf16[4,72,2304]{2,1,0:T(8,128)(2,1)S(1)}, u32[]{:S(2)}, u32[]{:S(2)}) %collective-permute-start.24) | collective-permute-done | bytes 1327136 | tf_op jit(solution)/shard_map/ppermute | solution.py:119
  189.4 14.8 %collective-permute-done.26 = bf16[2,72,2304]{2,1,0:T(8,128)(2,1)S(1)} collective-permute-done((bf16[2,72,2304]{2,1,0:T(8,128)(2,1)S(1)}, bf16[2,72,2304]{2,1,0:T(8,128)(2,1)S(1)}, u32[]{:S(2)}, u32[]{:S(2)}) %collective-permute-start.26) | collective-permute-done | bytes 663584 | tf_op jit(solution)/shard_map/ppermute | solution.py:119
  205.1 15.8 %collective-permute-done.28 = bf16[2,72,2304]{2,1,0:T(8,128)(2,1)S(1)} collective-permute-done((bf16[2,72,2304]{2,1,0:T(8,128)(2,1)S(1)}, bf16[2,72,2304]{2,1,0:T(8,128)(2,1)S(1)}, u32[]{:S(2)}, u32[]{:S(2)}) %collective-permute-start.28) | collective-permute-done | bytes 663584 | tf_op jit(solution)/shard_map/ppermute | solution.py:119
  222.3 14.9 %collective-permute-done.32.refs_2_ = bf16[4,72,1152]{2,1,0:T(8,128)(2,1)S(1)} collective-permute-done((bf16[4,72,1152]{2,1,0:T(8,128)(2,1)S(1)}, bf16[4,72,1152]{2,1,0:T(8,128)(2,1)S(1)}, u32[]{:S(2)}, u32[]{:S(2)}) %collective-permute-start.32) | collective-permute-done | bytes 663584 | tf_op jit(solution)/shard_map/ppermute | solution.py:119
  238.6 13.6 %collective-permute-done.35.refs_2_ = bf16[4,72,1152]{2,1,0:T(8,128)(2,1)S(1)} collective-permute-done((bf16[4,72,1152]{2,1,0:T(8,128)(2,1)S(1)}, bf16[4,72,1152]{2,1,0:T(8,128)(2,1)S(1)}, u32[]{:S(2)}, u32[]{:S(2)}) %collective-permute-start.35) | collective-permute-done | bytes 663584 | tf_op jit(solution)/shard_map/ppermute | solution.py:119
  264.3 10.6 %mlp_forward.1 = (f32[512,1152]{1,0:T(8,128)}, f32[512,1152]{1,0:T(8,128)}, bf16[512,1152]{1,0:T(8,128)(2,1)S(1)}, bf16[512,1152]{1,0:T(8,128)(2,1)S(1)}, f32[25...) custom-call(bf16[256,1152]{1,0:T(8,128)(2,1)S(1)} %get-tuple-element.282.refs_0_, ...), custom_call_target="tpu_custom_call" | custom-call | flops 1 | bytes 1 | tf_op jit(solution)/shard_map/mlp_forward/pallas_call | solution.py:473
  285.6 21.8 %collective-permute-done.40.refs_2_ = bf16[4,72,2304]{2,1,0:T(8,128)(2,1)S(1)} collective-permute-done((bf16[4,72,2304]{2,1,0:T(8,128)(2,1)S(1)}, bf16[4,72,2304]{2,1,0:T(8,128)(2,1)S(1)}, u32[]{:S(2)}, u32[]{:S(2)}) %collective-permute-start.40) | collective-permute-done | bytes 1327136 | tf_op jit(solution)/shard_map/ppermute | solution.py:119
  325.5 15.4 %collective-permute-done.46.refs_2_ = bf16[4,72,2304]{2,1,0:T(8,128)(2,1)} collective-permute-done((bf16[4,72,2304]{2,1,0:T(8,128)(2,1)}, bf16[4,72,2304]{2,1,0:T(8,128)(2,1)}, u32[]{:S(2)}, u32[]{:S(2)}) %collective-permute-start.46) | collective-permute-done | bytes 1327136 | tf_op jit(solution)/shard_map/ppermute | solution.py:119
  345.5 7.5 collective-permute-done.42
  353.0 36.6 %collective-permute-done.44 = bf16[2,64,1728]{2,1,0:T(8,128)(2,1)S(1)} collective-permute-done((bf16[2,64,1728]{2,1,0:T(8,128)(2,1)S(1)}, bf16[2,64,1728]{2,1,0:T(8,128)(2,1)S(1)}, u32[]{:S(2)}, u32[]{:S(2)}) %collective-permute-start.44) | collective-permute-done | bytes 442400 | tf_op jit(solution)/shard_map/ppermute | solution.py:119
  446.4 7.8 mlp_backward.4
  463.4 8.4 mlp_backward.5
  502.0 7.3 collective-permute-done.60
  538.9 10.3 %attend_grad.2 = (bf16[2,256,1728]{2,1,0:T(8,128)(2,1)S(1)}, f32[2,2,576]{2,1,0:T(2,128)S(1)}) custom-call(bf16[2,256,1728]{2,1,0:T(8,128)(2,1)S(1)} %bitcast.446, bf16[2,256,1728]{2,1,0:T(8,128)(2,1)S(1)} %bitcast.447, bf16[2,256,576]{2,1,0:T(8,128)(2,1)S(1)} %bitcast.484), custom_call_target="tpu_custom_call" | custom-call | flops 1 | bytes 1 | tf_op jit(solution)/shard_map/attend_grad/pallas_call | solution.py:428
  557.8 8.5 collective-permute-done.65
  648.9 7.3 mlp_backward.7
  687.6 10.8 %attend_grad.3 = (bf16[2,256,1152]{2,1,0:T(8,128)(2,1)S(1)}, bf16[2,256,1152]{2,1,0:T(8,128)(2,1)S(1)}, f32[2,2,576]{2,1,0:T(2,128)S(1)}) custom-call(bf16[2,256,1152]{2,1,0:T(8,128)(2,1)S(1)} %bitcast.473, bf16[2,256,1152]{2,1,0:T(8,128)(2,1)S(1)} %bitcast.475, bf16[2,256,1152]{2,1,0:T(8,128)(2,1)S(1)} %bitcast.487), custom_call_target="tpu_custom_call" | custom-call | flops 1 | bytes 1 | tf_op jit(solution)/shard_map/attend_grad/pallas_call | solution.py:428
  722.8 9.4 %collective-permute-done.105 = bf16[2,72,1152]{2,1,0:T(8,128)(2,1)S(1)} collective-permute-done((bf16[2,72,1152]{2,1,0:T(8,128)(2,1)S(1)}, bf16[2,72,1152]{2,1,0:T(8,128)(2,1)S(1)}, u32[]{:S(2)}, u32[]{:S(2)}) %collective-permute-start.105) | collective-permute-done | bytes 331808 | tf_op jit(solution)/shard_map/ppermute | solution.py:119
  755.4 8.5 collective-permute-done.94
  775.1 14.6 %collective-permute-done.107 = bf16[2,72,1152]{2,1,0:T(8,128)(2,1)S(1)} collective-permute-done((bf16[2,72,1152]{2,1,0:T(8,128)(2,1)S(1)}, bf16[2,72,1152]{2,1,0:T(8,128)(2,1)S(1)}, u32[]{:S(2)}, u32[]{:S(2)}) %collective-permute-start.107) | collective-permute-done | bytes 331808 | tf_op jit(solution)/shard_map/ppermute | solution.py:119
  791.9 14.6 %collective-permute-done.101 = bf16[4,72,1152]{2,1,0:T(8,128)(2,1)S(1)} collective-permute-done((bf16[4,72,1152]{2,1,0:T(8,128)(2,1)S(1)}, bf16[4,72,1152]{2,1,0:T(8,128)(2,1)S(1)}, u32[]{:S(2)}, u32[]{:S(2)}) %collective-permute-start.101) | collective-permute-done | bytes 663584 | tf_op jit(solution)/shard_map/ppermute | solution.py:119
  827.7 12.4 %collective-permute-done.109 = bf16[2,72,1152]{2,1,0:T(8,128)(2,1)S(1)} collective-permute-done((bf16[2,72,1152]{2,1,0:T(8,128)(2,1)S(1)}, bf16[2,72,1152]{2,1,0:T(8,128)(2,1)S(1)}, u32[]{:S(2)}, u32[]{:S(2)}) %collective-permute-start.109) | collective-permute-done | bytes 331808 | tf_op jit(solution)/shard_map/ppermute | solution.py:119
  843.9 13.8 %collective-permute-done.110 = bf16[2,2,72,1152]{3,2,0,1:T(8,128)(2,1)S(1)} collective-permute-done((bf16[2,2,72,1152]{3,2,0,1:T(8,128)(2,1)S(1)}, bf16[2,2,72,1152]{3,2,0,1:T(8,128)(2,1)S(1)}, u32[]{:S(2)}, u32[]{:S(2)}) %collective-permute-start.110) | collective-permute-done | bytes 663584 | tf_op jit(solution)/shard_map/ppermute | solution.py:119
  860.1 13.3 %collective-permute-done.111 = bf16[2,72,1152]{2,1,0:T(8,128)(2,1)S(1)} collective-permute-done((bf16[2,72,1152]{2,1,0:T(8,128)(2,1)S(1)}, bf16[2,72,1152]{2,1,0:T(8,128)(2,1)S(1)}, u32[]{:S(2)}, u32[]{:S(2)}) %collective-permute-start.111) | collective-permute-done | bytes 331808 | tf_op jit(solution)/shard_map/ppermute | solution.py:119
  (916 shorter events, 481.2 us)
Async XLA Ops:
  47.6 34.6 %collective-permute-start.9 = (bf16[4,80,1152]{2,1,0:T(8,128)(2,1)S(1)}, bf16[4,80,1152]{2,1,0:T(8,128)(2,1)S(1)}, u32[]{:S(2)}, u32[]{:S(2)}) collective-permute-start(bf16[4,80,1152]{2,1,0:T(8,128)(2,1)S(1)} %pad_maximum_fusion.13.refs_0_), channel_id=1, source_target_pairs={{0,4},{2,6},{4,0},{6,2},{1,5},{3,7},{5,1},{7,3},{8,12},{10,14},{12... | collective-permute-start | bytes 2211848 | tf_op jit(solution)/shard_map/ppermute | solution.py:119
  49.9 33.0 %collective-permute-start.8 = (bf16[4,80,1152]{2,1,0:T(8,128)(2,1)S(1)}, bf16[4,80,1152]{2,1,0:T(8,128)(2,1)S(1)}, u32[]{:S(2)}, u32[]{:S(2)}) collective-permute-start(bf16[4,80,1152]{2,1,0:T(8,128)(2,1)S(1)} %pad_maximum_fusion.13.refs_0_), channel_id=1, source_target_pairs={{0,2},{2,0},{4,6},{6,4},{1,3},{3,1},{5,7},{7,5},{8,10},{10,8},{12,... | collective-permute-start | bytes 2211848 | tf_op jit(solution)/shard_map/ppermute | solution.py:119
  67.4 53.8 %collective-permute-start.4 = (f32[13824]{0:T(1024)S(1)}, f32[13824]{0:T(1024)S(1)}, u32[]{:S(2)}, u32[]{:S(2)}) collective-permute-start(f32[13824]{0:T(1024)S(1)} %add.600), channel_id=1, source_target_pairs={{0,4},{2,6},{4,0},{6,2},{1,5},{3,7},{5,1},{7,3},{8,12},{10,14},{12... | collective-permute-start | bytes 165896 | tf_op jit(solution)/shard_map/ppermute | solution.py:119
  117.5 37.0 %collective-permute-start.21 = (bf16[4,72,2304]{2,1,0:T(8,128)(2,1)}, bf16[4,72,2304]{2,1,0:T(8,128)(2,1)}, u32[]{:S(2)}, u32[]{:S(2)}) collective-permute-start(bf16[4,72,2304]{2,1,0:T(8,128)(2,1)} %pad_maximum_fusion.2.refs_0_), channel_id=1, source_target_pairs={{0,4},{2,6},{4,0},{6,2},{1,5},{3,7},{5,1},{7,3},{8,12},{10,14},{12... | collective-permute-start | bytes 3981320 | tf_op jit(solution)/shard_map/ppermute | solution.py:119
  118.7 36.1 %collective-permute-start.20 = (bf16[4,72,2304]{2,1,0:T(8,128)(2,1)}, bf16[4,72,2304]{2,1,0:T(8,128)(2,1)}, u32[]{:S(2)}, u32[]{:S(2)}) collective-permute-start(bf16[4,72,2304]{2,1,0:T(8,128)(2,1)} %pad_maximum_fusion.2.refs_0_), channel_id=1, source_target_pairs={{0,2},{2,0},{4,6},{6,4},{1,3},{3,1},{5,7},{7,5},{8,10},{10,8},{12,... | collective-permute-start | bytes 3981320 | tf_op jit(solution)/shard_map/ppermute | solution.py:119
  153.6 34.1 %collective-permute-start.18 = (f32[256,1152]{1,0:T(8,128)S(1)}, f32[256,1152]{1,0:T(8,128)S(1)}, u32[]{:S(2)}, u32[]{:S(2)}) collective-permute-start(f32[256,1152]{1,0:T(8,128)S(1)} %get-tuple-element.260), channel_id=1, source_target_pairs={{0,1},{1,0},{2,3},{3,2},{4,5},{5,4},{6,7},{7,6},{8,9},{9,8},{10,11... | collective-permute-start | bytes 3538952 | tf_op jit(solution)/shard_map/ppermute | solution.py:119
  186.0 35.2 %collective-permute-start.29 = (bf16[4,72,2304]{2,1,0:T(8,128)(2,1)}, bf16[4,72,2304]{2,1,0:T(8,128)(2,1)S(1)}, u32[]{:S(2)}, u32[]{:S(2)}) collective-permute-start(bf16[4,72,2304]{2,1,0:T(8,128)(2,1)} %collective-permute-done.20.refs_1_), channel_id=1, source_target_pairs={{0,4},{2,6},{4,0},{6,2},{1,5},{3,7},{5,1},{7,3},{8,12},{10,14},{12... | collective-permute-start | bytes 3981320 | tf_op jit(solution)/shard_map/ppermute | solution.py:119
  189.4 74.9 %collective-permute-start.33 = (bf16[256,1152]{1,0:T(8,128)(2,1)S(1)}, bf16[256,1152]{1,0:T(8,128)(2,1)S(1)}, u32[]{:S(2)}, u32[]{:S(2)}) collective-permute-start(bf16[256,1152]{1,0:T(8,128)(2,1)S(1)} %get-tuple-element.282.refs_0_), channel_id=1, source_target_pairs={{0,1},{1,0},{2,3},{3,2},{4,5},{5,4},{6,7},{7,6},{8,9},{9,8},{10,11... | collective-permute-start | bytes 1769480 | tf_op jit(solution)/shard_map/ppermute | solution.py:119
  204.2 33.3 %collective-permute-start.31 = (bf16[4,72,2304]{2,1,0:T(8,128)(2,1)S(1)}, bf16[4,72,2304]{2,1,0:T(8,128)(2,1)S(1)}, u32[]{:S(2)}, u32[]{:S(2)}) collective-permute-start(bf16[4,72,2304]{2,1,0:T(8,128)(2,1)S(1)} %collective-permute-done.25.refs_2_), channel_id=1, source_target_pairs={{0,2},{2,0},{4,6},{6,4},{1,3},{3,1},{5,7},{7,5},{8,10},{10,8},{12,... | collective-permute-start | bytes 3981320 | tf_op jit(solution)/shard_map/ppermute | solution.py:119
  284.2 34.9 %collective-permute-start.41 = (bf16[256,1152]{1,0:T(8,128)(2,1)S(1)}, bf16[256,1152]{1,0:T(8,128)(2,1)S(1)}, u32[]{:S(2)}, u32[]{:S(2)}) collective-permute-start(bf16[256,1152]{1,0:T(8,128)(2,1)S(1)} %get-tuple-element.300.refs_0_), channel_id=1, source_target_pairs={{0,1},{1,0},{2,3},{3,2},{4,5},{5,4},{6,7},{7,6},{8,9},{9,8},{10,11... | collective-permute-start | bytes 1769480 | tf_op jit(solution)/shard_map/ppermute | solution.py:119
  308.5 32.4 %collective-permute-start.46 = (bf16[4,72,2304]{2,1,0:T(8,128)(2,1)}, bf16[4,72,2304]{2,1,0:T(8,128)(2,1)}, u32[]{:S(2)}, u32[]{:S(2)}) collective-permute-start(bf16[4,72,2304]{2,1,0:T(8,128)(2,1)} %pad_maximum_fusion.4.refs_0_), channel_id=1, source_target_pairs={{0,4},{2,6},{4,0},{6,2},{1,5},{3,7},{5,1},{7,3},{8,12},{10,14},{12... | collective-permute-start | bytes 3981320 | tf_op jit(solution)/shard_map/ppermute | solution.py:119
  310.9 32.4 %collective-permute-start.45 = (bf16[4,72,2304]{2,1,0:T(8,128)(2,1)}, bf16[4,72,2304]{2,1,0:T(8,128)(2,1)}, u32[]{:S(2)}, u32[]{:S(2)}) collective-permute-start(bf16[4,72,2304]{2,1,0:T(8,128)(2,1)} %pad_maximum_fusion.4.refs_0_), channel_id=1, source_target_pairs={{0,2},{2,0},{4,6},{6,4},{1,3},{3,1},{5,7},{7,5},{8,10},{10,8},{12,... | collective-permute-start | bytes 3981320 | tf_op jit(solution)/shard_map/ppermute | solution.py:119
  340.9 63.9 %collective-permute-start.51 = (bf16[4,72,2304]{2,1,0:T(8,128)(2,1)}, bf16[4,72,2304]{2,1,0:T(8,128)(2,1)S(1)}, u32[]{:S(2)}, u32[]{:S(2)}) collective-permute-start(bf16[4,72,2304]{2,1,0:T(8,128)(2,1)} %collective-permute-done.38.refs_1_), channel_id=1, source_target_pairs={{0,4},{2,6},{4,0},{6,2},{1,5},{3,7},{5,1},{7,3},{8,12},{10,14},{12... | collective-permute-start | bytes 3981320 | tf_op jit(solution)/shard_map/ppermute | solution.py:119
  343.3 62.6 %collective-permute-start.50 = (bf16[4,72,2304]{2,1,0:T(8,128)(2,1)}, bf16[4,72,2304]{2,1,0:T(8,128)(2,1)S(1)}, u32[]{:S(2)}, u32[]{:S(2)}) collective-permute-start(bf16[4,72,2304]{2,1,0:T(8,128)(2,1)} %collective-permute-done.46.refs_2_), channel_id=1, source_target_pairs={{0,2},{2,0},{4,6},{6,4},{1,3},{3,1},{5,7},{7,5},{8,10},{10,8},{12,... | collective-permute-start | bytes 3981320 | tf_op jit(solution)/shard_map/ppermute | solution.py:119
  345.3 44.3 %collective-permute-start.44 = (bf16[2,64,1728]{2,1,0:T(8,128)(2,1)S(1)}, bf16[2,64,1728]{2,1,0:T(8,128)(2,1)S(1)}, u32[]{:S(2)}, u32[]{:S(2)}) collective-permute-start(bf16[2,64,1728]{2,1,0:T(8,128)(2,1)S(1)} %pad_maximum_fusion.21), channel_id=1, source_target_pairs={{0,6},{2,4},{4,2},{6,0},{1,7},{3,5},{5,3},{7,1},{8,14},{10,12},{12... | collective-permute-start | bytes 1327112 | tf_op jit(solution)/shard_map/ppermute | solution.py:119
  445.8 36.5 %collective-permute-start.57 = (bf16[4,2,72,1152]{3,2,1,0:T(8,128)(2,1)}, bf16[4,2,72,1152]{3,2,1,0:T(8,128)(2,1)}, u32[]{:S(2)}, u32[]{:S(2)}) collective-permute-start(bf16[4,2,72,1152]{3,2,1,0:T(8,128)(2,1)} %get-tuple-element.344), channel_id=1, source_target_pairs={{0,2},{2,0},{4,6},{6,4},{1,3},{3,1},{5,7},{7,5},{8,10},{10,8},{12,... | collective-permute-start | bytes 3981320 | tf_op jit(solution)/shard_map/ppermute | solution.py:119
  454.3 32.4 %collective-permute-start.56 = (bf16[4,2,72,1152]{3,2,1,0:T(8,128)(2,1)}, bf16[4,2,72,1152]{3,2,1,0:T(8,128)(2,1)}, u32[]{:S(2)}, u32[]{:S(2)}) collective-permute-start(bf16[4,2,72,1152]{3,2,1,0:T(8,128)(2,1)} %copy-done.135), channel_id=1, source_target_pairs={{0,4},{2,6},{4,0},{6,2},{1,5},{3,7},{5,1},{7,3},{8,12},{10,14},{12... | collective-permute-start | bytes 3981320 | tf_op jit(solution)/shard_map/ppermute | solution.py:119
  479.0 39.6 %collective-permute-start.59 = (bf16[4,2,72,1152]{3,2,1,0:T(8,128)(2,1)S(1)}, bf16[4,2,72,1152]{3,2,1,0:T(8,128)(2,1)S(1)}, u32[]{:S(2)}, u32[]{:S(2)}) collective-permute-start(bf16[4,2,72,1152]{3,2,1,0:T(8,128)(2,1)S(1)} %copy-done.134), channel_id=1, source_target_pairs={{0,4},{2,6},{4,0},{6,2},{1,5},{3,7},{5,1},{7,3},{8,12},{10,14},{12... | collective-permute-start | bytes 3981320 | tf_op jit(solution)/shard_map/ppermute | solution.py:119
  528.5 52.9 %collective-permute-start.67 = (f32[256,1152]{1,0:T(8,128)}, f32[256,1152]{1,0:T(8,128)}, u32[]{:S(2)}, u32[]{:S(2)}) collective-permute-start(f32[256,1152]{1,0:T(8,128)} %get-tuple-element.361), channel_id=1, source_target_pairs={{0,1},{1,0},{2,3},{3,2},{4,5},{5,4},{6,7},{7,6},{8,9},{9,8},{10,11... | collective-permute-start | bytes 3538952 | tf_op jit(solution)/shard_map/ppermute | solution.py:119
  595.6 38.5 %collective-permute-start.78 = (bf16[4,2,72,1152]{3,2,1,0:T(8,128)(2,1)S(1)}, bf16[4,2,72,1152]{3,2,1,0:T(8,128)(2,1)S(1)}, u32[]{:S(2)}, u32[]{:S(2)}) collective-permute-start(bf16[4,2,72,1152]{3,2,1,0:T(8,128)(2,1)S(1)} %get-tuple-element.389), channel_id=1, source_target_pairs={{0,4},{2,6},{4,0},{6,2},{1,5},{3,7},{5,1},{7,3},{8,12},{10,14},{12... | collective-permute-start | bytes 3981320 | tf_op jit(solution)/shard_map/ppermute | solution.py:119
  618.7 43.6 %collective-permute-start.82 = (bf16[4,2,72,1152]{3,2,1,0:T(8,128)(2,1)S(1)}, bf16[4,2,72,1152]{3,2,1,0:T(8,128)(2,1)S(1)}, u32[]{:S(2)}, u32[]{:S(2)}) collective-permute-start(bf16[4,2,72,1152]{3,2,1,0:T(8,128)(2,1)S(1)} %get-tuple-element.406), channel_id=1, source_target_pairs={{0,4},{2,6},{4,0},{6,2},{1,5},{3,7},{5,1},{7,3},{8,12},{10,14},{12... | collective-permute-start | bytes 3981320 | tf_op jit(solution)/shard_map/ppermute | solution.py:119
  626.2 39.9 %collective-permute-start.83 = (bf16[4,2,72,1152]{3,2,1,0:T(8,128)(2,1)S(1)}, bf16[4,2,72,1152]{3,2,1,0:T(8,128)(2,1)S(1)}, u32[]{:S(2)}, u32[]{:S(2)}) collective-permute-start(bf16[4,2,72,1152]{3,2,1,0:T(8,128)(2,1)S(1)} %get-tuple-element.408), channel_id=1, source_target_pairs={{0,2},{2,0},{4,6},{6,4},{1,3},{3,1},{5,7},{7,5},{8,10},{10,8},{12,... | collective-permute-start | bytes 3981320 | tf_op jit(solution)/shard_map/ppermute | solution.py:119
  637.9 34.2 %collective-permute-start.85 = (bf16[4,72,1152]{2,1,0:T(8,128)(2,1)S(1)}, bf16[4,72,1152]{2,1,0:T(8,128)(2,1)S(1)}, u32[]{:S(2)}, u32[]{:S(2)}) collective-permute-start(bf16[4,72,1152]{2,1,0:T(8,128)(2,1)S(1)} %get-tuple-element.411), channel_id=1, source_target_pairs={{0,4},{2,6},{4,0},{6,2},{1,5},{3,7},{5,1},{7,3},{8,12},{10,14},{12... | collective-permute-start | bytes 1990664 | tf_op jit(solution)/shard_map/ppermute | solution.py:119
  639.0 41.3 %collective-permute-start.86 = (bf16[4,72,1152]{2,1,0:T(8,128)(2,1)}, bf16[4,72,1152]{2,1,0:T(8,128)(2,1)S(1)}, u32[]{:S(2)}, u32[]{:S(2)}) collective-permute-start(bf16[4,72,1152]{2,1,0:T(8,128)(2,1)} %get-tuple-element.414), channel_id=1, source_target_pairs={{0,2},{2,0},{4,6},{6,4},{1,3},{3,1},{5,7},{7,5},{8,10},{10,8},{12,... | collective-permute-start | bytes 1990664 | tf_op jit(solution)/shard_map/ppermute | solution.py:119
  666.0 46.3 %collective-permute-start.87 = (bf16[4,72,1152]{2,1,0:T(8,128)(2,1)}, bf16[4,72,1152]{2,1,0:T(8,128)(2,1)}, u32[]{:S(2)}, u32[]{:S(2)}) collective-permute-start(bf16[4,72,1152]{2,1,0:T(8,128)(2,1)} %get-tuple-element.418), channel_id=1, source_target_pairs={{0,2},{2,0},{4,6},{6,4},{1,3},{3,1},{5,7},{7,5},{8,10},{10,8},{12,... | collective-permute-start | bytes 1990664 | tf_op jit(solution)/shard_map/ppermute | solution.py:119
  666.8 73.4 %collective-permute-start.95 = (bf16[4,2,72,1152]{3,2,1,0:T(8,128)(2,1)}, bf16[4,2,72,1152]{3,2,1,0:T(8,128)(2,1)}, u32[]{:S(2)}, u32[]{:S(2)}) collective-permute-start(bf16[4,2,72,1152]{3,2,1,0:T(8,128)(2,1)} %get-tuple-element.438), channel_id=1, source_target_pairs={{0,4},{2,6},{4,0},{6,2},{1,5},{3,7},{5,1},{7,3},{8,12},{10,14},{12... | collective-permute-start | bytes 3981320 | tf_op jit(solution)/shard_map/ppermute | solution.py:119
  672.2 42.5 %collective-permute-start.102 = (bf16[4,72,1152]{2,1,0:T(8,128)(2,1)}, bf16[4,72,1152]{2,1,0:T(8,128)(2,1)}, u32[]{:S(2)}, u32[]{:S(2)}) collective-permute-start(bf16[4,72,1152]{2,1,0:T(8,128)(2,1)} %get-tuple-element.449), channel_id=1, source_target_pairs={{0,4},{2,6},{4,0},{6,2},{1,5},{3,7},{5,1},{7,3},{8,12},{10,14},{12... | collective-permute-start | bytes 1990664 | tf_op jit(solution)/shard_map/ppermute | solution.py:119
  684.5 61.8 %collective-permute-start.100 = (bf16[4,2,72,1152]{3,2,1,0:T(8,128)(2,1)}, bf16[4,2,72,1152]{3,2,1,0:T(8,128)(2,1)}, u32[]{:S(2)}, u32[]{:S(2)}) collective-permute-start(bf16[4,2,72,1152]{3,2,1,0:T(8,128)(2,1)} %get-tuple-element.447), channel_id=1, source_target_pairs={{0,2},{2,0},{4,6},{6,4},{1,3},{3,1},{5,7},{7,5},{8,10},{10,8},{12,... | collective-permute-start | bytes 3981320 | tf_op jit(solution)/shard_map/ppermute | solution.py:119
  732.2 40.5 %collective-permute-start.106 = (bf16[2,2,72,1152]{3,2,0,1:T(8,128)(2,1)}, bf16[2,2,72,1152]{3,2,0,1:T(8,128)(2,1)}, u32[]{:S(2)}, u32[]{:S(2)}) collective-permute-start(bf16[2,2,72,1152]{3,2,0,1:T(8,128)(2,1)} %fusion.19), channel_id=1, source_target_pairs={{0,8},{8,0},{16,24},{24,16},{1,9},{9,1},{17,25},{25,17},{2,10},{10... | collective-permute-start | bytes 1990664 | tf_op jit(solution)/shard_map/ppermute | solution.py:119
  732.9 77.6 %collective-permute-start.89 = (f32[256,1152]{1,0:T(8,128)}, f32[256,1152]{1,0:T(8,128)}, u32[]{:S(2)}, u32[]{:S(2)}) collective-permute-start(f32[256,1152]{1,0:T(8,128)} %get-tuple-element.423), channel_id=1, source_target_pairs={{0,1},{1,0},{2,3},{3,2},{4,5},{5,4},{6,7},{7,6},{8,9},{9,8},{10,11... | collective-permute-start | bytes 3538952 | tf_op jit(solution)/shard_map/ppermute | solution.py:119
  738.8 75.0 %collective-permute-start.97 = (bf16[4,2,72,1152]{3,2,1,0:T(8,128)(2,1)}, bf16[4,2,72,1152]{3,2,1,0:T(8,128)(2,1)}, u32[]{:S(2)}, u32[]{:S(2)}) collective-permute-start(bf16[4,2,72,1152]{3,2,1,0:T(8,128)(2,1)} %get-tuple-element.442), channel_id=1, source_target_pairs={{0,2},{2,0},{4,6},{6,4},{1,3},{3,1},{5,7},{7,5},{8,10},{10,8},{12,... | collective-permute-start | bytes 3981320 | tf_op jit(solution)/shard_map/ppermute | solution.py:119
  745.2 70.6 %collective-permute-start.96 = (bf16[4,2,72,1152]{3,2,1,0:T(8,128)(2,1)}, bf16[4,2,72,1152]{3,2,1,0:T(8,128)(2,1)}, u32[]{:S(2)}, u32[]{:S(2)}) collective-permute-start(bf16[4,2,72,1152]{3,2,1,0:T(8,128)(2,1)} %get-tuple-element.439), channel_id=1, source_target_pairs={{0,4},{2,6},{4,0},{6,2},{1,5},{3,7},{5,1},{7,3},{8,12},{10,14},{12... | collective-permute-start | bytes 3981320 | tf_op jit(solution)/shard_map/ppermute | solution.py:119
  (286 other events, 3622.2 us)
